TPU v7x, 128 devices: a whole 4x4x4 slice. The times are simulated.
128 devices in a mesh: tm: 16 (over z, y_hi, core), head: 8 (over y_lo, x).
Axes of the slice: x: 4, y: 4 (y_hi: 2, y_lo: 2; y = y_hi * 2 + y_lo), z: 4, core: 2. Of those that a mesh axis runs over, the one named last changes fastest.
Arguments:
- query: bfloat16 [20480, 24, 128], P(('tm', 'head')), may hold values from -15 to 15
- key: bfloat16 [20480, 24, 128], P(('tm', 'head')), may hold values from -15 to 15
- value: bfloat16 [20480, 24, 128], P(('tm', 'head')), may hold values from -6 to 6
- far_list: int32 [160, 16], P('tm'), may hold values from 0 to 159, as said below
- far_count: int32 [160, 16], P('tm'), may hold values from 0 to 1, as said below
Outputs:
- attended: bfloat16 [20480, 24, 128], P(('tm', 'head'))
Inputs may be any that keep to these rules, and one draw needn't show every extreme that they name: far_list[b, g] is a block of frame g: far_list[b, g] // 10 == g. far_count[b, g] is 0 where the frame of block b and frame g are less than 2 apart. For frames f and g at distance d >= 2, exactly min(5, max(1, 2, 2 * 5 // d)) of the 10 blocks of frame f have far_count 1 for g; so at most 5 blocks of a frame list blocks of one other frame, and exactly 5 at distance 2.
All inputs are finite; a program needn't handle non-finite values.
Results may differ from a plain program's by a relative error of at most 0.012.
Values may be sent and summed in bfloat16 or wider, within the bound.
No kernel may reach another device: no remote copies, remote signals or barrier semaphores. Data moves between devices by JAX's collectives and lax.ppermute only.
A program may use at most 128 MiB of HBM per device.

v0:
```python
import jax
import jax.numpy as jnp
from jax import lax
from jax.sharding import PartitionSpec as P

FH = 16
FW = 80
BLK = 128
RT = 16
RH = 56
RW = 56


THETA = 256.0


def padded(block, sides, width):
    for axis, dim in sides:
        count = lax.axis_size(axis)
        forward = [(i, i + 1) for i in range(count - 1)]
        backward = [(target, source) for source, target in forward]
        low = lax.ppermute(
            lax.slice_in_dim(block, block.shape[dim] - width, None, axis=dim), axis, forward
        )
        high = lax.ppermute(lax.slice_in_dim(block, 0, width, axis=dim), axis, backward)
        block = jnp.concatenate([low, block, high], axis=dim)
    return block


def swap_matrix(head_width):
    row_ids = jnp.arange(head_width)[:, None]
    col_ids = jnp.arange(head_width)[None, :]
    minus_one = (row_ids == col_ids + 1) & (col_ids % 2 == 0)
    plus_one = (col_ids == row_ids + 1) & (row_ids % 2 == 0)
    return jnp.where(plus_one, 1.0, jnp.where(minus_one, -1.0, 0.0)).astype(jnp.bfloat16)


def axis_angles(positions, span_width):
    pair_index = jnp.arange(span_width // 2).astype(jnp.float32)
    inverse = THETA ** (-2.0 * pair_index / span_width)
    return positions[:, None] * inverse[None, :]


def rotate(values, frame_pos, row_pos, col_pos):
    token_count, head_count, head_width = values.shape
    angles = jnp.concatenate(
        [axis_angles(frame_pos, RT), axis_angles(row_pos, RH), axis_angles(col_pos, RW)], axis=1
    )
    angles = jnp.repeat(angles, 2, axis=1)
    swapped = jnp.dot(
        values.reshape(token_count * head_count, head_width),
        swap_matrix(head_width),
        preferred_element_type=jnp.float32,
    )
    swapped = swapped.reshape(token_count, head_count, head_width)
    turned = (
        values.astype(jnp.float32) * jnp.cos(angles)[:, None, :]
        + swapped * jnp.sin(angles)[:, None, :]
    )
    return turned.astype(jnp.bfloat16)


def far_update(running, query_blocks, chosen, present, score_scale):
    row_max, row_total, summed = running
    head_count, block_count, block_rows, head_width = query_blocks.shape
    scores = (
        jnp.einsum("hqid,hqjd->hqij", query_blocks, chosen[0], preferred_element_type=jnp.float32)
        * score_scale
    )
    scores = jnp.where(present[None, :, None, None], scores, -jnp.inf)
    old_max = row_max.reshape(head_count, block_count, block_rows)
    new_max = jnp.maximum(old_max, jnp.max(scores, axis=3))
    weights = jnp.exp(scores - new_max[..., None])
    factor = jnp.exp(old_max - new_max)
    new_total = row_total.reshape(head_count, block_count, block_rows) * factor + jnp.sum(
        weights, axis=3
    )
    new_terms = jnp.einsum(
        "hqij,hqjd->hqid",
        weights.astype(jnp.bfloat16),
        chosen[1],
        preferred_element_type=jnp.float32,
    )
    new_sum = (
        summed.reshape(head_count, block_count, block_rows, head_width) * factor[..., None]
        + new_terms
    )
    token_count = block_count * block_rows
    return (
        new_max.reshape(head_count, token_count),
        new_total.reshape(head_count, token_count),
        new_sum.reshape(head_count, token_count, head_width),
    )


def shards(query, key, value, far_list, far_count):
    frame_tok = FH * FW
    blocks_frame = frame_tok // BLK
    frame_total = lax.axis_size("tm")
    frame_index = lax.axis_index("tm")
    rows_q, rows_k, rows_v = (
        lax.all_to_all(query, "head", split_axis=1, concat_axis=0, tiled=True),
        lax.all_to_all(key, "head", split_axis=1, concat_axis=0, tiled=True),
        lax.all_to_all(value, "head", split_axis=1, concat_axis=0, tiled=True),
    )
    head_count = rows_q.shape[1]
    head_width = rows_q.shape[2]
    token_index = jnp.arange(frame_tok)
    frame_pos = jnp.zeros((frame_tok,), jnp.float32) + frame_index.astype(jnp.float32)
    row_pos = (token_index // FW).astype(jnp.float32)
    col_pos = (token_index % FW).astype(jnp.float32)
    turned_q = jnp.transpose(rotate(rows_q, frame_pos, row_pos, col_pos), (1, 0, 2))
    turned_k = jnp.transpose(rotate(rows_k, frame_pos, row_pos, col_pos), (1, 0, 2))
    kv_pair = jnp.stack([turned_k, jnp.transpose(rows_v, (1, 0, 2))], axis=0)
    score_scale = head_width ** (-0.5)
    beside_all = padded(kv_pair, (("tm", 2),), frame_tok)
    key_frame = jnp.arange(3 * frame_tok) // frame_tok + frame_index - 1
    near_ok = (key_frame >= 0) & (key_frame < frame_total)
    query_span = min(frame_tok, 640)
    pieces = frame_tok // query_span

    def near_part(task_index):
        head_pick = task_index // pieces
        first_row = task_index % pieces * query_span
        head_rows = lax.dynamic_index_in_dim(turned_q, head_pick, 0, keepdims=False)
        query_rows = lax.dynamic_slice_in_dim(head_rows, first_row, query_span, 0)
        near_keys = lax.dynamic_index_in_dim(beside_all[0], head_pick, 0, keepdims=False)
        near_values = lax.dynamic_index_in_dim(beside_all[1], head_pick, 0, keepdims=False)
        scores = (
            jnp.einsum("id,jd->ij", query_rows, near_keys, preferred_element_type=jnp.float32)
            * score_scale
        )
        scores = jnp.where(near_ok[None, :], scores, -jnp.inf)
        row_max = jnp.max(scores, axis=1)
        weights = jnp.exp(scores - row_max[:, None])
        row_total = jnp.sum(weights, axis=1)
        summed = jnp.dot(
            weights.astype(jnp.bfloat16), near_values, preferred_element_type=jnp.float32
        )
        return (row_max, row_total, summed)

    row_max, row_total, summed = lax.map(near_part, jnp.arange(head_count * pieces))
    running = (
        row_max.reshape(head_count, frame_tok),
        row_total.reshape(head_count, frame_tok),
        summed.reshape(head_count, frame_tok, head_width),
    )
    query_blocks = turned_q.reshape(head_count, blocks_frame, BLK, head_width)
    carried = running
    gathered = lax.all_gather(kv_pair, "tm", axis=2, tiled=True)
    frame_count = gathered.shape[2] // frame_tok
    grouped = gathered.reshape(2, head_count, frame_count, blocks_frame, BLK, head_width)

    def one_frame(inner_state, frame_step):
        frame_kv = lax.dynamic_index_in_dim(grouped, frame_step, 2, keepdims=False)
        wanted = (
            lax.dynamic_index_in_dim(far_list, frame_step, 1, keepdims=False)
            - frame_step * blocks_frame
        )
        present = lax.dynamic_index_in_dim(far_count, frame_step, 1, keepdims=False) > 0
        chosen = jnp.take(frame_kv, jnp.clip(wanted, 0, blocks_frame - 1), axis=2)
        return (far_update(inner_state, query_blocks, chosen, present, score_scale), None)

    carried, _ = lax.scan(one_frame, carried, jnp.arange(frame_count))
    running = carried
    row_max, row_total, summed = running
    attended = (summed / row_total[..., None]).astype(jnp.bfloat16)
    attended = jnp.transpose(attended, (1, 0, 2))
    return lax.all_to_all(attended, "head", split_axis=0, concat_axis=1, tiled=True)


def solution(mesh):
    in_specs = (
        P(("tm", "head"), None, None),
        P(("tm", "head"), None, None),
        P(("tm", "head"), None, None),
        P("tm", None),
        P("tm", None),
    )
    out_specs = P(("tm", "head"), None, None)
    return jax.shard_map(shards, mesh=mesh, in_specs=in_specs, out_specs=out_specs, check_vma=False)
```

profile of v0, /device:TPU:32, one launch (start us, length us, event | category | flops | bytes accessed | tf_op | source)
XLA Modules:
  0.0 609.3 jit_solution(16862570343975704698)
XLA Ops:
  15.4 13.9 %all-to-all-done.1 = bf16[160,24,128]{2,0,1:T(8,128)(2,1)S(1)} async-done(((bf16[160,24,128]{2,0,1:T(8,128)(2,1)}), bf16[160,24,128]{2,0,1:T(8,128)(2,1)S(1)}, u32[]{:S(2)}, u32[]{:S(2)}) %all-to-all-start.1) | async-done | bytes 983072 | tf_op jit(solution)/shard_map/all_to_all | solution.py:103
  34.1 13.7 %all-to-all-done = bf16[160,24,128]{2,0,1:T(8,128)(2,1)S(1)} async-done(((bf16[160,24,128]{2,0,1:T(8,128)(2,1)}), bf16[160,24,128]{2,0,1:T(8,128)(2,1)S(1)}, u32[]{:S(2)}, u32[]{:S(2)}) %all-to-all-start) | async-done | bytes 983072 | tf_op jit(solution)/shard_map/all_to_all | solution.py:102
  100.6 59.7 %collective-permute-done.1 = bf16[2,3,1280,128]{3,2,1,0:T(8,128)(2,1)} collective-permute-done((bf16[2,3,1280,128]{3,2,1,0:T(8,128)(2,1)}, bf16[2,3,1280,128]{3,2,1,0:T(8,128)(2,1)}, u32[]{:S(2)}, u32[]{:S(2)}) %collective-permute-start.1) | collective-permute-done | bytes 1966112 | tf_op jit(solution)/shard_map/ppermute | solution.py:25
  169.4 165.6 %while.33 = (s32[]{:T(128)}, f32[6,640]{1,0:T(8,128)S(1)}, f32[6,640]{1,0:T(8,128)S(1)}, f32[6,640,128]{2,1,0:T(8,128)}, s32[6]{0:T(128)S(1)}, /*index=5*/bf16[3...) while((s32[]{:T(128)}, f32[6,640]{1,0:T(8,128)S(1)}, ...), condition=%wide.region_3.4_spmd.clone, body=%wide.region_0.3_spmd.clone.sunk | while | flops 1285373440 | bytes 43792108 | solution.py:142
  177.2 6.2 %fusion.91 = (f32[640]{0:T(1024)S(1)}, f32[640,3840]{1,0:T(8,128)}) fusion(pred[3840]{0:T(1024)(128)(4,1)S(1)} %compare_and_fusion.2, bf16[1,3,3840,128]{3,2,1,0:T(8,128)(2,1)S(1)} %get-tuple-element.436, s32[]{:T(128)S(6)} %select_n.238, bf16[3,1280,128]{2,1,0:T(8,128)(2,1)} %get-tuple-element.475, s32[]{:T(128)S(6)} %select_n.239, s32[]{:T(128)S(6)} %select_n.242), kind=kOutput, calls=%fused_computation.34.clone.1 | convolution fusion | flops 636517760 | bytes 10983948 | tf_op jit(solution)/shard_map/while/body/eval_jaxpr/id,jd->ij/dot_general | solution.py:130
  183.5 8.8 %fusion.92 = f32[640]{0:T(1024)S(1)} fusion(f32[640,3840]{1,0:T(8,128)} %get-tuple-element.438, f32[640]{0:T(1024)S(1)} %get-tuple-element.437, pred[3840]{0:T(1024)(128)(4,1)S(1)} %compare_and_fusion.2), kind=kLoop, calls=%fused_computation.36.clone.1 | loop fusion | flops 9829760 | bytes 9839360 | tf_op jit(solution)/shard_map/while/body/eval_jaxpr/reduce_sum | solution.py:136
  192.3 6.8 %fusion.93 = f32[6,640,128]{2,1,0:T(8,128)} fusion(f32[6,640,128]{2,1,0:T(8,128)} %get-tuple-element.458, s32[]{:T(128)S(6)} %copy.112, f32[640,3840]{1,0:T(8,128)} %get-tuple-element.438, f32[640]{0:T(1024)S(1)} %get-tuple-element.437, pred[3840]{0:T(1024)(128)(4,1)S(1)} %compare_and_fusion.2, bf16[1,3,3840,128]{3,2,1,0:T(8,128)(2,1)} %get-tuple-element.439, ...), kind=kOutput, calls=%fused_computation.40.clone.1 | convolution fusion | flops 638976000 | bytes 11147528 | tf_op jit(solution)/shard_map/while/body/eval_jaxpr/dot_general | solution.py:137
  207.0 6.2 %fusion.91 = (f32[640]{0:T(1024)S(1)}, f32[640,3840]{1,0:T(8,128)}) fusion(pred[3840]{0:T(1024)(128)(4,1)S(1)} %compare_and_fusion.2, bf16[1,3,3840,128]{3,2,1,0:T(8,128)(2,1)S(1)} %get-tuple-element.436, s32[]{:T(128)S(6)} %select_n.238, bf16[3,1280,128]{2,1,0:T(8,128)(2,1)} %get-tuple-element.475, s32[]{:T(128)S(6)} %select_n.239, s32[]{:T(128)S(6)} %select_n.242), kind=kOutput, calls=%fused_computation.34.clone.1 | convolution fusion | flops 636517760 | bytes 10983948 | tf_op jit(solution)/shard_map/while/body/eval_jaxpr/id,jd->ij/dot_general | solution.py:130
  213.3 6.0 fusion.92
  219.3 6.8 %fusion.93 = f32[6,640,128]{2,1,0:T(8,128)} fusion(f32[6,640,128]{2,1,0:T(8,128)} %get-tuple-element.458, s32[]{:T(128)S(6)} %copy.112, f32[640,3840]{1,0:T(8,128)} %get-tuple-element.438, f32[640]{0:T(1024)S(1)} %get-tuple-element.437, pred[3840]{0:T(1024)(128)(4,1)S(1)} %compare_and_fusion.2, bf16[1,3,3840,128]{3,2,1,0:T(8,128)(2,1)} %get-tuple-element.439, ...), kind=kOutput, calls=%fused_computation.40.clone.1 | convolution fusion | flops 638976000 | bytes 11147528 | tf_op jit(solution)/shard_map/while/body/eval_jaxpr/dot_general | solution.py:137
  233.9 6.2 %fusion.91 = (f32[640]{0:T(1024)S(1)}, f32[640,3840]{1,0:T(8,128)}) fusion(pred[3840]{0:T(1024)(128)(4,1)S(1)} %compare_and_fusion.2, bf16[1,3,3840,128]{3,2,1,0:T(8,128)(2,1)S(1)} %get-tuple-element.436, s32[]{:T(128)S(6)} %select_n.238, bf16[3,1280,128]{2,1,0:T(8,128)(2,1)} %get-tuple-element.475, s32[]{:T(128)S(6)} %select_n.239, s32[]{:T(128)S(6)} %select_n.242), kind=kOutput, calls=%fused_computation.34.clone.1 | convolution fusion | flops 636517760 | bytes 10983948 | tf_op jit(solution)/shard_map/while/body/eval_jaxpr/id,jd->ij/dot_general | solution.py:130
  240.2 6.0 fusion.92
  246.2 6.7 %fusion.93 = f32[6,640,128]{2,1,0:T(8,128)} fusion(f32[6,640,128]{2,1,0:T(8,128)} %get-tuple-element.458, s32[]{:T(128)S(6)} %copy.112, f32[640,3840]{1,0:T(8,128)} %get-tuple-element.438, f32[640]{0:T(1024)S(1)} %get-tuple-element.437, pred[3840]{0:T(1024)(128)(4,1)S(1)} %compare_and_fusion.2, bf16[1,3,3840,128]{3,2,1,0:T(8,128)(2,1)} %get-tuple-element.439, ...), kind=kOutput, calls=%fused_computation.40.clone.1 | convolution fusion | flops 638976000 | bytes 11147528 | tf_op jit(solution)/shard_map/while/body/eval_jaxpr/dot_general | solution.py:137
  260.9 6.2 %fusion.91 = (f32[640]{0:T(1024)S(1)}, f32[640,3840]{1,0:T(8,128)}) fusion(pred[3840]{0:T(1024)(128)(4,1)S(1)} %compare_and_fusion.2, bf16[1,3,3840,128]{3,2,1,0:T(8,128)(2,1)S(1)} %get-tuple-element.436, s32[]{:T(128)S(6)} %select_n.238, bf16[3,1280,128]{2,1,0:T(8,128)(2,1)} %get-tuple-element.475, s32[]{:T(128)S(6)} %select_n.239, s32[]{:T(128)S(6)} %select_n.242), kind=kOutput, calls=%fused_computation.34.clone.1 | convolution fusion | flops 636517760 | bytes 10983948 | tf_op jit(solution)/shard_map/while/body/eval_jaxpr/id,jd->ij/dot_general | solution.py:130
  267.1 6.0 fusion.92
  273.2 7.2 %fusion.93 = f32[6,640,128]{2,1,0:T(8,128)} fusion(f32[6,640,128]{2,1,0:T(8,128)} %get-tuple-element.458, s32[]{:T(128)S(6)} %copy.112, f32[640,3840]{1,0:T(8,128)} %get-tuple-element.438, f32[640]{0:T(1024)S(1)} %get-tuple-element.437, pred[3840]{0:T(1024)(128)(4,1)S(1)} %compare_and_fusion.2, bf16[1,3,3840,128]{3,2,1,0:T(8,128)(2,1)} %get-tuple-element.439, ...), kind=kOutput, calls=%fused_computation.40.clone.1 | convolution fusion | flops 638976000 | bytes 11147528 | tf_op jit(solution)/shard_map/while/body/eval_jaxpr/dot_general | solution.py:137
  288.6 6.3 %fusion.91 = (f32[640]{0:T(1024)S(1)}, f32[640,3840]{1,0:T(8,128)}) fusion(pred[3840]{0:T(1024)(128)(4,1)S(1)} %compare_and_fusion.2, bf16[1,3,3840,128]{3,2,1,0:T(8,128)(2,1)S(1)} %get-tuple-element.436, s32[]{:T(128)S(6)} %select_n.238, bf16[3,1280,128]{2,1,0:T(8,128)(2,1)} %get-tuple-element.475, s32[]{:T(128)S(6)} %select_n.239, s32[]{:T(128)S(6)} %select_n.242), kind=kOutput, calls=%fused_computation.34.clone.1 | convolution fusion | flops 636517760 | bytes 10983948 | tf_op jit(solution)/shard_map/while/body/eval_jaxpr/id,jd->ij/dot_general | solution.py:130
  294.9 6.4 %fusion.92 = f32[640]{0:T(1024)S(1)} fusion(f32[640,3840]{1,0:T(8,128)} %get-tuple-element.438, f32[640]{0:T(1024)S(1)} %get-tuple-element.437, pred[3840]{0:T(1024)(128)(4,1)S(1)} %compare_and_fusion.2), kind=kLoop, calls=%fused_computation.36.clone.1 | loop fusion | flops 9829760 | bytes 9839360 | tf_op jit(solution)/shard_map/while/body/eval_jaxpr/reduce_sum | solution.py:136
  301.4 6.7 %fusion.93 = f32[6,640,128]{2,1,0:T(8,128)} fusion(f32[6,640,128]{2,1,0:T(8,128)} %get-tuple-element.458, s32[]{:T(128)S(6)} %copy.112, f32[640,3840]{1,0:T(8,128)} %get-tuple-element.438, f32[640]{0:T(1024)S(1)} %get-tuple-element.437, pred[3840]{0:T(1024)(128)(4,1)S(1)} %compare_and_fusion.2, bf16[1,3,3840,128]{3,2,1,0:T(8,128)(2,1)} %get-tuple-element.439, ...), kind=kOutput, calls=%fused_computation.40.clone.1 | convolution fusion | flops 638976000 | bytes 11147528 | tf_op jit(solution)/shard_map/while/body/eval_jaxpr/dot_general | solution.py:137
  316.0 6.2 %fusion.91 = (f32[640]{0:T(1024)S(1)}, f32[640,3840]{1,0:T(8,128)}) fusion(pred[3840]{0:T(1024)(128)(4,1)S(1)} %compare_and_fusion.2, bf16[1,3,3840,128]{3,2,1,0:T(8,128)(2,1)S(1)} %get-tuple-element.436, s32[]{:T(128)S(6)} %select_n.238, bf16[3,1280,128]{2,1,0:T(8,128)(2,1)} %get-tuple-element.475, s32[]{:T(128)S(6)} %select_n.239, s32[]{:T(128)S(6)} %select_n.242), kind=kOutput, calls=%fused_computation.34.clone.1 | convolution fusion | flops 636517760 | bytes 10983948 | tf_op jit(solution)/shard_map/while/body/eval_jaxpr/id,jd->ij/dot_general | solution.py:130
  322.2 6.0 fusion.92
  328.3 6.7 %fusion.93 = f32[6,640,128]{2,1,0:T(8,128)} fusion(f32[6,640,128]{2,1,0:T(8,128)} %get-tuple-element.458, s32[]{:T(128)S(6)} %copy.112, f32[640,3840]{1,0:T(8,128)} %get-tuple-element.438, f32[640]{0:T(1024)S(1)} %get-tuple-element.437, pred[3840]{0:T(1024)(128)(4,1)S(1)} %compare_and_fusion.2, bf16[1,3,3840,128]{3,2,1,0:T(8,128)(2,1)} %get-tuple-element.439, ...), kind=kOutput, calls=%fused_computation.40.clone.1 | convolution fusion | flops 638976000 | bytes 11147528 | tf_op jit(solution)/shard_map/while/body/eval_jaxpr/dot_general | solution.py:137
  335.1 238.2 %while.32 = (s32[]{:T(128)}, f32[3,1280]{1,0:T(4,128)S(1)}, f32[3,1280]{1,0:T(4,128)S(1)}, f32[3,1280,128]{2,1,0:T(8,128)}, s32[16]{0:T(128)S(1)}, /*index=5*/s3...) while((s32[]{:T(128)}, f32[3,1280]{1,0:T(4,128)S(1)}, ...), condition=%wide.region_7.8_spmd, body=%wide.region_4.7_spmd.sunk | while | flops 259047520 | bytes 44522000 | solution.py:164
  579.1 21.8 %all_to_all.66 = bf16[1280,3,128]{2,1,0:T(4,128)(2,1)S(1)} all-to-all(bf16[1280,3,128]{2,1,0:T(4,128)(2,1)S(1)} %fusion.49), channel_id=1, replica_groups=mesh['tm'=16,'head'=8] {'head'}, dimensions={0} | all-to-all | bytes 1966080 | tf_op jit(solution)/shard_map/all_to_all | solution.py:169
  (423 shorter events, 316.8 us)
Async XLA Ops:
  6.5 7.7 %copy-start.9 = (bf16[160,24,128]{2,1,0:T(8,128)(2,1)S(1)}, bf16[160,24,128]{2,1,0:T(8,128)(2,1)}, u32[]{:S(2)}) copy-start(bf16[160,24,128]{2,1,0:T(8,128)(2,1)} %param.9) | copy-start | bytes 2949124
  8.9 20.3 %all-to-all-start.1 = ((bf16[160,24,128]{2,0,1:T(8,128)(2,1)}), bf16[160,24,128]{2,0,1:T(8,128)(2,1)S(1)}, u32[]{:S(2)}, u32[]{:S(2)}) async-start(bf16[160,24,128]{2,0,1:T(8,128)(2,1)} %copy.65), calls=%async_computation.1 | async-start | bytes 1966080 | tf_op jit(solution)/shard_map/all_to_all | solution.py:103
  14.2 18.6 %copy-start.10 = (bf16[160,24,128]{2,1,0:T(8,128)(2,1)S(1)}, bf16[160,24,128]{2,1,0:T(8,128)(2,1)}, u32[]{:S(2)}) copy-start(bf16[160,24,128]{2,1,0:T(8,128)(2,1)} %param.11) | copy-start | bytes 2949124
  29.2 18.6 %all-to-all-start = ((bf16[160,24,128]{2,0,1:T(8,128)(2,1)}), bf16[160,24,128]{2,0,1:T(8,128)(2,1)S(1)}, u32[]{:S(2)}, u32[]{:S(2)}) async-start(bf16[160,24,128]{2,0,1:T(8,128)(2,1)} %copy.58), calls=%async_computation | async-start | bytes 1966080 | tf_op jit(solution)/shard_map/all_to_all | solution.py:102
  47.8 38.0 %all-to-all-start.2 = ((bf16[160,24,128]{2,0,1:T(8,128)(2,1)}), bf16[160,24,128]{2,0,1:T(8,128)(2,1)}, u32[]{:S(2)}, u32[]{:S(2)}) async-start(bf16[160,24,128]{2,0,1:T(8,128)(2,1)} %copy.70), calls=%async_computation.2 | async-start | bytes 1966080 | tf_op jit(solution)/shard_map/all_to_all | solution.py:104
  52.1 283.0 %all-gather.2.cloned.1.call-start = ((), (), s32[]{:S(2)}) async-start(), calls=%async_computation.4 | async-start | bytes 33423360 | tf_op jit(solution)/shard_map/all_gather | solution.py:150
  81.7 5.6 copy-start.8
  87.7 4.3 copy-start.3
  94.5 6.0 copy-start.11
  94.5 6.1 copy-start.12
  94.5 69.7 %copy-start.4 = (bf16[8,160,3,128]{3,1,0,2:T(8,128)(2,1)S(1)}, bf16[8,160,3,128]{3,1,0,2:T(8,128)(2,1)}, u32[]{:S(2)}) copy-start(bf16[8,160,3,128]{3,1,0,2:T(8,128)(2,1)} %copy-done.3) | copy-start | bytes 2949124
  94.5 69.7 %copy-start.6 = (bf16[1280,3,128]{2,0,1:T(8,128)(2,1)S(1)}, bf16[1280,3,128]{2,0,1:T(8,128)(2,1)}, u32[]{:S(2)}) copy-start(bf16[1280,3,128]{2,0,1:T(8,128)(2,1)} %copy-done.5) | copy-start | bytes 2949124
  94.5 65.8 %collective-permute-start.1 = (bf16[2,3,1280,128]{3,2,1,0:T(8,128)(2,1)}, bf16[2,3,1280,128]{3,2,1,0:T(8,128)(2,1)}, u32[]{:S(2)}, u32[]{:S(2)}) collective-permute-start(bf16[2,3,1280,128]{3,2,1,0:T(8,128)(2,1)} %pad_maximum_fusion.1), channel_id=1, source_target_pairs={{8,0},{16,8},{24,16},{32,24},{40,32},{48,40},{56,48},{64,56},{72,6... | collective-permute-start | bytes 5898248 | tf_op jit(solution)/shard_map/ppermute | solution.py:25
  98.3 65.9 %collective-permute-start = (bf16[2,3,1280,128]{3,2,1,0:T(8,128)(2,1)}, bf16[2,3,1280,128]{3,2,1,0:T(8,128)(2,1)}, u32[]{:S(2)}, u32[]{:S(2)}) collective-permute-start(bf16[2,3,1280,128]{3,2,1,0:T(8,128)(2,1)} %pad_maximum_fusion.1), channel_id=1, source_target_pairs={{0,8},{8,16},{16,24},{24,32},{32,40},{40,48},{48,56},{56,64},{64,7... | collective-permute-start | bytes 5898248 | tf_op jit(solution)/shard_map/ppermute | solution.py:22
  356.7 1.9 copy-start.2
  371.6 1.9 copy-start.2
  386.5 1.9 copy-start.2
  431.1 1.9 copy-start.2
  446.0 1.9 copy-start.2
  460.9 1.9 copy-start.2
  505.6 1.9 copy-start.2
  520.4 1.9 copy-start.2
  535.3 1.9 copy-start.2
  565.1 1.9 copy-start.2
  (40 other events, 59.0 us)
Sparse Core Ops, SparseCore 0:
  94.6 203.9 all-gather.1
where the time goes:
time: 613 us; the launch traced here: 609 us
  local copies, waits for them, and re-layouts  162 us (26%)
  matrix products  151 us (25%)
  other arithmetic  98.1 us (16%)
  waiting for transfers between devices  91.1 us (15%)
  loops' own time  52.6 us (9%)
  blocking collectives  21.8 us (4%)
  starting transfers between devices  19 us (3%)
  between operations  13.6 us (2%)
    ppermute x1, waiting for transfers between devices, padded(): lax.ppermute(lax.slice_in_dim(block, 0, width, axis=dim), axis, backward)  59.7 us
    dot_general x16, matrix products, far_update(): jnp.einsum('hqij,hqjd->hqid', weights.astype(jnp.bfloat16), chosen[1], pr...  54.8 us
    dot_general x6, matrix products, near_part(): jnp.dot(weights.astype(jnp.bfloat16), near_values, preferred_element_type...  40.9 us
    reduce_sum x6, other arithmetic, near_part(): row_total = jnp.sum(weights, axis=1)  39 us
    dot_general x6, matrix products, near_part(): jnp.einsum('id,jd->ij', query_rows, near_keys, preferred_element_type=jnp...  37.2 us
    another operation x1, loops' own time, shards(): carried, _ = lax.scan(one_frame, carried, jnp.arange(frame_count))  37.1 us
    gather x16, local copies, waits for them, and re-layouts, one_frame(): chosen = jnp.take(frame_kv, jnp.clip(wanted, 0, blocks_frame - 1), axis=2)  34.7 us
    select_n x16, other arithmetic, one_frame(): chosen = jnp.take(frame_kv, jnp.clip(wanted, 0, blocks_frame - 1), axis=2)  30.1 us
  transfers between devices with their start and end apart: 6, of which 4 were waited for; matrix products, arithmetic and copies ran while one was open for 31% of the time, Pallas kernels for 0%

commit v1 on v0

v1 whole, which is shorter than its diff:
```python
import jax
import jax.numpy as jnp
import numpy as np
from jax import lax
from jax.experimental import pallas as pl
from jax.experimental.pallas import tpu as pltpu
from jax.sharding import Mesh
from jax.sharding import PartitionSpec as P

FW = 80
TOK = 1280
BLK = 128
CH = 160
NB = 10
DH = 128
RT, RH, RW = 16, 56, 56
HEADS = 24
PER = 3
PLANE = 4
THETA = 256.0
SCALE = float(DH**-0.5 * np.log2(np.e))
CHUNKS = ((0, 1, 2),)

BASE = 8
BIG, MID, ONE = 12, 4, 1
BIG_AT, MID_AT, ONE_AT = 32, 44, 48
VMEM = 58 * 2**20

i32 = jnp.int32


def params():
    return pltpu.CompilerParams(vmem_limit_bytes=VMEM)


def smem():
    return pl.BlockSpec(memory_space=pltpu.SMEM)


def table_body(place_ref, list_ref, count_ref, want_ref, qslot_ref, plane_ref, kb_ref, qb_ref):
    z, r = place_ref[0], place_ref[1]
    f = PLANE * z + r

    def frame_lists(g, carry):
        for j in range(8):
            kb_ref[g * 8 + j] = 0
            qb_ref[g * 8 + j] = 0

        def one_block(n, filled):
            kb_ref[g * 8 + filled] = list_ref[n, g] - NB * g
            qb_ref[g * 8 + filled] = n
            return filled + jnp.where(count_ref[n, g] > 0, 1, 0).astype(i32)

        lax.fori_loop(0, NB, one_block, jnp.int32(0))
        return carry

    lax.fori_loop(0, PLANE * 4, frame_lists, jnp.int32(0))

    def clear(s, carry):
        for zp in range(4):
            want_ref[zp, s] = 0
        return carry

    lax.fori_loop(0, 128, clear, jnp.int32(0))
    for s in range(64):
        qslot_ref[s] = -1
    for zp in range(4):
        for i in range(PLANE):
            g = PLANE * zp + i
            far = jnp.abs(f - g) >= 2
            for j in range(2):
                want_ref[zp, 2 * i + j] = NB * i + kb_ref[g * 8 + j]
                qslot_ref[zp * BASE + 2 * i + j] = jnp.where(far & (z != zp), qb_ref[g * 8 + j], -1)

    def listed(zp, s, slot, i, j):
        at = (PLANE * zp + i) * 8 + j
        want_ref[zp, s] = NB * i + kb_ref[at]
        qslot_ref[slot] = qb_ref[at]

    def side(up, first, second, third):
        zp = z - 1 if up else z + 1
        exists = z > 0 if up else z < 3
        near, two, three = (3, 2, 1) if up else (0, 1, 2)

        @pl.when(exists & (r == first))
        def _():
            for j in range(2):
                listed(zp, 2 * near + j, zp * BASE + 2 * near + j, two, 2 + j)
            for n in range(NB):
                want_ref[zp, BASE + n] = NB * near + n
            listed(zp, BASE + 10, BIG_AT + 10, two, 4)
            listed(zp, BASE + 11, BIG_AT + 11, three, 2)

        @pl.when(exists & (r == second))
        def _():
            for j in range(3):
                listed(zp, BASE + BIG + j, MID_AT + j, near, 2 + j)
            listed(zp, BASE + BIG + 3, MID_AT + 3, two, 2)

        @pl.when(exists & (r == third))
        def _():
            listed(zp, BASE + BIG + MID, ONE_AT, near, 2)

    side(True, 0, 1, 2)
    side(False, 3, 2, 1)

    two = (r + 2) % PLANE
    three = PLANE - 1 - r
    for j in range(5):
        at = (PLANE * z + two) * 8 + j
        plane_ref[2 * j] = qb_ref[at]
        plane_ref[2 * j + 1] = NB * two + kb_ref[at]
    for j in range(3):
        at = (PLANE * z + three) * 8 + j
        plane_ref[10 + 2 * j] = qb_ref[at]
        plane_ref[10 + 2 * j + 1] = NB * three + kb_ref[at]


def tables(place, far_list, far_count):
    return pl.pallas_call(
        table_body,
        in_specs=[smem(), smem(), smem()],
        out_specs=[smem(), smem(), smem()],
        out_shape=[
            jax.ShapeDtypeStruct((4, 128), i32),
            jax.ShapeDtypeStruct((64,), i32),
            jax.ShapeDtypeStruct((16,), i32),
        ],
        scratch_shapes=[pltpu.SMEM((128,), i32), pltpu.SMEM((128,), i32)],
        name="tables",
    )(place, far_list, far_count)


def lane_rates():
    rates = []
    for width in (RT, RH, RW):
        rates.append(np.float32(THETA) ** (np.float32(-2.0) * np.arange(width // 2, dtype=np.float32) / np.float32(width)))
    return np.repeat(np.concatenate(rates), 2)[None].astype(np.float32)


def turn_tables(frame, chunk, rates):
    lane = lax.broadcasted_iota(i32, (CH, DH), 1)
    token = lax.broadcasted_iota(i32, (CH, DH), 0)
    below = (token >= FW).astype(i32)
    position = jnp.where(lane < RT, frame, jnp.where(lane < RT + RH, 2 * chunk + below, token - FW * below))
    angle = position.astype(jnp.float32) * rates
    even = lane % 2 == 0
    sine = jnp.sin(angle)
    return jnp.cos(angle), jnp.where(even, -sine, sine), even


def turn(x, tables_):
    cosine, sine, even = tables_
    swapped = jnp.where(even, pltpu.roll(x, DH - 1, 1), pltpu.roll(x, 1, 1))
    return x * cosine + swapped * sine


def enter_kv_body(rows, place_ref, rates_ref, k_ref, v_ref, o_ref, ks, vs):
    tabs = turn_tables(place_ref[2], place_ref[3], rates_ref[...])
    ks[...] = k_ref[...].astype(jnp.float32).reshape(CH * HEADS, DH)
    vs[...] = v_ref[...].astype(jnp.float32).reshape(CH * HEADS, DH)
    for hd in range(8):
        for at, row in enumerate(rows):
            pick = pl.ds(hd * PER + row, CH, stride=HEADS)
            turned = turn(ks[pick, :], tabs).astype(jnp.bfloat16)
            kept = vs[pick, :].astype(jnp.bfloat16)
            for yh in range(2):
                o_ref[yh, hd, at, 0] = turned
                o_ref[yh, hd, at, 1] = kept


def enter_kv(place, rates, key, value, rows):
    return pl.pallas_call(
        lambda *refs: enter_kv_body(rows, *refs),
        in_specs=[smem()] + [pl.BlockSpec(memory_space=pltpu.VMEM)] * 3,
        out_specs=pl.BlockSpec(memory_space=pltpu.VMEM),
        out_shape=jax.ShapeDtypeStruct((2, 8, len(rows), 2, CH, DH), jnp.bfloat16),
        scratch_shapes=[pltpu.VMEM((CH * HEADS, DH), jnp.float32)] * 2,
        compiler_params=params(),
        name="enter_kv",
    )(place, rates, key, value)


def enter_q_body(rows, place_ref, rates_ref, q_ref, o_ref, qs):
    tabs = turn_tables(place_ref[2], place_ref[3], rates_ref[...])
    qs[...] = q_ref[...].astype(jnp.float32).reshape(CH * HEADS, DH)
    for hd in range(8):
        for at, row in enumerate(rows):
            pick = pl.ds(hd * PER + row, CH, stride=HEADS)
            o_ref[hd, at] = turn(qs[pick, :], tabs).astype(jnp.bfloat16)


def enter_q(place, rates, query, rows):
    return pl.pallas_call(
        lambda *refs: enter_q_body(rows, *refs),
        in_specs=[smem()] + [pl.BlockSpec(memory_space=pltpu.VMEM)] * 2,
        out_specs=pl.BlockSpec(memory_space=pltpu.VMEM),
        out_shape=jax.ShapeDtypeStruct((8, len(rows), CH, DH), jnp.bfloat16),
        scratch_shapes=[pltpu.VMEM((CH * HEADS, DH), jnp.float32)],
        compiler_params=params(),
        name="enter_q",
    )(place, rates, query)


def pack_body(place_ref, want_ref, own_ref, sib_ref, base_ref, big_ref, mid_ref, one_ref, frames):
    z, r, c = place_ref[0], place_ref[1], place_ref[4]
    for b in range(2):
        for ref, core in ((own_ref, c), (sib_ref, 1 - c)):
            start = pl.multiple_of((2 * b + core) * TOK, TOK)
            frames[pl.ds(start, TOK), :] = ref[b, :, 0, 0].reshape(TOK, DH)

    def block(index):
        return frames[pl.ds(pl.multiple_of(index * BLK, BLK), BLK), :]

    for zp in range(4):
        for s in range(BASE):
            base_ref[zp, s, 0, 0] = block(want_ref[zp, s])
    low, high = jnp.minimum(z + 1, 3), jnp.maximum(z - 1, 0)
    outer = jnp.where(r < 2, low, high)
    inner = jnp.where(r < 2, high, low)
    for s in range(BIG):
        big_ref[s, 0, 0] = block(want_ref[outer, BASE + s])
    for s in range(MID):
        mid_ref[s, 0, 0] = block(want_ref[outer, BASE + BIG + s])
    one_ref[0, 0, 0] = block(want_ref[inner, BASE + BIG + MID])


def pack(place, asked, own, sib):
    nh = own.shape[2]
    whole = pl.BlockSpec((2, 8, 1, 1, CH, DH), lambda h, kv: (0, 0, h, kv, 0, 0))

    def out(*lead):
        zeros = (0,) * len(lead)
        return pl.BlockSpec((*lead, 1, 1, BLK, DH), lambda h, kv: (*zeros, h, kv, 0, 0))

    def shape(*lead):
        return jax.ShapeDtypeStruct((*lead, nh, 2, BLK, DH), jnp.bfloat16)

    return pl.pallas_call(
        pack_body,
        grid=(nh, 2),
        in_specs=[smem(), smem(), whole, whole],
        out_specs=[out(4, BASE), out(BIG), out(MID), out(ONE)],
        out_shape=[shape(4, BASE), shape(BIG), shape(MID), shape(ONE)],
        scratch_shapes=[pltpu.VMEM((PLANE * TOK, DH), jnp.bfloat16)],
        compiler_params=params(),
        name="pack",
    )(place, asked, own, sib)


def dot_t(a, b):
    return lax.dot_general(a, b, (((1,), (1,)), ((), ())), preferred_element_type=jnp.float32)


def flash(q, k, v, rows, m_ref, l_ref, acc_ref, first=False):
    s = dot_t(q, k) * SCALE
    top = jnp.max(s, axis=1, keepdims=True)
    if first:
        m_new = jnp.broadcast_to(top, (q.shape[0], DH))
    else:
        m_old = m_ref[rows, :]
        m_new = jnp.maximum(m_old, top)
    p = jnp.exp2(s - m_new[:, :1])
    total = jnp.sum(p, axis=1, keepdims=True)
    mixed = jnp.dot(p.astype(jnp.bfloat16), v, preferred_element_type=jnp.float32)
    if first:
        l_ref[rows, :] = jnp.broadcast_to(total, (q.shape[0], DH))
        acc_ref[rows, :] = mixed
    else:
        fade = jnp.exp2(m_old - m_new)
        l_ref[rows, :] = l_ref[rows, :] * fade + total
        acc_ref[rows, :] = acc_ref[rows, :] * fade + mixed
    m_ref[rows, :] = m_new


QT = 256


def near_body(place_ref, plane_ref, q_ref, own_ref, sib_ref, acc_ref, m_ref, l_ref, qs, kf, vf):
    r, c = place_ref[1], place_ref[4]
    qs[...] = q_ref[:, 0].reshape(TOK, DH)
    for b in range(2):
        for ref, core in ((own_ref, c), (sib_ref, 1 - c)):
            start = pl.multiple_of((2 * b + core) * TOK, TOK)
            kf[pl.ds(start, TOK), :] = ref[b, :, 0, 0].reshape(TOK, DH)
            vf[pl.ds(start, TOK), :] = ref[b, :, 0, 1].reshape(TOK, DH)
    acc, m, l = acc_ref.at[0], m_ref.at[0], l_ref.at[0]

    def frame(i, first):
        at = pl.ds(pl.multiple_of(i * TOK, TOK), TOK)

        def tile(t, carry):
            rows = pl.ds(pl.multiple_of(t * QT, QT), QT)
            flash(qs[rows, :], kf[at, :], vf[at, :], rows, m, l, acc, first)
            return carry

        lax.fori_loop(0, TOK // QT, tile, jnp.int32(0))

    frame(r, True)

    @pl.when(r > 0)
    def _():
        frame(r - 1, False)

    @pl.when(r < PLANE - 1)
    def _():
        frame(r + 1, False)

    def pair(p, carry):
        rows = pl.ds(pl.multiple_of(plane_ref[2 * p] * BLK, BLK), BLK)
        at = pl.ds(pl.multiple_of(plane_ref[2 * p + 1] * BLK, BLK), BLK)
        flash(qs[rows, :], kf[at, :], vf[at, :], rows, m, l, acc)
        return carry

    lax.fori_loop(0, jnp.where((r == 0) | (r == PLANE - 1), 8, 5), pair, jnp.int32(0))


def near(place, plane_pairs, q, own, sib):
    nh = q.shape[1]
    frames = pl.BlockSpec((2, 8, 1, 2, CH, DH), lambda h: (0, 0, h, 0, 0, 0))
    state = pl.BlockSpec((1, TOK, DH), lambda h: (h, 0, 0))
    return pl.pallas_call(
        near_body,
        grid=(nh,),
        in_specs=[smem(), smem(), pl.BlockSpec((8, 1, CH, DH), lambda h: (0, h, 0, 0)), frames, frames],
        out_specs=[state] * 3,
        out_shape=[jax.ShapeDtypeStruct((nh, TOK, DH), jnp.float32)] * 3,
        scratch_shapes=[
            pltpu.VMEM((TOK, DH), jnp.bfloat16),
            pltpu.VMEM((PLANE * TOK, DH), jnp.bfloat16),
            pltpu.VMEM((PLANE * TOK, DH), jnp.bfloat16),
        ],
        compiler_params=params(),
        cost_estimate=pl.CostEstimate(
            flops=nh * 3 * TOK * TOK * DH * 4, transcendentals=nh * 3 * TOK * TOK, bytes_accessed=nh * 4 * 2**20
        ),
        name="near",
    )(place, plane_pairs, q, own, sib)


def far_body(
    place_ref, qslot_ref, q_ref, acc_in, m_in, l_in, base_ref, big_ref, mid_ref, one_ref, o_ref, qs, acc, m, l
):
    z, r = place_ref[0], place_ref[1]
    qs[...] = q_ref[:, 0].reshape(TOK, DH)
    acc[...] = acc_in[0]
    m[...] = m_in[0]
    l[...] = l_in[0]

    @pl.when(((r == 0) & (z > 0)) | ((r == PLANE - 1) & (z < 3)))
    def _():
        def tile(t, carry):
            rows = pl.ds(pl.multiple_of(t * QT, QT), QT)
            k = big_ref[:NB, 0, 0].reshape(TOK, DH)
            v = big_ref[:NB, 0, 1].reshape(TOK, DH)
            flash(qs[rows, :], k, v, rows, m, l, acc)
            return carry

        lax.fori_loop(0, TOK // QT, tile, jnp.int32(0))

    def pair(slot, k, v):
        block = qslot_ref[slot]

        @pl.when(block >= 0)
        def _():
            rows = pl.ds(pl.multiple_of(block * BLK, BLK), BLK)
            flash(qs[rows, :], k(), v(), rows, m, l, acc)

    def base(s, carry):
        pair(s, lambda: base_ref[s // BASE, s % BASE, 0, 0], lambda: base_ref[s // BASE, s % BASE, 0, 1])
        return carry

    lax.fori_loop(0, 4 * BASE, base, jnp.int32(0))
    for s in (10, 11):
        pair(BIG_AT + s, lambda: big_ref[s, 0, 0], lambda: big_ref[s, 0, 1])
    for s in range(MID):
        pair(MID_AT + s, lambda: mid_ref[s, 0, 0], lambda: mid_ref[s, 0, 1])
    pair(ONE_AT, lambda: one_ref[0, 0, 0], lambda: one_ref[0, 0, 1])
    o_ref[:, 0] = (acc[...] / l[...]).astype(jnp.bfloat16).reshape(8, CH, DH)


def far(place, qslot, q, state, base, big, mid, one):
    nh = q.shape[1]
    tokens = pl.BlockSpec((8, 1, CH, DH), lambda h: (0, h, 0, 0))
    held = pl.BlockSpec((1, TOK, DH), lambda h: (h, 0, 0))

    def blocks(*lead):
        zeros = (0,) * len(lead)
        return pl.BlockSpec((*lead, 1, 2, BLK, DH), lambda h: (*zeros, h, 0, 0, 0))

    return pl.pallas_call(
        far_body,
        grid=(nh,),
        in_specs=[smem(), smem(), tokens, held, held, held, blocks(4, BASE), blocks(BIG), blocks(MID), blocks(ONE)],
        out_specs=tokens,
        out_shape=jax.ShapeDtypeStruct((8, nh, CH, DH), jnp.bfloat16),
        scratch_shapes=[pltpu.VMEM((TOK, DH), jnp.bfloat16)] + [pltpu.VMEM((TOK, DH), jnp.float32)] * 3,
        compiler_params=params(),
        name="far",
    )(place, qslot, q, *state, base, big, mid, one)


def leave_body(groups, *refs):
    *in_refs, o_ref, s = refs
    for ref, rows in zip(in_refs, groups, strict=True):
        for hd in range(8):
            for at, row in enumerate(rows):
                s[pl.ds(hd * PER + row, CH, stride=HEADS), :] = ref[hd, at].astype(jnp.float32)
    o_ref[...] = s[...].reshape(CH, HEADS, DH).astype(jnp.bfloat16)


def leave(parts, groups):
    return pl.pallas_call(
        lambda *refs: leave_body(groups, *refs),
        in_specs=[pl.BlockSpec(memory_space=pltpu.VMEM)] * len(parts),
        out_specs=pl.BlockSpec(memory_space=pltpu.VMEM),
        out_shape=jax.ShapeDtypeStruct((CH, HEADS, DH), jnp.bfloat16),
        scratch_shapes=[pltpu.VMEM((CH * HEADS, DH), jnp.float32)],
        compiler_params=params(),
        name="leave",
    )(*parts)


def at_plane(z, r):
    return PLANE * z + r


TM = ("z", "yh", "c")
BIG_PAIRS = [(at_plane(z, 0), at_plane(z + 1, 0)) for z in range(3)] + [(at_plane(z + 1, 3), at_plane(z, 3)) for z in range(3)]
MID_PAIRS = [(at_plane(z, 1), at_plane(z + 1, 1)) for z in range(3)] + [(at_plane(z + 1, 2), at_plane(z, 2)) for z in range(3)]
ONE_PAIRS = [(at_plane(z, 2), at_plane(z + 1, 2)) for z in range(3)] + [(at_plane(z + 1, 1), at_plane(z, 1)) for z in range(3)]


def shards(query, key, value, far_list, far_count):
    z, yh, c, hd = (lax.axis_index(a) for a in ("z", "yh", "c", "head"))
    r = 2 * yh + c
    place = jnp.stack([z, r, PLANE * z + r, hd, c]).astype(i32)
    rates = jnp.asarray(lane_rates())
    want, qslot, plane_pairs = tables(place, far_list, far_count)
    asked = lax.all_to_all(want, "z", 0, 0, tiled=True)
    parts = []
    for rows in CHUNKS:
        sent = enter_kv(place, rates, key, value, rows)
        own = lax.all_to_all(sent.reshape(16, len(rows), 2, CH, DH), ("yh", "head"), 0, 0, tiled=True)
        own = own.reshape(2, 8, len(rows), 2, CH, DH)
        sib = lax.ppermute(own, "c", [(0, 1), (1, 0)])
        q = lax.all_to_all(enter_q(place, rates, query, rows), "head", 0, 0, tiled=True)
        base, big, mid, one = pack(place, asked, own, sib)
        big = lax.ppermute(big, TM, BIG_PAIRS)
        base = lax.all_to_all(base, "z", 0, 0, tiled=True)
        mid = lax.ppermute(mid, TM, MID_PAIRS)
        one = lax.ppermute(one, TM, ONE_PAIRS)
        state = near(place, plane_pairs, q, own, sib)
        out = far(place, qslot, q, state, base, big, mid, one)
        parts.append(lax.all_to_all(out, "head", 0, 0, tiled=True))
    return leave(parts, CHUNKS)


def solution(mesh):
    split = Mesh(mesh.devices.reshape(4, 2, 2, 8), ("z", "yh", "c", "head"))
    tokens = P(("z", "yh", "c", "head"), None, None)
    blocks = P(TM, None)
    return jax.shard_map(
        shards,
        mesh=split,
        in_specs=(tokens, tokens, tokens, blocks, blocks),
        out_specs=tokens,
        check_vma=False,
    )
```

time: 613 us -> 277 us (0.45)
  local copies, waits for them, and re-layouts: 162 us -> 2.92 us
  matrix products: 151 us -> 0 us
  Pallas kernels: 0 us -> 121 us
  other arithmetic: 98.1 us -> 0 us
  loops' own time: 52.6 us -> 0 us
  blocking collectives: 21.8 us -> 70.6 us
  waiting for transfers between devices: 91.1 us -> 62.1 us
  between operations: 13.6 us -> 0.11 us
    dot_general x46 -> x0, matrix products: 151 us -> none  [the longest x16 54.8 us: far_update(): jnp.einsum('hqij,hqjd->hqid', weights.astype(jnp.bfloat16), chosen[1], pr...]
    pallas_call x0 -> x7, Pallas kernels: none -> 121 us  [the longest x1 54.5 us: far(): pl.pallas_call(far_body, grid=(nh,), in_specs=[smem(), smem(), tokens, he...]
    another operation x2 -> x0, loops' own time: 52.6 us -> none  [the longest x1 37.1 us: shards(): carried, _ = lax.scan(one_frame, carried, jnp.arange(frame_count))]
    all_to_all x1 -> x2, blocking collectives: 21.8 us -> 70.6 us  [the longest x1 55.2 us: shards(): lax.all_to_all(sent.reshape(16, len(rows), 2, CH, DH), ('yh', 'head'), 0,...]
    reduce_sum x22 -> x0, other arithmetic: 47.5 us -> none  [the longest x6 39 us: near_part(): row_total = jnp.sum(weights, axis=1)]
    gather x16 -> x0, local copies, waits for them, and re-layouts: 34.7 us -> none  [one_frame(): chosen = jnp.take(frame_kv, jnp.clip(wanted, 0, blocks_frame - 1), axis=2)]
    select_n x16 -> x0, other arithmetic: 30.1 us -> none  [one_frame(): chosen = jnp.take(frame_kv, jnp.clip(wanted, 0, blocks_frame - 1), axis=2)]
    slice x6 -> x0, local copies, waits for them, and re-layouts: 28.4 us -> none  [near_part(): beside_all[1]]
  transfers between devices with their start and end apart: 6 -> 7, of which waited for: 4 -> 3; matrix products, arithmetic and copies ran while one was open for 31% -> 0% of each run, Pallas kernels for 0% -> 21%
where the time goes in v1:
time: 277 us; the launch traced here: 276 us
  Pallas kernels  121 us (44%)
  blocking collectives  70.6 us (25%)
  waiting for transfers between devices  62.1 us (22%)
  starting transfers between devices  19.7 us (7%)
  local copies, waits for them, and re-layouts  2.92 us (1%)
    ppermute x1, waiting for transfers between devices, shards(): big = lax.ppermute(big, TM, BIG_PAIRS)  55.3 us
    all_to_all x1, blocking collectives, shards(): lax.all_to_all(sent.reshape(16, len(rows), 2, CH, DH), ('yh', 'head'), 0,...  55.2 us
    pallas_call x1, Pallas kernels, far(): pl.pallas_call(far_body, grid=(nh,), in_specs=[smem(), smem(), tokens, he...  54.5 us
    pallas_call x1, Pallas kernels, near(): pl.pallas_call(near_body, grid=(nh,), in_specs=[smem(), smem(), pl.BlockS...  41.8 us
    all_to_all x1, blocking collectives, shards(): parts.append(lax.all_to_all(out, 'head', 0, 0, tiled=True))  15.4 us
    pallas_call x1, Pallas kernels, pack(): pl.pallas_call(pack_body, grid=(nh, 2), in_specs=[smem(), smem(), whole,...  8.48 us
    all_to_all x1, waiting for transfers between devices, shards(): lax.all_to_all(enter_q(place, rates, query, rows), 'head', 0, 0, tiled=True)  6.62 us
    all_to_all x1, starting transfers between devices, shards(): base = lax.all_to_all(base, 'z', 0, 0, tiled=True)  6.01 us
  transfers between devices with their start and end apart: 7, of which 3 were waited for; matrix products, arithmetic and copies ran while one was open for 0% of the time, Pallas kernels for 21%

profile of v1, /device:TPU:32, one launch (start us, length us, event | category | flops | bytes accessed | tf_op | source)
XLA Modules:
  0.0 276.1 jit_solution(6693412011695005479)
XLA Ops:
  0.0 0.6 stack.23.place_ref.refs_0_
  0.6 5.2 %enter_kv.1 = bf16[2,8,3,2,160,128]{5,4,3,2,1,0:T(8,128)(2,1)} custom-call(s32[5]{0:T(128)} %stack.23.place_ref.refs_0_, f32[1,128]{1,0:T(1,128)} %constant.24.clone.refs_1_, bf16[160,24,128]{2,1,0:T(8,128)(2,1)} %refs_2_.3, bf16[160,24,128]{2,1,0:T(8,128)(2,1)} %refs_3_.1), custom_call_target="tpu_custom_call" | custom-call | tf_op jit(solution)/shard_map/enter_kv/pallas_call | solution.py:173
  5.8 55.2 %all_to_all.31 = bf16[16,3,2,160,128]{4,3,2,1,0:T(8,128)(2,1)} all-to-all(bf16[16,3,2,160,128]{4,3,2,1,0:T(8,128)(2,1)} %bitcast.11), channel_id=1, replica_groups=mesh['z'=4,'yh'=2,'c'=2,'head'=8] {'yh','head'}, dimensions={0} | all-to-all | bytes 7864320 | tf_op jit(solution)/shard_map/all_to_all | solution.py:444
  61.0 4.3 %tables.1 = (s32[4,128]{1,0:T(4,128)}, s32[64]{0:T(128)}, s32[16]{0:T(128)}) custom-call(s32[5]{0:T(128)} %stack.23.place_ref.refs_0_, s32[10,16]{1,0:T(8,128)} %list_ref.1, s32[10,16]{1,0:T(8,128)} %count_ref.1), custom_call_target="tpu_custom_call" | custom-call | tf_op jit(solution)/shard_map/tables/pallas_call | solution.py:120
  65.3 5.4 %all-to-all-start.2 = ((s32[4,1,128]{2,1,0:T(1,128)}), s32[4,1,128]{2,1,0:T(1,128)S(1)}, u32[]{:S(2)}, u32[]{:S(2)}) async-start(s32[4,1,128]{2,1,0:T(1,128)} %bitcast.13), calls=%async_computation.2 | async-start | bytes 4096 | tf_op jit(solution)/shard_map/all_to_all | solution.py:440
  70.7 3.6 %enter_q.1 = bf16[8,3,160,128]{3,2,1,0:T(8,128)(2,1)} custom-call(s32[5]{0:T(128)} %stack.23.place_ref.refs_0_, f32[1,128]{1,0:T(1,128)} %constant.24.clone.refs_1_, bf16[160,24,128]{2,1,0:T(8,128)(2,1)} %refs_2_.2), custom_call_target="tpu_custom_call" | custom-call | tf_op jit(solution)/shard_map/enter_q/pallas_call | solution.py:194
  74.3 0.2 all-to-all-done.2
  74.5 3.6 %all-to-all-start = ((bf16[8,3,160,128]{3,2,1,0:T(8,128)(2,1)}), bf16[8,3,160,128]{3,2,1,0:T(8,128)(2,1)S(1)}, u32[]{:S(2)}, u32[]{:S(2)}) async-start(bf16[8,3,160,128]{3,2,1,0:T(8,128)(2,1)} %enter_q.1), calls=%async_computation | async-start | bytes 1966080 | tf_op jit(solution)/shard_map/all_to_all | solution.py:447
  78.0 0.0 collective-permute-done.sib_ref
  78.1 8.5 %pack.1 = (bf16[4,8,3,2,128,128]{5,4,3,2,1,0:T(8,128)(2,1)}, bf16[12,3,2,128,128]{4,3,2,1,0:T(8,128)(2,1)}, bf16[4,3,2,128,128]{4,3,2,1,0:T(8,128)(2,1)}, bf16[1,3,2,128,128]{4,3,2,1,0:T(8,128)(2,1)}) custom-call(s32[5]{0:T(128)} %stack.23.place_ref.refs_0_, s32[4,128]{1,0:T(4,128)} %bitcast.12, bf16[2,8,3,2,160,128]{5,4,3,2,1,0:T(8,128)(2,1)} %bitcast.6.own_ref, ...), custom_call_target="tpu_custom_call" | custom-call | tf_op jit(solution)/shard_map/pack/pallas_call | solution.py:239
  86.5 6.6 %all-to-all-done.q_ref = bf16[8,3,160,128]{3,2,1,0:T(8,128)(2,1)S(1)} async-done(((bf16[8,3,160,128]{3,2,1,0:T(8,128)(2,1)}), bf16[8,3,160,128]{3,2,1,0:T(8,128)(2,1)S(1)}, u32[]{:S(2)}, u32[]{:S(2)}) %all-to-all-start) | async-done | bytes 983072 | tf_op jit(solution)/shard_map/all_to_all | solution.py:447
  93.2 0.9 copy-done
  94.1 6.0 %all-to-all-start.3 = ((bf16[4,8,3,2,128,128]{5,4,3,2,1,0:T(8,128)(2,1)}), bf16[4,8,3,2,128,128]{5,4,3,2,1,0:T(8,128)(2,1)}, u32[]{:S(2)}, u32[]{:S(2)}) async-start(bf16[4,8,3,2,128,128]{5,4,3,2,1,0:T(8,128)(2,1)} %get-tuple-element.21), calls=%async_computation.3 | async-start | bytes 12582912 | tf_op jit(solution)/shard_map/all_to_all | solution.py:450
  100.1 3.4 %collective-permute-start.1 = (bf16[12,3,2,128,128]{4,3,2,1,0:T(8,128)(2,1)}, bf16[12,3,2,128,128]{4,3,2,1,0:T(8,128)(2,1)S(1)}, u32[]{:S(2)}, u32[]{:S(2)}) collective-permute-start(bf16[12,3,2,128,128]{4,3,2,1,0:T(8,128)(2,1)} %get-tuple-element.22), channel_id=1, source_target_pairs={{0,32},{32,64},{64,96},{56,24},{88,56},{120,88},{1,33},{33,65},{65... | collective-permute-start | bytes 7077896 | tf_op jit(solution)/shard_map/ppermute | solution.py:449
  103.5 0.7 collective-permute-start.2
  104.2 0.7 collective-permute-start.3
  104.9 41.8 %near.1 = (f32[3,1280,128]{2,1,0:T(8,128)}, f32[3,1280,128]{2,1,0:T(8,128)}, f32[3,1280,128]{2,1,0:T(8,128)}) custom-call(s32[5]{0:T(128)} %stack.23.place_ref.refs_0_, s32[16]{0:T(128)} %get-tuple-element.16.plane_ref, bf16[8,3,160,128]{3,2,1,0:T(8,128)(2,1)} %copy-done, bf16[2,8,3,2,160,128]{5,4,3,2,1,0:T(8,128)(2,1)} %bitcast.6.own_ref, ...), custom_call_target="tpu_custom_call" | custom-call | flops 7549747200 | bytes 12582912 | tf_op jit(solution)/shard_map/near/pallas_call | solution.py:322
  146.7 0.0 collective-permute-done.3.one_ref
  146.8 0.0 collective-permute-done.2.mid_ref
  146.8 55.3 %collective-permute-done.1.big_ref = bf16[12,3,2,128,128]{4,3,2,1,0:T(8,128)(2,1)S(1)} collective-permute-done((bf16[12,3,2,128,128]{4,3,2,1,0:T(8,128)(2,1)}, bf16[12,3,2,128,128]{4,3,2,1,0:T(8,128)(2,1)S(1)}, u32[]{:S(2)}, u32[]{:S(2)}) %collective-permute-start.1) | collective-permute-done | bytes 2359328 | tf_op jit(solution)/shard_map/ppermute | solution.py:449
  202.0 1.4 copy-done.1
  203.4 54.5 %far.1 = bf16[8,3,160,128]{3,2,1,0:T(8,128)(2,1)} custom-call(s32[5]{0:T(128)} %stack.23.place_ref.refs_0_, s32[64]{0:T(128)} %get-tuple-element.15.qslot_ref, bf16[8,3,160,128]{3,2,1,0:T(8,128)(2,1)} %copy-done, f32[3,1280,128]{2,1,0:T(8,128)} %get-tuple-element.17.acc_in, f32[3,1280,128]{2,1,0:T(8,128)} %get-tuple-element.18.m_in, ...), custom_call_target="tpu_custom_call" | custom-call | tf_op jit(solution)/shard_map/far/pallas_call | solution.py:391
  257.9 15.4 %all_to_all.32.refs_0_ = bf16[8,3,160,128]{3,2,1,0:T(8,128)(2,1)} all-to-all(bf16[8,3,160,128]{3,2,1,0:T(8,128)(2,1)} %far.1), channel_id=1, replica_groups=mesh['z'=4,'yh'=2,'c'=2,'head'=8] {'head'}, dimensions={0} | all-to-all | bytes 1966080 | tf_op jit(solution)/shard_map/all_to_all | solution.py:455
  273.3 2.7 leave.1
  (12 shorter events, 0.0 us)
Async XLA Ops:
  61.0 17.1 %collective-permute-start = (bf16[2,8,3,2,160,128]{5,4,3,2,1,0:T(8,128)(2,1)}, bf16[2,8,3,2,160,128]{5,4,3,2,1,0:T(8,128)(2,1)}, u32[]{:S(2)}, u32[]{:S(2)}) collective-permute-start(bf16[2,8,3,2,160,128]{5,4,3,2,1,0:T(8,128)(2,1)} %bitcast.6.own_ref), channel_id=1, source_target_pairs={{0,8},{8,0},{1,9},{9,1},{2,10},{10,2},{3,11},{11,3},{4,12},{12,4},... | collective-permute-start | bytes 11796488 | tf_op jit(solution)/shard_map/ppermute | solution.py:446
  65.3 9.2 %all-to-all-start.2 = ((s32[4,1,128]{2,1,0:T(1,128)}), s32[4,1,128]{2,1,0:T(1,128)S(1)}, u32[]{:S(2)}, u32[]{:S(2)}) async-start(s32[4,1,128]{2,1,0:T(1,128)} %bitcast.13), calls=%async_computation.2 | async-start | bytes 4096 | tf_op jit(solution)/shard_map/all_to_all | solution.py:440
  74.5 3.6 %copy-start.4 = (s32[4,1,128]{2,1,0:T(1,128)}, s32[4,1,128]{2,1,0:T(1,128)S(1)}, u32[]{:S(2)}) copy-start(s32[4,1,128]{2,1,0:T(1,128)S(1)} %all-to-all-done.2) | copy-start | bytes 6148
  74.5 18.7 %all-to-all-start = ((bf16[8,3,160,128]{3,2,1,0:T(8,128)(2,1)}), bf16[8,3,160,128]{3,2,1,0:T(8,128)(2,1)S(1)}, u32[]{:S(2)}, u32[]{:S(2)}) async-start(bf16[8,3,160,128]{3,2,1,0:T(8,128)(2,1)} %enter_q.1), calls=%async_computation | async-start | bytes 1966080 | tf_op jit(solution)/shard_map/all_to_all | solution.py:447
  93.2 0.9 copy-start
  93.2 11.0 %copy-start.5 = (bf16[1,3,2,128,128]{4,3,2,1,0:T(8,128)(2,1)S(1)}, bf16[1,3,2,128,128]{4,3,2,1,0:T(8,128)(2,1)}, u32[]{:S(2)}) copy-start(bf16[1,3,2,128,128]{4,3,2,1,0:T(8,128)(2,1)} %get-tuple-element.24) | copy-start | bytes 589828
  94.1 107.9 %all-to-all-start.3 = ((bf16[4,8,3,2,128,128]{5,4,3,2,1,0:T(8,128)(2,1)}), bf16[4,8,3,2,128,128]{5,4,3,2,1,0:T(8,128)(2,1)}, u32[]{:S(2)}, u32[]{:S(2)}) async-start(bf16[4,8,3,2,128,128]{5,4,3,2,1,0:T(8,128)(2,1)} %get-tuple-element.21), calls=%async_computation.3 | async-start | bytes 12582912 | tf_op jit(solution)/shard_map/all_to_all | solution.py:450
  100.1 101.9 %collective-permute-start.1 = (bf16[12,3,2,128,128]{4,3,2,1,0:T(8,128)(2,1)}, bf16[12,3,2,128,128]{4,3,2,1,0:T(8,128)(2,1)S(1)}, u32[]{:S(2)}, u32[]{:S(2)}) collective-permute-start(bf16[12,3,2,128,128]{4,3,2,1,0:T(8,128)(2,1)} %get-tuple-element.22), channel_id=1, source_target_pairs={{0,32},{32,64},{64,96},{56,24},{88,56},{120,88},{1,33},{33,65},{65... | collective-permute-start | bytes 7077896 | tf_op jit(solution)/shard_map/ppermute | solution.py:449
  103.5 43.3 %collective-permute-start.2 = (bf16[4,3,2,128,128]{4,3,2,1,0:T(8,128)(2,1)}, bf16[4,3,2,128,128]{4,3,2,1,0:T(8,128)(2,1)S(1)}, u32[]{:S(2)}, u32[]{:S(2)}) collective-permute-start(bf16[4,3,2,128,128]{4,3,2,1,0:T(8,128)(2,1)} %get-tuple-element.23), channel_id=1, source_target_pairs={{8,40},{40,72},{72,104},{48,16},{80,48},{112,80},{9,41},{41,73},{7... | collective-permute-start | bytes 2359304 | tf_op jit(solution)/shard_map/ppermute | solution.py:451
  104.2 42.5 %collective-permute-start.3 = (bf16[1,3,2,128,128]{4,3,2,1,0:T(8,128)(2,1)S(1)}, bf16[1,3,2,128,128]{4,3,2,1,0:T(8,128)(2,1)S(1)}, u32[]{:S(2)}, u32[]{:S(2)}) collective-permute-start(bf16[1,3,2,128,128]{4,3,2,1,0:T(8,128)(2,1)S(1)} %copy-done.5), channel_id=1, source_target_pairs={{16,48},{48,80},{80,112},{40,8},{72,40},{104,72},{17,49},{49,81},{... | collective-permute-start | bytes 589832 | tf_op jit(solution)/shard_map/ppermute | solution.py:452
  146.7 55.3 %copy-start.3 = (bf16[1,3,2,128,128]{4,3,2,1,0:T(8,128)(2,1)}, bf16[1,3,2,128,128]{4,3,2,1,0:T(8,128)(2,1)S(1)}, u32[]{:S(2)}) copy-start(bf16[1,3,2,128,128]{4,3,2,1,0:T(8,128)(2,1)S(1)} %collective-permute-done.3.one_ref) | copy-start | bytes 589828
  146.8 55.3 %copy-start.2 = (bf16[4,3,2,128,128]{4,3,2,1,0:T(8,128)(2,1)}, bf16[4,3,2,128,128]{4,3,2,1,0:T(8,128)(2,1)S(1)}, u32[]{:S(2)}) copy-start(bf16[4,3,2,128,128]{4,3,2,1,0:T(8,128)(2,1)S(1)} %collective-permute-done.2.mid_ref) | copy-start | bytes 2359300
  202.0 1.4 copy-start.1

commit v2 on v1

v2 whole, which is shorter than its diff:
```python
import jax
import jax.numpy as jnp
import numpy as np
from jax import lax
from jax.experimental import pallas as pl
from jax.experimental.pallas import tpu as pltpu
from jax.sharding import Mesh
from jax.sharding import PartitionSpec as P

FW = 80
TOK = 1280
BLK = 128
CH = 160
NB = 10
DH = 128
RT, RH, RW = 16, 56, 56
HEADS = 24
PER = 3
PLANE = 4
THETA = 256.0
SCALE = float(DH**-0.5 * np.log2(np.e))
CHUNKS = ((0,), (1, 2))

BASE = 8
BESIDE = 9
BIG = 11
MID = 3
VMEM = 58 * 2**20

i32 = jnp.int32


def params():
    return pltpu.CompilerParams(vmem_limit_bytes=VMEM)


def smem():
    return pl.BlockSpec(memory_space=pltpu.SMEM)


def table_body(place_ref, list_ref, count_ref, want_ref, qslot_ref, late_ref, plane_ref, kb_ref, qb_ref):
    z, r = place_ref[0], place_ref[1]
    f = PLANE * z + r

    def frame_lists(g, carry):
        for j in range(8):
            kb_ref[g * 8 + j] = 0
            qb_ref[g * 8 + j] = 0

        def one_block(n, filled):
            kb_ref[g * 8 + filled] = list_ref[n, g] - NB * g
            qb_ref[g * 8 + filled] = n
            return filled + jnp.where(count_ref[n, g] > 0, 1, 0).astype(i32)

        lax.fori_loop(0, NB, one_block, jnp.int32(0))
        return carry

    lax.fori_loop(0, PLANE * 4, frame_lists, jnp.int32(0))

    def clear(s, carry):
        for zp in range(4):
            want_ref[zp, s] = 0
        return carry

    lax.fori_loop(0, 128, clear, jnp.int32(0))
    for s in range(64):
        qslot_ref[s] = -1
    for s in range(MID):
        late_ref[s] = -1
    for zp in range(4):
        for i in range(PLANE):
            g = PLANE * zp + i
            far = jnp.abs(f - g) >= 2
            for j in range(2):
                want_ref[zp, 2 * i + j] = NB * i + kb_ref[g * 8 + j]
                qslot_ref[zp * BESIDE + 2 * i + j] = jnp.where(far & (z != zp), qb_ref[g * 8 + j], -1)

    def listed(zp, s, i, j):
        at = (PLANE * zp + i) * 8 + j
        want_ref[zp, s] = NB * i + kb_ref[at]
        qslot_ref[zp * BESIDE + s] = qb_ref[at]

    def side(up, first, second, third):
        zp = z - 1 if up else z + 1
        exists = z > 0 if up else z < 3
        near, two, three = (3, 2, 1) if up else (0, 1, 2)

        @pl.when(exists & (r == first))
        def _():
            for j in range(2):
                listed(zp, 2 * near + j, two, 2 + j)
            listed(zp, BASE, two, 4)
            for n in range(NB):
                want_ref[zp, BESIDE + n] = NB * near + n
            at = (PLANE * zp + three) * 8 + 2
            want_ref[zp, BESIDE + NB] = NB * three + kb_ref[at]
            late_ref[0] = qb_ref[at]

        @pl.when(exists & (r == second))
        def _():
            listed(zp, BASE, two, 2)
            for j in range(MID):
                at = (PLANE * zp + near) * 8 + 2 + j
                want_ref[zp, BESIDE + BIG + j] = NB * near + kb_ref[at]
                late_ref[j] = qb_ref[at]

        @pl.when(exists & (r == third))
        def _():
            listed(zp, BASE, near, 2)

    side(True, 0, 1, 2)
    side(False, 3, 2, 1)

    two = (r + 2) % PLANE
    three = PLANE - 1 - r
    outer = (r == 0) | (r == PLANE - 1)
    for j in range(5):
        at = (PLANE * z + two) * 8 + j
        plane_ref[2 * j] = qb_ref[at]
        plane_ref[2 * j + 1] = NB * two + kb_ref[at]
    for j in range(3):
        at = (PLANE * z + three) * 8 + j
        plane_ref[10 + 2 * j] = jnp.where(outer, qb_ref[at], -1)
        plane_ref[10 + 2 * j + 1] = NB * three + kb_ref[at]


def tables(place, far_list, far_count):
    return pl.pallas_call(
        table_body,
        in_specs=[smem(), smem(), smem()],
        out_specs=[smem(), smem(), smem(), smem()],
        out_shape=[
            jax.ShapeDtypeStruct((4, 128), i32),
            jax.ShapeDtypeStruct((64,), i32),
            jax.ShapeDtypeStruct((MID,), i32),
            jax.ShapeDtypeStruct((16,), i32),
        ],
        scratch_shapes=[pltpu.SMEM((128,), i32), pltpu.SMEM((128,), i32)],
        name="tables",
    )(place, far_list, far_count)


def lane_rates():
    rates = []
    for width in (RT, RH, RW):
        rates.append(np.float32(THETA) ** (np.float32(-2.0) * np.arange(width // 2, dtype=np.float32) / np.float32(width)))
    return np.repeat(np.concatenate(rates), 2)[None].astype(np.float32)


def turn_tables(frame, chunk, rates):
    lane = lax.broadcasted_iota(i32, (CH, DH), 1)
    token = lax.broadcasted_iota(i32, (CH, DH), 0)
    below = (token >= FW).astype(i32)
    position = jnp.where(lane < RT, frame, jnp.where(lane < RT + RH, 2 * chunk + below, token - FW * below))
    angle = position.astype(jnp.float32) * rates
    even = lane % 2 == 0
    sine = jnp.sin(angle)
    return jnp.cos(angle), jnp.where(even, -sine, sine), even


def turn(x, tables_):
    cosine, sine, even = tables_
    swapped = jnp.where(even, pltpu.roll(x, DH - 1, 1), pltpu.roll(x, 1, 1))
    return x * cosine + swapped * sine


def enter_kv_body(rows, place_ref, rates_ref, k_ref, v_ref, o_ref, ks, vs):
    tabs = turn_tables(place_ref[2], place_ref[3], rates_ref[...])
    ks[...] = k_ref[...].astype(jnp.float32).reshape(CH * HEADS, DH)
    vs[...] = v_ref[...].astype(jnp.float32).reshape(CH * HEADS, DH)
    for hd in range(8):
        for at, row in enumerate(rows):
            pick = pl.ds(hd * PER + row, CH, stride=HEADS)
            turned = turn(ks[pick, :], tabs).astype(jnp.bfloat16)
            kept = vs[pick, :].astype(jnp.bfloat16)
            for yh in range(2):
                o_ref[yh, hd, at, 0] = turned
                o_ref[yh, hd, at, 1] = kept


def enter_kv(place, rates, key, value, rows):
    return pl.pallas_call(
        lambda *refs: enter_kv_body(rows, *refs),
        in_specs=[smem()] + [pl.BlockSpec(memory_space=pltpu.VMEM)] * 3,
        out_specs=pl.BlockSpec(memory_space=pltpu.VMEM),
        out_shape=jax.ShapeDtypeStruct((2, 8, len(rows), 2, CH, DH), jnp.bfloat16),
        scratch_shapes=[pltpu.VMEM((CH * HEADS, DH), jnp.float32)] * 2,
        compiler_params=params(),
        name="enter_kv",
    )(place, rates, key, value)


def enter_q_body(rows, place_ref, rates_ref, q_ref, o_ref, qs):
    tabs = turn_tables(place_ref[2], place_ref[3], rates_ref[...])
    qs[...] = q_ref[...].astype(jnp.float32).reshape(CH * HEADS, DH)
    for hd in range(8):
        for at, row in enumerate(rows):
            pick = pl.ds(hd * PER + row, CH, stride=HEADS)
            o_ref[hd, at] = turn(qs[pick, :], tabs).astype(jnp.bfloat16)


def enter_q(place, rates, query, rows):
    return pl.pallas_call(
        lambda *refs: enter_q_body(rows, *refs),
        in_specs=[smem()] + [pl.BlockSpec(memory_space=pltpu.VMEM)] * 2,
        out_specs=pl.BlockSpec(memory_space=pltpu.VMEM),
        out_shape=jax.ShapeDtypeStruct((8, len(rows), CH, DH), jnp.bfloat16),
        scratch_shapes=[pltpu.VMEM((CH * HEADS, DH), jnp.float32)],
        compiler_params=params(),
        name="enter_q",
    )(place, rates, query)


def pack_body(place_ref, ask1, ask2, ask3, own_ref, sib_ref, big_ref, mid_ref, out1, out2, out3, frames):
    z, r, c = place_ref[0], place_ref[1], place_ref[4]
    for b in range(2):
        for ref, core in ((own_ref, c), (sib_ref, 1 - c)):
            start = pl.multiple_of((2 * b + core) * TOK, TOK)
            frames[pl.ds(start, TOK), :] = ref[b, :, 0, 0].reshape(TOK, DH)

    def block(index):
        return frames[pl.ds(pl.multiple_of(index * BLK, BLK), BLK), :]

    for s in range(BIG + MID):
        index = jnp.where(r < 2, ask1[z, BESIDE + s], ask3[z, BESIDE + s])
        if s < BIG:
            big_ref[s, 0, 0] = block(index)
        else:
            mid_ref[s - BIG, 0, 0] = block(index)
    for ask, ref in ((ask1, out1), (ask2, out2), (ask3, out3)):
        for s in range(ref.shape[0]):
            ref[s, 0, 0] = block(ask[z, s])


def pack(place, asked, own, sib):
    nh = own.shape[2]
    whole = pl.BlockSpec((2, 8, 1, 1, CH, DH), lambda h, kv: (0, 0, h, kv, 0, 0))

    def out(n):
        return pl.BlockSpec((n, 1, 1, BLK, DH), lambda h, kv: (0, h, kv, 0, 0))

    sizes = (BIG, MID, BESIDE, BASE, BESIDE)
    return pl.pallas_call(
        pack_body,
        grid=(nh, 2),
        in_specs=[smem()] * 4 + [whole, whole],
        out_specs=[out(n) for n in sizes],
        out_shape=[jax.ShapeDtypeStruct((n, nh, 2, BLK, DH), jnp.bfloat16) for n in sizes],
        scratch_shapes=[pltpu.VMEM((PLANE * TOK, DH), jnp.bfloat16)],
        compiler_params=params(),
        name="pack",
    )(place, *asked, own, sib)


def dot_t(a, b):
    return lax.dot_general(a, b, (((1,), (1,)), ((), ())), preferred_element_type=jnp.float32)


def lane_sum(p):
    total = p[:, :DH]
    for at in range(DH, p.shape[1], DH):
        total = total + p[:, at : at + DH]
    return total


def by_lane(op, x):
    total = x[:, :DH]
    for at in range(DH, x.shape[1], DH):
        total = op(total, x[:, at : at + DH])
    return total


def listed_pairs(pairs, qs, m, l, acc, top, scores):
    def rows_of(block):
        return pl.ds(pl.multiple_of(jnp.maximum(block, 0) * BLK, BLK), BLK)

    top[...] = m[...]
    for n, (block, k, _) in enumerate(pairs):
        rows = rows_of(block)
        s = jnp.where(block >= 0, dot_t(qs[rows, :], k()) * SCALE, NONE)
        scores[n] = s
        top[rows, :] = jnp.maximum(top[rows, :], s)
    m_new = jnp.broadcast_to(jnp.max(top[...], axis=1, keepdims=True), (TOK, DH))
    fade = jnp.exp2(m[...] - m_new)
    acc[...] = acc[...] * fade
    l[...] = l[...] * fade
    m[...] = m_new
    for n, (block, _, v) in enumerate(pairs):
        rows = rows_of(block)
        p = jnp.exp2(scores[n] - m[rows, :])
        l[rows, :] += p
        acc[rows, :] += jnp.dot(p.astype(jnp.bfloat16), v(), preferred_element_type=jnp.float32)


QT = 256
NONE = -1e30


def near_body(place_ref, plane_ref, q_ref, own_ref, sib_ref, acc_ref, m_ref, l_ref, qs, kf, vf, top, scores):
    r, c = place_ref[1], place_ref[4]
    qs[...] = q_ref[:, 0].reshape(TOK, DH)
    for b in range(2):
        for ref, core in ((own_ref, c), (sib_ref, 1 - c)):
            start = pl.multiple_of((2 * b + core) * TOK, TOK)
            kf[pl.ds(start, TOK), :] = ref[b, :, 0, 0].reshape(TOK, DH)
            vf[pl.ds(start, TOK), :] = ref[b, :, 0, 1].reshape(TOK, DH)
    acc, m, l = acc_ref.at[0], m_ref.at[0], l_ref.at[0]

    def part(index, size):
        return pl.ds(pl.multiple_of(index * size, size), size)

    third = (r > 0) & (r < PLANE - 1)
    frames = [part(i, TOK) for i in (r, jnp.where(r == 0, 1, r - 1), jnp.where(third, r + 1, r))]

    def tile(t, carry):
        rows = part(t, QT)
        q = qs[rows, :]
        scored = [dot_t(q, kf[at, :]) * SCALE for at in frames]
        scored[2] = jnp.where(third, scored[2], NONE)
        tops = [by_lane(jnp.maximum, s) for s in scored]
        best = jnp.max(jnp.maximum(jnp.maximum(tops[0], tops[1]), tops[2]), axis=1, keepdims=True)
        total = mixed = 0.0
        for s, at in zip(scored, frames, strict=True):
            p = jnp.exp2(s - best)
            total = total + by_lane(jnp.add, p)
            mixed = mixed + jnp.dot(p.astype(jnp.bfloat16), vf[at, :], preferred_element_type=jnp.float32)
        m[rows, :] = jnp.broadcast_to(best, (QT, DH))
        l[rows, :] = total
        acc[rows, :] = mixed
        return carry

    lax.fori_loop(0, TOK // QT, tile, jnp.int32(0))

    def pair(p):
        at = part(plane_ref[2 * p + 1], BLK)
        return plane_ref[2 * p], lambda: kf[at, :], lambda: vf[at, :]

    listed_pairs([pair(p) for p in range(8)], qs, m, l, acc, top, scores)


def head_specs(first):
    tokens = pl.BlockSpec((8, 1, CH, DH), lambda h: (0, h + first if first else h, 0, 0))
    state = pl.BlockSpec((1, TOK, DH), lambda h: (h, 0, 0))
    return tokens, state


def state_shapes(nh):
    return [jax.ShapeDtypeStruct((nh, TOK, DH), jnp.float32)] * 3


def near(place, plane_pairs, q, own, sib, first):
    nh = own.shape[2]
    frames = pl.BlockSpec((2, 8, 1, 2, CH, DH), lambda h: (0, 0, h, 0, 0, 0))
    tokens, state = head_specs(first)
    return pl.pallas_call(
        near_body,
        grid=(nh,),
        in_specs=[smem(), smem(), tokens, frames, frames],
        out_specs=[state] * 3,
        out_shape=state_shapes(nh),
        scratch_shapes=[
            pltpu.VMEM((TOK, DH), jnp.bfloat16),
            pltpu.VMEM((PLANE * TOK, DH), jnp.bfloat16),
            pltpu.VMEM((PLANE * TOK, DH), jnp.bfloat16),
            pltpu.VMEM((TOK, DH), jnp.float32),
            pltpu.VMEM((8, BLK, BLK), jnp.float32),
        ],
        compiler_params=params(),
        name="near",
    )(place, plane_pairs, q, own, sib)


def cross_body(place_ref, q_ref, big_ref, acc_in, m_in, l_in, acc_ref, m_ref, l_ref):
    z, r = place_ref[0], place_ref[1]
    touches = ((r == 0) & (z > 0)) | ((r == PLANE - 1) & (z < 3))

    @pl.when(touches)
    def _():
        k = big_ref[:NB, 0, 0].reshape(TOK, DH)
        v = big_ref[:NB, 0, 1].reshape(TOK, DH)
        q = q_ref[:, 0].reshape(TOK, DH)
        for t in range(TOK // QT):
            rows = slice(t * QT, (t + 1) * QT)
            s = dot_t(q[rows], k) * SCALE
            m_old = m_in[0, rows]
            m_new = jnp.maximum(m_old, jnp.max(by_lane(jnp.maximum, s), axis=1, keepdims=True))
            p = jnp.exp2(s - m_new[:, :1])
            fade = jnp.exp2(m_old - m_new)
            m_ref[0, rows] = m_new
            l_ref[0, rows] = l_in[0, rows] * fade + by_lane(jnp.add, p)
            mixed = jnp.dot(p.astype(jnp.bfloat16), v, preferred_element_type=jnp.float32)
            acc_ref[0, rows] = acc_in[0, rows] * fade + mixed

    @pl.when(jnp.logical_not(touches))
    def _():
        acc_ref[...] = acc_in[...]
        m_ref[...] = m_in[...]
        l_ref[...] = l_in[...]


def cross(place, q, big, state, first):
    nh = big.shape[1]
    tokens, held = head_specs(first)
    blocks = pl.BlockSpec((BIG, 1, 2, BLK, DH), lambda h: (0, h, 0, 0, 0))
    return pl.pallas_call(
        cross_body,
        grid=(nh,),
        in_specs=[smem(), tokens, blocks, held, held, held],
        out_specs=[held] * 3,
        out_shape=state_shapes(nh),
        compiler_params=params(),
        name="cross",
    )(place, q, big, *state)


def far_body(
    place_ref, qslot_ref, late_ref, q_ref, acc_in, m_in, l_in, in1, in2, in3, big_ref, mid_ref, o_ref, qs, acc, m, l, top, scores
):
    z, r = place_ref[0], place_ref[1]
    qs[...] = q_ref[:, 0].reshape(TOK, DH)
    acc[...] = acc_in[0]
    m[...] = m_in[0]
    l[...] = l_in[0]
    pairs = []
    for shift, ref in ((1, in1), (2, in2), (3, in3)):
        zp = (z + 4 - shift) % 4
        for s in range(ref.shape[0]):
            block = qslot_ref[zp * BESIDE + s]
            pairs.append((block, lambda ref=ref, s=s: ref[s, 0, 0], lambda ref=ref, s=s: ref[s, 0, 1]))
    outer = (r == 0) | (r == PLANE - 1)
    for s in range(MID):

        def either(kv, s=s):
            return jnp.where(outer, big_ref[NB, 0, kv], mid_ref[s, 0, kv])

        pairs.append((late_ref[s], lambda either=either: either(0), lambda either=either: either(1)))
    listed_pairs(pairs, qs, m, l, acc, top, scores)
    total = jnp.sum(l[...], axis=1, keepdims=True)
    o_ref[:, 0] = (acc[...] / total).astype(jnp.bfloat16).reshape(8, CH, DH)


def far(place, qslot, late, q, state, crossed, first):
    nh = crossed[0].shape[1]
    tokens, held = head_specs(first)
    blocks = [pl.BlockSpec((x.shape[0], 1, 2, BLK, DH), lambda h: (0, h, 0, 0, 0)) for x in crossed]
    return pl.pallas_call(
        far_body,
        grid=(nh,),
        in_specs=[smem(), smem(), smem(), tokens, held, held, held] + blocks,
        out_specs=pl.BlockSpec((8, 1, CH, DH), lambda h: (0, h, 0, 0)),
        out_shape=jax.ShapeDtypeStruct((8, nh, CH, DH), jnp.bfloat16),
        scratch_shapes=[pltpu.VMEM((TOK, DH), jnp.bfloat16)]
        + [pltpu.VMEM((TOK, DH), jnp.float32)] * 4
        + [pltpu.VMEM((2 * BESIDE + BASE + MID, BLK, BLK), jnp.float32)],
        compiler_params=params(),
        name="far",
    )(place, qslot, late, q, *state, *crossed)


def leave_body(groups, *refs):
    *in_refs, o_ref, s = refs
    for ref, rows in zip(in_refs, groups, strict=True):
        for hd in range(8):
            for at, row in enumerate(rows):
                s[pl.ds(hd * PER + row, CH, stride=HEADS), :] = ref[hd, at].astype(jnp.float32)
    o_ref[...] = s[...].reshape(CH, HEADS, DH).astype(jnp.bfloat16)


def leave(parts, groups):
    return pl.pallas_call(
        lambda *refs: leave_body(groups, *refs),
        in_specs=[pl.BlockSpec(memory_space=pltpu.VMEM)] * len(parts),
        out_specs=pl.BlockSpec(memory_space=pltpu.VMEM),
        out_shape=jax.ShapeDtypeStruct((CH, HEADS, DH), jnp.bfloat16),
        scratch_shapes=[pltpu.VMEM((CH * HEADS, DH), jnp.float32)],
        compiler_params=params(),
        name="leave",
    )(*parts)


def at_plane(z, r):
    return PLANE * z + r


TM = ("z", "yh", "c")
BIG_PAIRS = [(at_plane(z, 0), at_plane(z + 1, 0)) for z in range(3)] + [(at_plane(z + 1, 3), at_plane(z, 3)) for z in range(3)]

MID_PAIRS = [(at_plane(z, 1), at_plane(z + 1, 1)) for z in range(3)] + [(at_plane(z + 1, 2), at_plane(z, 2)) for z in range(3)]


def together(*values):
    return lax.optimization_barrier(values)


def shards(query, key, value, far_list, far_count):
    z, yh, c, hd = (lax.axis_index(a) for a in ("z", "yh", "c", "head"))
    r = 2 * yh + c
    place = jnp.stack([z, r, PLANE * z + r, hd, c]).astype(i32)
    rates = jnp.asarray(lane_rates())
    first, rest = CHUNKS
    a_at, b_at = first[0], rest[0]

    def around(x, shift):
        return lax.ppermute(x, "z", [(i, (i + shift) % 4) for i in range(4)])

    def entry(sent):
        nh = sent.shape[2]
        own = lax.all_to_all(sent.reshape(16, nh, 2, CH, DH), ("yh", "head"), 0, 0, tiled=True)
        return own.reshape(2, 8, nh, 2, CH, DH)

    def swap(x):
        return lax.ppermute(x, "c", [(0, 1), (1, 0)])

    def by_head(x):
        return lax.all_to_all(x, "head", 0, 0, tiled=True)

    def send(packed):
        big, mid, *base = packed
        big = lax.ppermute(big, TM, BIG_PAIRS)
        base = [around(x, shift) for shift, x in zip((1, 2, 3), base, strict=True)]
        return [*base, big, lax.ppermute(mid, TM, MID_PAIRS)]

    sent_a = enter_kv(place, rates, key, value, first)
    far_list, key, value, query, sent_a = together(far_list, key, value, query, sent_a)
    want, qslot, late, plane_pairs = tables(place, far_list, far_count)
    asked = [around(want, -shift) for shift in (1, 2, 3)]
    sent_b = enter_kv(place, rates, key, value, rest)
    sent_q = enter_q(place, rates, query, first + rest)
    own_a = entry(sent_a)
    own_a, sent_b, sent_q, asked = together(own_a, sent_b, sent_q, asked)
    sib_a = swap(own_a)
    own_b = entry(sent_b)
    packed_a = pack(place, asked, own_a, sib_a)
    crossed_a = send(packed_a)
    own_b, sent_q, crossed_a = together(own_b, sent_q, crossed_a)
    sib_b = swap(own_b)
    q = by_head(sent_q)
    packed_b = pack(place, asked, own_b, sib_b)
    crossed_b = send(packed_b)
    q, _ = together(q, packed_b)
    state_a = near(place, plane_pairs, q, own_a, sib_a, a_at)
    state_a = cross(place, q, crossed_a[3], state_a, a_at)
    done_a = far(place, qslot, late, q, state_a, crossed_a, a_at)
    out_a = by_head(done_a)
    q, _ = together(q, done_a)
    state_b = near(place, plane_pairs, q, own_b, sib_b, b_at)
    state_b = cross(place, q, crossed_b[3], state_b, b_at)
    out_b = by_head(far(place, qslot, late, q, state_b, crossed_b, b_at))
    return leave((out_a, out_b), CHUNKS)


def solution(mesh):
    split = Mesh(mesh.devices.reshape(4, 2, 2, 8), ("z", "yh", "c", "head"))
    tokens = P(("z", "yh", "c", "head"), None, None)
    blocks = P(TM, None)
    return jax.shard_map(
        shards,
        mesh=split,
        in_specs=(tokens, tokens, tokens, blocks, blocks),
        out_specs=tokens,
        check_vma=False,
    )
```

time: 277 us -> 209 us (0.75)
  blocking collectives: 70.6 us -> 14.9 us
  Pallas kernels: 121 us -> 90.5 us
  starting transfers between devices: 19.7 us -> 47.1 us
  waiting for transfers between devices: 62.1 us -> 46.7 us
  local copies, waits for them, and re-layouts: 2.92 us -> 8.16 us
    all_to_all x2 -> x1, blocking collectives: 70.6 us -> 14.9 us  [by_head(): return lax.all_to_all(x, 'head', 0, 0, tiled=True)]
    pallas_call x3 -> x8, Pallas kernels: 105 us -> 72 us  [the longest x2 34.5 us: near(): pl.pallas_call(near_body, grid=(nh,), in_specs=[smem(), smem(), tokens, f...]
    ppermute x4 -> x15, waiting for transfers between devices: 55.3 us -> 32.8 us  [the longest x9 24.7 us: around(): return lax.ppermute(x, 'z', [(i, (i + shift) % 4) for i in range(4)])]
    ppermute x4 -> x15, starting transfers between devices: 4.75 us -> 26.5 us  [the longest x2 12.4 us: send(): big = lax.ppermute(big, TM, BIG_PAIRS)]
    all_to_all x3 -> x4, waiting for transfers between devices: 6.83 us -> 13.9 us  [the longest x2 11 us: by_head(): return lax.all_to_all(x, 'head', 0, 0, tiled=True)]
    all_to_all x3 -> x4, starting transfers between devices: 15 us -> 20.6 us  [the longest x2 11.4 us: entry(): lax.all_to_all(sent.reshape(16, nh, 2, CH, DH), ('yh', 'head'), 0, 0, til...]
    unnamed x12 -> x30, local copies, waits for them, and re-layouts: 2.33 us -> 7.5 us
    pallas_call x1 -> x2, Pallas kernels: 5.18 us -> 7.89 us  [enter_kv(): pl.pallas_call(lambda *refs: enter_kv_body(rows, *refs), in_specs=[smem()...]
  transfers between devices with their start and end apart: 7 -> 19, of which waited for: 3 -> 6; matrix products, arithmetic and copies ran while one was open for 0% -> 0% of each run, Pallas kernels for 21% -> 38%
where the time goes in v2:
time: 209 us; the launch traced here: 208 us
  Pallas kernels  90.5 us (43%)
  starting transfers between devices  47.1 us (23%)
  waiting for transfers between devices  46.7 us (22%)
  blocking collectives  14.9 us (7%)
  local copies, waits for them, and re-layouts  8.16 us (4%)
    pallas_call x2, Pallas kernels, near(): pl.pallas_call(near_body, grid=(nh,), in_specs=[smem(), smem(), tokens, f...  34.5 us
    ppermute x9, waiting for transfers between devices, around(): return lax.ppermute(x, 'z', [(i, (i + shift) % 4) for i in range(4)])  24.7 us
    pallas_call x2, Pallas kernels, cross(): pl.pallas_call(cross_body, grid=(nh,), in_specs=[smem(), tokens, blocks,...  17.1 us
    all_to_all x1, blocking collectives, by_head(): return lax.all_to_all(x, 'head', 0, 0, tiled=True)  14.9 us
    ppermute x2, starting transfers between devices, send(): big = lax.ppermute(big, TM, BIG_PAIRS)  12.4 us
    ppermute x9, starting transfers between devices, around(): return lax.ppermute(x, 'z', [(i, (i + shift) % 4) for i in range(4)])  11.9 us
    pallas_call x2, Pallas kernels, far(): pl.pallas_call(far_body, grid=(nh,), in_specs=[smem(), smem(), smem(), to...  11.9 us
    all_to_all x2, starting transfers between devices, entry(): lax.all_to_all(sent.reshape(16, nh, 2, CH, DH), ('yh', 'head'), 0, 0, til...  11.4 us
  transfers between devices with their start and end apart: 19, of which 6 were waited for; matrix products, arithmetic and copies ran while one was open for 0% of the time, Pallas kernels for 38%

profile of v2, /device:TPU:32, one launch (start us, length us, event | category | flops | bytes accessed | tf_op | source)
XLA Modules:
  0.0 207.6 jit_solution(6621228350534273654)
XLA Ops:
  0.7 3.5 %enter_kv.2 = bf16[2,8,1,2,160,128]{5,4,3,2,1,0:T(8,128)(2,1)} custom-call(s32[5]{0:T(128)} %stack.23.refs_0_.place_ref, f32[1,128]{1,0:T(1,128)} %constant.24.clone.refs_1_, bf16[160,24,128]{2,1,0:T(8,128)(2,1)} %refs_2_.2, bf16[160,24,128]{2,1,0:T(8,128)(2,1)} %refs_3_.2), custom_call_target="tpu_custom_call" | custom-call | tf_op jit(solution)/shard_map/enter_kv/pallas_call | solution.py:182
  4.2 7.0 %all-to-all-start = ((bf16[16,1,2,160,128]{4,3,2,1,0:T(8,128)(2,1)}), bf16[16,1,2,160,128]{4,3,2,1,0:T(8,128)(2,1)S(1)}, u32[]{:S(2)}, u32[]{:S(2)}) async-start(bf16[16,1,2,160,128]{4,3,2,1,0:T(8,128)(2,1)} %bitcast.18), calls=%async_computation | async-start | bytes 2621440 | tf_op jit(solution)/shard_map/all_to_all | solution.py:508
  11.2 4.3 %tables.1 = (s32[4,128]{1,0:T(4,128)}, s32[64]{0:T(128)}, s32[3]{0:T(128)}, s32[16]{0:T(128)}) custom-call(s32[5]{0:T(128)} %stack.23.refs_0_.place_ref, s32[10,16]{1,0:T(8,128)} %list_ref, s32[10,16]{1,0:T(8,128)} %count_ref.1), custom_call_target="tpu_custom_call" | custom-call | tf_op jit(solution)/shard_map/tables/pallas_call | solution.py:128
  21.2 3.6 %enter_q.1 = bf16[8,3,160,128]{3,2,1,0:T(8,128)(2,1)} custom-call(s32[5]{0:T(128)} %stack.23.refs_0_.place_ref, f32[1,128]{1,0:T(1,128)} %constant.24.clone.refs_1_, bf16[160,24,128]{2,1,0:T(8,128)(2,1)} %refs_2_.3), custom_call_target="tpu_custom_call" | custom-call | tf_op jit(solution)/shard_map/enter_q/pallas_call | solution.py:203
  24.8 4.4 %enter_kv.3 = bf16[2,8,2,2,160,128]{5,4,3,2,1,0:T(8,128)(2,1)} custom-call(s32[5]{0:T(128)} %stack.23.refs_0_.place_ref, f32[1,128]{1,0:T(1,128)} %constant.24.clone.refs_1_, bf16[160,24,128]{2,1,0:T(8,128)(2,1)} %refs_2_.2, bf16[160,24,128]{2,1,0:T(8,128)(2,1)} %refs_3_.2), custom_call_target="tpu_custom_call" | custom-call | tf_op jit(solution)/shard_map/enter_kv/pallas_call | solution.py:182
  29.2 2.9 %all-to-all-done = bf16[16,1,2,160,128]{4,3,2,1,0:T(8,128)(2,1)S(1)} async-done(((bf16[16,1,2,160,128]{4,3,2,1,0:T(8,128)(2,1)}), bf16[16,1,2,160,128]{4,3,2,1,0:T(8,128)(2,1)S(1)}, u32[]{:S(2)}, u32[]{:S(2)}) %all-to-all-start) | async-done | bytes 1310752 | tf_op jit(solution)/shard_map/all_to_all | solution.py:508
  33.2 4.4 %all-to-all-start.1 = ((bf16[16,2,2,160,128]{4,3,2,1,0:T(8,128)(2,1)}), bf16[16,2,2,160,128]{4,3,2,1,0:T(8,128)(2,1)S(1)}, u32[]{:S(2)}, u32[]{:S(2)}) async-start(bf16[16,2,2,160,128]{4,3,2,1,0:T(8,128)(2,1)} %bitcast.17), calls=%async_computation.1 | async-start | bytes 5242880 | tf_op jit(solution)/shard_map/all_to_all | solution.py:508
  37.6 3.2 %collective-permute-done.3.sib_ref = bf16[2,8,1,2,160,128]{5,4,3,2,1,0:T(8,128)(2,1)S(1)} collective-permute-done((bf16[2,8,1,2,160,128]{5,4,3,2,1,0:T(8,128)(2,1)}, bf16[2,8,1,2,160,128]{5,4,3,2,1,0:T(8,128)(2,1)S(1)}, u32[]{:S(2)}, u32[]{:S(2)}) %collective-permute-start.3) | collective-permute-done | bytes 1310752 | tf_op jit(solution)/shard_map/ppermute | solution.py:512
  42.0 3.0 %pack.2 = (bf16[11,1,2,128,128]{4,3,2,1,0:T(8,128)(2,1)}, bf16[3,1,2,128,128]{4,3,2,1,0:T(8,128)(2,1)}, bf16[9,1,2,128,128]{4,3,2,1,0:T(8,128)(2,1)}, bf16[8,1,2...) custom-call(s32[5]{0:T(128)} %stack.23.refs_0_.place_ref, s32[4,128]{1,0:T(4,128)} %copy-done.14, ...), custom_call_target="tpu_custom_call" | custom-call | tf_op jit(solution)/shard_map/pack/pallas_call | solution.py:243
  45.0 3.2 %collective-permute-start.7 = (bf16[11,1,2,128,128]{4,3,2,1,0:T(8,128)(2,1)}, bf16[11,1,2,128,128]{4,3,2,1,0:T(8,128)(2,1)S(1)}, u32[]{:S(2)}, u32[]{:S(2)}) collective-permute-start(bf16[11,1,2,128,128]{4,3,2,1,0:T(8,128)(2,1)} %get-tuple-element.68), channel_id=1, source_target_pairs={{0,32},{32,64},{64,96},{56,24},{88,56},{120,88},{1,33},{33,65},{65... | collective-permute-start | bytes 2162696 | tf_op jit(solution)/shard_map/ppermute | solution.py:519
  52.2 22.5 %collective-permute-done.5.in2 = bf16[8,1,2,128,128]{4,3,2,1,0:T(8,128)(2,1)S(1)} collective-permute-done((bf16[8,1,2,128,128]{4,3,2,1,0:T(8,128)(2,1)}, bf16[8,1,2,128,128]{4,3,2,1,0:T(8,128)(2,1)S(1)}, u32[]{:S(2)}, u32[]{:S(2)}) %collective-permute-start.5) | collective-permute-done | bytes 524320 | tf_op jit(solution)/shard_map/ppermute | solution.py:504
  78.6 4.9 %collective-permute-done.9.sib_ref = bf16[2,8,2,2,160,128]{5,4,3,2,1,0:T(8,128)(2,1)S(1)} collective-permute-done((bf16[2,8,2,2,160,128]{5,4,3,2,1,0:T(8,128)(2,1)S(1)}, bf16[2,8,2,2,160,128]{5,4,3,2,1,0:T(8,128)(2,1)S(1)}, u32[]{:S(2)}, u32[]{:S(2)}) %collective-permute-start.9) | collective-permute-done | bytes 2621472 | tf_op jit(solution)/shard_map/ppermute | solution.py:512
  85.0 5.5 %pack.3 = (bf16[11,2,2,128,128]{4,3,2,1,0:T(8,128)(2,1)}, bf16[3,2,2,128,128]{4,3,2,1,0:T(8,128)(2,1)}, bf16[9,2,2,128,128]{4,3,2,1,0:T(8,128)(2,1)}, bf16[8,2,2...) custom-call(s32[5]{0:T(128)} %stack.23.refs_0_.place_ref, s32[4,128]{1,0:T(4,128)} %copy-done.14, ...), custom_call_target="tpu_custom_call" | custom-call | tf_op jit(solution)/shard_map/pack/pallas_call | solution.py:243
  90.5 9.2 %collective-permute-start.10 = (bf16[11,2,2,128,128]{4,3,2,1,0:T(8,128)(2,1)}, bf16[11,2,2,128,128]{4,3,2,1,0:T(8,128)(2,1)S(1)}, u32[]{:S(2)}, u32[]{:S(2)}) collective-permute-start(bf16[11,2,2,128,128]{4,3,2,1,0:T(8,128)(2,1)} %get-tuple-element.72), channel_id=1, source_target_pairs={{0,32},{32,64},{64,96},{56,24},{88,56},{120,88},{1,33},{33,65},{65... | collective-permute-start | bytes 4325384 | tf_op jit(solution)/shard_map/ppermute | solution.py:519
  101.8 5.5 %all-to-all-start.2 = ((bf16[8,3,160,128]{3,2,1,0:T(8,128)(2,1)}), bf16[8,3,160,128]{3,2,1,0:T(8,128)(2,1)S(1)}, u32[]{:S(2)}, u32[]{:S(2)}) async-start(bf16[8,3,160,128]{3,2,1,0:T(8,128)(2,1)} %enter_q.1), calls=%async_computation.2 | async-start | bytes 1966080 | tf_op jit(solution)/shard_map/all_to_all | solution.py:515
  109.7 11.0 %all-to-all-done.2.q_ref = bf16[8,3,160,128]{3,2,1,0:T(8,128)(2,1)S(1)} async-done(((bf16[8,3,160,128]{3,2,1,0:T(8,128)(2,1)}), bf16[8,3,160,128]{3,2,1,0:T(8,128)(2,1)S(1)}, u32[]{:S(2)}, u32[]{:S(2)}) %all-to-all-start.2) | async-done | bytes 983072 | tf_op jit(solution)/shard_map/all_to_all | solution.py:515
  121.6 12.4 %near.2 = (f32[1,1280,128]{2,1,0:T(8,128)}, f32[1,1280,128]{2,1,0:T(8,128)}, f32[1,1280,128]{2,1,0:T(8,128)}) custom-call(s32[5]{0:T(128)} %stack.23.refs_0_.place_ref, s32[16]{0:T(128)} %get-tuple-element.79.plane_ref, bf16[8,3,160,128]{3,2,1,0:T(8,128)(2,1)} %copy-done, bf16[2,8,1,2,160,128]{5,4,3,2,1,0:T(8,128)(2,1)} %bitcast.16, ...), custom_call_target="tpu_custom_call" | custom-call | tf_op jit(solution)/shard_map/near/pallas_call | solution.py:355
  134.1 6.7 %cross.2 = (f32[1,1280,128]{2,1,0:T(8,128)}, f32[1,1280,128]{2,1,0:T(8,128)}, f32[1,1280,128]{2,1,0:T(8,128)}) custom-call(s32[5]{0:T(128)} %stack.23.refs_0_.place_ref, bf16[8,3,160,128]{3,2,1,0:T(8,128)(2,1)} %copy-done, bf16[11,1,2,128,128]{4,3,2,1,0:T(8,128)(2,1)} %copy-done.6, f32[1,1280,128]{2,1,0:T(8,128)} %get-tuple-element.80.acc_in, ...), custom_call_target="tpu_custom_call" | custom-call | tf_op jit(solution)/shard_map/cross/pallas_call | solution.py:405
  140.8 4.9 %far.2 = bf16[8,1,160,128]{3,2,1,0:T(8,128)(2,1)} custom-call(s32[5]{0:T(128)} %stack.23.refs_0_.place_ref, s32[64]{0:T(128)} %get-tuple-element.52.qslot_ref, s32[3]{0:T(128)} %get-tuple-element.53.late_ref, bf16[8,3,160,128]{3,2,1,0:T(8,128)(2,1)} %copy-done, f32[1,1280,128]{2,1,0:T(8,128)} %get-tuple-element.83.acc_in, ...), custom_call_target="tpu_custom_call" | custom-call | tf_op jit(solution)/shard_map/far/pallas_call | solution.py:446
  145.7 3.7 %all-to-all-start.3 = ((bf16[8,1,160,128]{3,2,1,0:T(8,128)(2,1)}), bf16[8,1,160,128]{3,2,1,0:T(8,128)(2,1)S(1)}, u32[]{:S(2)}, u32[]{:S(2)}) async-start(bf16[8,1,160,128]{3,2,1,0:T(8,128)(2,1)} %far.2), calls=%async_computation.3 | async-start | bytes 655360 | tf_op jit(solution)/shard_map/all_to_all | solution.py:515
  149.4 22.0 %near.3 = (f32[2,1280,128]{2,1,0:T(8,128)}, f32[2,1280,128]{2,1,0:T(8,128)}, f32[2,1280,128]{2,1,0:T(8,128)}) custom-call(s32[5]{0:T(128)} %stack.23.refs_0_.place_ref, s32[16]{0:T(128)} %get-tuple-element.79.plane_ref, bf16[8,3,160,128]{3,2,1,0:T(8,128)(2,1)} %copy-done, bf16[2,8,2,2,160,128]{5,4,3,2,1,0:T(8,128)(2,1)} %bitcast.13, ...), custom_call_target="tpu_custom_call" | custom-call | tf_op jit(solution)/shard_map/near/pallas_call | solution.py:355
  172.6 10.4 %cross.3 = (f32[2,1280,128]{2,1,0:T(8,128)}, f32[2,1280,128]{2,1,0:T(8,128)}, f32[2,1280,128]{2,1,0:T(8,128)}) custom-call(s32[5]{0:T(128)} %stack.23.refs_0_.place_ref, bf16[8,3,160,128]{3,2,1,0:T(8,128)(2,1)} %copy-done, bf16[11,2,2,128,128]{4,3,2,1,0:T(8,128)(2,1)} %copy-done.4, f32[2,1280,128]{2,1,0:T(8,128)} %get-tuple-element.91.acc_in, ...), custom_call_target="tpu_custom_call" | custom-call | tf_op jit(solution)/shard_map/cross/pallas_call | solution.py:405
  183.0 7.0 %far.3 = bf16[8,2,160,128]{3,2,1,0:T(8,128)(2,1)} custom-call(s32[5]{0:T(128)} %stack.23.refs_0_.place_ref, s32[64]{0:T(128)} %get-tuple-element.52.qslot_ref, s32[3]{0:T(128)} %get-tuple-element.53.late_ref, bf16[8,3,160,128]{3,2,1,0:T(8,128)(2,1)} %copy-done, f32[2,1280,128]{2,1,0:T(8,128)} %get-tuple-element.94.acc_in, ...), custom_call_target="tpu_custom_call" | custom-call | tf_op jit(solution)/shard_map/far/pallas_call | solution.py:446
  190.0 14.9 %all_to_all.25.refs_1_ = bf16[8,2,160,128]{3,2,1,0:T(8,128)(2,1)} all-to-all(bf16[8,2,160,128]{3,2,1,0:T(8,128)(2,1)} %far.3), channel_id=1, replica_groups=mesh['z'=4,'yh'=2,'c'=2,'head'=8] {'head'}, dimensions={0} | all-to-all | bytes 1310720 | tf_op jit(solution)/shard_map/all_to_all | solution.py:515
  (59 shorter events, 27.2 us)
Async XLA Ops:
  4.2 27.9 %all-to-all-start = ((bf16[16,1,2,160,128]{4,3,2,1,0:T(8,128)(2,1)}), bf16[16,1,2,160,128]{4,3,2,1,0:T(8,128)(2,1)S(1)}, u32[]{:S(2)}, u32[]{:S(2)}) async-start(bf16[16,1,2,160,128]{4,3,2,1,0:T(8,128)(2,1)} %bitcast.18), calls=%async_computation | async-start | bytes 2621440 | tf_op jit(solution)/shard_map/all_to_all | solution.py:508
  15.5 13.6 %collective-permute-start.2 = (s32[4,128]{1,0:T(4,128)}, s32[4,128]{1,0:T(4,128)S(1)}, u32[]{:S(2)}, u32[]{:S(2)}) collective-permute-start(s32[4,128]{1,0:T(4,128)} %get-tuple-element.58), channel_id=1, source_target_pairs={{0,32},{32,64},{64,96},{96,0},{1,33},{33,65},{65,97},{97,1},{2,34}... | collective-permute-start | bytes 6152 | tf_op jit(solution)/shard_map/ppermute | solution.py:504
  17.5 11.6 %collective-permute-start.1 = (s32[4,128]{1,0:T(4,128)}, s32[4,128]{1,0:T(4,128)S(1)}, u32[]{:S(2)}, u32[]{:S(2)}) collective-permute-start(s32[4,128]{1,0:T(4,128)} %get-tuple-element.58), channel_id=1, source_target_pairs={{0,64},{32,96},{64,0},{96,32},{1,65},{33,97},{65,1},{97,33},{2,66}... | collective-permute-start | bytes 6152 | tf_op jit(solution)/shard_map/ppermute | solution.py:504
  18.7 10.5 %collective-permute-start = (s32[4,128]{1,0:T(4,128)}, s32[4,128]{1,0:T(4,128)S(1)}, u32[]{:S(2)}, u32[]{:S(2)}) collective-permute-start(s32[4,128]{1,0:T(4,128)} %get-tuple-element.58), channel_id=1, source_target_pairs={{0,96},{32,0},{64,32},{96,64},{1,97},{33,1},{65,33},{97,65},{2,98}... | collective-permute-start | bytes 6152 | tf_op jit(solution)/shard_map/ppermute | solution.py:504
  29.2 11.7 %copy-start.13 = (s32[4,128]{1,0:T(4,128)}, s32[4,128]{1,0:T(4,128)S(1)}, u32[]{:S(2)}) copy-start(s32[4,128]{1,0:T(4,128)S(1)} %collective-permute-done.1.ask2) | copy-start | bytes 6148
  29.2 11.7 %copy-start.14 = (s32[4,128]{1,0:T(4,128)}, s32[4,128]{1,0:T(4,128)S(1)}, u32[]{:S(2)}) copy-start(s32[4,128]{1,0:T(4,128)S(1)} %collective-permute-done.ask1) | copy-start | bytes 6148
  33.2 45.3 %all-to-all-start.1 = ((bf16[16,2,2,160,128]{4,3,2,1,0:T(8,128)(2,1)}), bf16[16,2,2,160,128]{4,3,2,1,0:T(8,128)(2,1)S(1)}, u32[]{:S(2)}, u32[]{:S(2)}) async-start(bf16[16,2,2,160,128]{4,3,2,1,0:T(8,128)(2,1)} %bitcast.17), calls=%async_computation.1 | async-start | bytes 5242880 | tf_op jit(solution)/shard_map/all_to_all | solution.py:508
  37.6 3.3 %collective-permute-start.3 = (bf16[2,8,1,2,160,128]{5,4,3,2,1,0:T(8,128)(2,1)}, bf16[2,8,1,2,160,128]{5,4,3,2,1,0:T(8,128)(2,1)S(1)}, u32[]{:S(2)}, u32[]{:S(2)}) collective-permute-start(bf16[2,8,1,2,160,128]{5,4,3,2,1,0:T(8,128)(2,1)} %bitcast.14), channel_id=1, source_target_pairs={{0,8},{8,0},{1,9},{9,1},{2,10},{10,2},{3,11},{11,3},{4,12},{12,4},... | collective-permute-start | bytes 3932168 | tf_op jit(solution)/shard_map/ppermute | solution.py:512
  45.0 33.4 %collective-permute-start.7 = (bf16[11,1,2,128,128]{4,3,2,1,0:T(8,128)(2,1)}, bf16[11,1,2,128,128]{4,3,2,1,0:T(8,128)(2,1)S(1)}, u32[]{:S(2)}, u32[]{:S(2)}) collective-permute-start(bf16[11,1,2,128,128]{4,3,2,1,0:T(8,128)(2,1)} %get-tuple-element.68), channel_id=1, source_target_pairs={{0,32},{32,64},{64,96},{56,24},{88,56},{120,88},{1,33},{33,65},{65... | collective-permute-start | bytes 2162696 | tf_op jit(solution)/shard_map/ppermute | solution.py:519
  48.2 28.6 %collective-permute-start.4 = (bf16[9,1,2,128,128]{4,3,2,1,0:T(8,128)(2,1)}, bf16[9,1,2,128,128]{4,3,2,1,0:T(8,128)(2,1)S(1)}, u32[]{:S(2)}, u32[]{:S(2)}) collective-permute-start(bf16[9,1,2,128,128]{4,3,2,1,0:T(8,128)(2,1)} %get-tuple-element.65), channel_id=1, source_target_pairs={{0,32},{32,64},{64,96},{96,0},{1,33},{33,65},{65,97},{97,1},{2,34}... | collective-permute-start | bytes 1769480 | tf_op jit(solution)/shard_map/ppermute | solution.py:504
  49.9 26.9 %collective-permute-start.6 = (bf16[9,1,2,128,128]{4,3,2,1,0:T(8,128)(2,1)}, bf16[9,1,2,128,128]{4,3,2,1,0:T(8,128)(2,1)S(1)}, u32[]{:S(2)}, u32[]{:S(2)}) collective-permute-start(bf16[9,1,2,128,128]{4,3,2,1,0:T(8,128)(2,1)} %get-tuple-element.67), channel_id=1, source_target_pairs={{0,96},{32,0},{64,32},{96,64},{1,97},{33,1},{65,33},{97,65},{2,98}... | collective-permute-start | bytes 1769480 | tf_op jit(solution)/shard_map/ppermute | solution.py:504
  50.3 24.4 %collective-permute-start.5 = (bf16[8,1,2,128,128]{4,3,2,1,0:T(8,128)(2,1)}, bf16[8,1,2,128,128]{4,3,2,1,0:T(8,128)(2,1)S(1)}, u32[]{:S(2)}, u32[]{:S(2)}) collective-permute-start(bf16[8,1,2,128,128]{4,3,2,1,0:T(8,128)(2,1)} %get-tuple-element.66), channel_id=1, source_target_pairs={{0,64},{32,96},{64,0},{96,32},{1,65},{33,97},{65,1},{97,33},{2,66}... | collective-permute-start | bytes 1572872 | tf_op jit(solution)/shard_map/ppermute | solution.py:504
  51.5 0.7 collective-permute-start.8
  52.2 81.9 %copy-start.11 = (bf16[3,1,2,128,128]{4,3,2,1,0:T(8,128)(2,1)}, bf16[3,1,2,128,128]{4,3,2,1,0:T(8,128)(2,1)S(1)}, u32[]{:S(2)}) copy-start(bf16[3,1,2,128,128]{4,3,2,1,0:T(8,128)(2,1)S(1)} %collective-permute-done.8.mid_ref) | copy-start | bytes 589828
  78.5 55.6 %copy-start.6 = (bf16[11,1,2,128,128]{4,3,2,1,0:T(8,128)(2,1)}, bf16[11,1,2,128,128]{4,3,2,1,0:T(8,128)(2,1)S(1)}, u32[]{:S(2)}) copy-start(bf16[11,1,2,128,128]{4,3,2,1,0:T(8,128)(2,1)S(1)} %collective-permute-done.7.big_ref) | copy-start | bytes 2162692
  78.5 5.0 %collective-permute-start.9 = (bf16[2,8,2,2,160,128]{5,4,3,2,1,0:T(8,128)(2,1)S(1)}, bf16[2,8,2,2,160,128]{5,4,3,2,1,0:T(8,128)(2,1)S(1)}, u32[]{:S(2)}, u32[]{:S(2)}) collective-permute-start(bf16[2,8,2,2,160,128]{5,4,3,2,1,0:T(8,128)(2,1)S(1)} %bitcast.11), channel_id=1, source_target_pairs={{0,8},{8,0},{1,9},{9,1},{2,10},{10,2},{3,11},{11,3},{4,12},{12,4},... | collective-permute-start | bytes 7864328 | tf_op jit(solution)/shard_map/ppermute | solution.py:512
  90.5 80.9 %collective-permute-start.10 = (bf16[11,2,2,128,128]{4,3,2,1,0:T(8,128)(2,1)}, bf16[11,2,2,128,128]{4,3,2,1,0:T(8,128)(2,1)S(1)}, u32[]{:S(2)}, u32[]{:S(2)}) collective-permute-start(bf16[11,2,2,128,128]{4,3,2,1,0:T(8,128)(2,1)} %get-tuple-element.72), channel_id=1, source_target_pairs={{0,32},{32,64},{64,96},{56,24},{88,56},{120,88},{1,33},{33,65},{65... | collective-permute-start | bytes 4325384 | tf_op jit(solution)/shard_map/ppermute | solution.py:519
  99.7 83.3 %collective-permute-start.11 = (bf16[9,2,2,128,128]{4,3,2,1,0:T(8,128)(2,1)}, bf16[9,2,2,128,128]{4,3,2,1,0:T(8,128)(2,1)}, u32[]{:S(2)}, u32[]{:S(2)}) collective-permute-start(bf16[9,2,2,128,128]{4,3,2,1,0:T(8,128)(2,1)} %get-tuple-element.74), channel_id=1, source_target_pairs={{0,32},{32,64},{64,96},{96,0},{1,33},{33,65},{65,97},{97,1},{2,34}... | collective-permute-start | bytes 3538952 | tf_op jit(solution)/shard_map/ppermute | solution.py:504
  99.8 83.2 %collective-permute-start.13 = (bf16[9,2,2,128,128]{4,3,2,1,0:T(8,128)(2,1)}, bf16[9,2,2,128,128]{4,3,2,1,0:T(8,128)(2,1)}, u32[]{:S(2)}, u32[]{:S(2)}) collective-permute-start(bf16[9,2,2,128,128]{4,3,2,1,0:T(8,128)(2,1)} %get-tuple-element.76), channel_id=1, source_target_pairs={{0,96},{32,0},{64,32},{96,64},{1,97},{33,1},{65,33},{97,65},{2,98}... | collective-permute-start | bytes 3538952 | tf_op jit(solution)/shard_map/ppermute | solution.py:504
  101.8 18.9 %all-to-all-start.2 = ((bf16[8,3,160,128]{3,2,1,0:T(8,128)(2,1)}), bf16[8,3,160,128]{3,2,1,0:T(8,128)(2,1)S(1)}, u32[]{:S(2)}, u32[]{:S(2)}) async-start(bf16[8,3,160,128]{3,2,1,0:T(8,128)(2,1)} %enter_q.1), calls=%async_computation.2 | async-start | bytes 1966080 | tf_op jit(solution)/shard_map/all_to_all | solution.py:515
  107.3 75.7 %collective-permute-start.12 = (bf16[8,2,2,128,128]{4,3,2,1,0:T(8,128)(2,1)}, bf16[8,2,2,128,128]{4,3,2,1,0:T(8,128)(2,1)}, u32[]{:S(2)}, u32[]{:S(2)}) collective-permute-start(bf16[8,2,2,128,128]{4,3,2,1,0:T(8,128)(2,1)} %get-tuple-element.75), channel_id=1, source_target_pairs={{0,64},{32,96},{64,0},{96,32},{1,65},{33,97},{65,1},{97,33},{2,66}... | collective-permute-start | bytes 3145736 | tf_op jit(solution)/shard_map/ppermute | solution.py:504
  108.2 74.7 %collective-permute-start.14 = (bf16[3,2,2,128,128]{4,3,2,1,0:T(8,128)(2,1)}, bf16[3,2,2,128,128]{4,3,2,1,0:T(8,128)(2,1)}, u32[]{:S(2)}, u32[]{:S(2)}) collective-permute-start(bf16[3,2,2,128,128]{4,3,2,1,0:T(8,128)(2,1)} %get-tuple-element.73), channel_id=1, source_target_pairs={{8,40},{40,72},{72,104},{48,16},{80,48},{112,80},{9,41},{41,73},{7... | collective-permute-start | bytes 1179656 | tf_op jit(solution)/shard_map/ppermute | solution.py:521
  145.7 44.2 %all-to-all-start.3 = ((bf16[8,1,160,128]{3,2,1,0:T(8,128)(2,1)}), bf16[8,1,160,128]{3,2,1,0:T(8,128)(2,1)S(1)}, u32[]{:S(2)}, u32[]{:S(2)}) async-start(bf16[8,1,160,128]{3,2,1,0:T(8,128)(2,1)} %far.2), calls=%async_computation.3 | async-start | bytes 655360 | tf_op jit(solution)/shard_map/all_to_all | solution.py:515
  190.0 14.9 %copy-start.7 = (bf16[8,1,160,128]{3,2,1,0:T(8,128)(2,1)}, bf16[8,1,160,128]{3,2,1,0:T(8,128)(2,1)S(1)}, u32[]{:S(2)}) copy-start(bf16[8,1,160,128]{3,2,1,0:T(8,128)(2,1)S(1)} %all-to-all-done.3.refs_0_) | copy-start | bytes 983044
  (10 other events, 18.7 us)

commit v3 on v2

--- a/solution.py
+++ b/solution.py
@@ -22,9 +22,8 @@
 CHUNKS = ((0,), (1, 2))
 
 BASE = 8
-BESIDE = 9
-BIG = 11
-MID = 3
+BESIDE = 12
+BIG = 8
 VMEM = 58 * 2**20
 
 i32 = jnp.int32
@@ -38,7 +37,7 @@
     return pl.BlockSpec(memory_space=pltpu.SMEM)
 
 
-def table_body(place_ref, list_ref, count_ref, want_ref, qslot_ref, late_ref, plane_ref, kb_ref, qb_ref):
+def table_body(place_ref, list_ref, count_ref, want_ref, qslot_ref, plane_ref, kb_ref, qb_ref):
     z, r = place_ref[0], place_ref[1]
     f = PLANE * z + r
 
@@ -65,8 +64,6 @@
     lax.fori_loop(0, 128, clear, jnp.int32(0))
     for s in range(64):
         qslot_ref[s] = -1
-    for s in range(MID):
-        late_ref[s] = -1
     for zp in range(4):
         for i in range(PLANE):
             g = PLANE * zp + i
@@ -90,19 +87,17 @@
             for j in range(2):
                 listed(zp, 2 * near + j, two, 2 + j)
             listed(zp, BASE, two, 4)
-            for n in range(NB):
+            listed(zp, BESIDE - 1, three, 2)
+            for n in range(BIG):
                 want_ref[zp, BESIDE + n] = NB * near + n
-            at = (PLANE * zp + three) * 8 + 2
-            want_ref[zp, BESIDE + NB] = NB * three + kb_ref[at]
-            late_ref[0] = qb_ref[at]
+            for n in range(BIG, NB):
+                want_ref[zp, BASE + 1 + n - BIG] = NB * near + n
 
         @pl.when(exists & (r == second))
         def _():
             listed(zp, BASE, two, 2)
-            for j in range(MID):
-                at = (PLANE * zp + near) * 8 + 2 + j
-                want_ref[zp, BESIDE + BIG + j] = NB * near + kb_ref[at]
-                late_ref[j] = qb_ref[at]
+            for j in range(3):
+                listed(zp, BASE + 1 + j, near, 2 + j)
 
         @pl.when(exists & (r == third))
         def _():
@@ -128,11 +123,10 @@
     return pl.pallas_call(
         table_body,
         in_specs=[smem(), smem(), smem()],
-        out_specs=[smem(), smem(), smem(), smem()],
+        out_specs=[smem(), smem(), smem()],
         out_shape=[
             jax.ShapeDtypeStruct((4, 128), i32),
             jax.ShapeDtypeStruct((64,), i32),
-            jax.ShapeDtypeStruct((MID,), i32),
             jax.ShapeDtypeStruct((16,), i32),
         ],
         scratch_shapes=[pltpu.SMEM((128,), i32), pltpu.SMEM((128,), i32)],
@@ -211,7 +205,7 @@
     )(place, rates, query)
 
 
-def pack_body(place_ref, ask1, ask2, ask3, own_ref, sib_ref, big_ref, mid_ref, out1, out2, out3, frames):
+def pack_body(place_ref, ask1, ask2, ask3, own_ref, sib_ref, big_ref, out1, out2, out3, frames):
     z, r, c = place_ref[0], place_ref[1], place_ref[4]
     for b in range(2):
         for ref, core in ((own_ref, c), (sib_ref, 1 - c)):
@@ -221,12 +215,8 @@
     def block(index):
         return frames[pl.ds(pl.multiple_of(index * BLK, BLK), BLK), :]
 
-    for s in range(BIG + MID):
-        index = jnp.where(r < 2, ask1[z, BESIDE + s], ask3[z, BESIDE + s])
-        if s < BIG:
-            big_ref[s, 0, 0] = block(index)
-        else:
-            mid_ref[s - BIG, 0, 0] = block(index)
+    for s in range(BIG):
+        big_ref[s, 0, 0] = block(jnp.where(r < 2, ask1[z, BESIDE + s], ask3[z, BESIDE + s]))
     for ask, ref in ((ask1, out1), (ask2, out2), (ask3, out3)):
         for s in range(ref.shape[0]):
             ref[s, 0, 0] = block(ask[z, s])
@@ -239,7 +229,7 @@
     def out(n):
         return pl.BlockSpec((n, 1, 1, BLK, DH), lambda h, kv: (0, h, kv, 0, 0))
 
-    sizes = (BIG, MID, BESIDE, BASE, BESIDE)
+    sizes = (BIG, BESIDE, BASE, BESIDE)
     return pl.pallas_call(
         pack_body,
         grid=(nh, 2),
@@ -338,8 +328,8 @@
     listed_pairs([pair(p) for p in range(8)], qs, m, l, acc, top, scores)
 
 
-def head_specs(first):
-    tokens = pl.BlockSpec((8, 1, CH, DH), lambda h: (0, h + first if first else h, 0, 0))
+def head_specs(at=0):
+    tokens = pl.BlockSpec((8, 1, CH, DH), lambda h: (0, h + at if at else h, 0, 0))
     state = pl.BlockSpec((1, TOK, DH), lambda h: (h, 0, 0))
     return tokens, state
 
@@ -348,10 +338,10 @@
     return [jax.ShapeDtypeStruct((nh, TOK, DH), jnp.float32)] * 3
 
 
-def near(place, plane_pairs, q, own, sib, first):
+def near(place, plane_pairs, q, own, sib, at):
     nh = own.shape[2]
     frames = pl.BlockSpec((2, 8, 1, 2, CH, DH), lambda h: (0, 0, h, 0, 0, 0))
-    tokens, state = head_specs(first)
+    tokens, state = head_specs(at)
     return pl.pallas_call(
         near_body,
         grid=(nh,),
@@ -370,25 +360,28 @@
     )(place, plane_pairs, q, own, sib)
 
 
-def cross_body(place_ref, q_ref, big_ref, acc_in, m_in, l_in, acc_ref, m_ref, l_ref):
+def cross_body(place_ref, q_ref, big_ref, in1, in3, acc_in, m_in, l_in, acc_ref, m_ref, l_ref, kf, vf):
     z, r = place_ref[0], place_ref[1]
     touches = ((r == 0) & (z > 0)) | ((r == PLANE - 1) & (z < 3))
 
     @pl.when(touches)
     def _():
-        k = big_ref[:NB, 0, 0].reshape(TOK, DH)
-        v = big_ref[:NB, 0, 1].reshape(TOK, DH)
+        for kv, ref in ((0, kf), (1, vf)):
+            ref[: BIG * BLK] = big_ref[:, 0, kv].reshape(BIG * BLK, DH)
+            for n in range(BIG, NB):
+                s = BASE + 1 + n - BIG
+                ref[n * BLK : (n + 1) * BLK] = jnp.where(r == 0, in1[s, 0, kv], in3[s, 0, kv])
         q = q_ref[:, 0].reshape(TOK, DH)
         for t in range(TOK // QT):
             rows = slice(t * QT, (t + 1) * QT)
-            s = dot_t(q[rows], k) * SCALE
+            s = dot_t(q[rows], kf[...]) * SCALE
             m_old = m_in[0, rows]
             m_new = jnp.maximum(m_old, jnp.max(by_lane(jnp.maximum, s), axis=1, keepdims=True))
             p = jnp.exp2(s - m_new[:, :1])
             fade = jnp.exp2(m_old - m_new)
             m_ref[0, rows] = m_new
             l_ref[0, rows] = l_in[0, rows] * fade + by_lane(jnp.add, p)
-            mixed = jnp.dot(p.astype(jnp.bfloat16), v, preferred_element_type=jnp.float32)
+            mixed = jnp.dot(p.astype(jnp.bfloat16), vf[...], preferred_element_type=jnp.float32)
             acc_ref[0, rows] = acc_in[0, rows] * fade + mixed
 
     @pl.when(jnp.logical_not(touches))
@@ -398,25 +391,27 @@
         l_ref[...] = l_in[...]
 
 
-def cross(place, q, big, state, first):
+def block_specs(arrays):
+    return [pl.BlockSpec((x.shape[0], 1, 2, BLK, DH), lambda h: (0, h, 0, 0, 0)) for x in arrays]
+
+
+def cross(place, q, big, in1, in3, state, at):
     nh = big.shape[1]
-    tokens, held = head_specs(first)
-    blocks = pl.BlockSpec((BIG, 1, 2, BLK, DH), lambda h: (0, h, 0, 0, 0))
+    tokens, held = head_specs(at)
     return pl.pallas_call(
         cross_body,
         grid=(nh,),
-        in_specs=[smem(), tokens, blocks, held, held, held],
+        in_specs=[smem(), tokens] + block_specs((big, in1, in3)) + [held] * 3,
         out_specs=[held] * 3,
         out_shape=state_shapes(nh),
+        scratch_shapes=[pltpu.VMEM((TOK, DH), jnp.bfloat16)] * 2,
         compiler_params=params(),
         name="cross",
-    )(place, q, big, *state)
-
-
-def far_body(
-    place_ref, qslot_ref, late_ref, q_ref, acc_in, m_in, l_in, in1, in2, in3, big_ref, mid_ref, o_ref, qs, acc, m, l, top, scores
-):
-    z, r = place_ref[0], place_ref[1]
+    )(place, q, big, in1, in3, *state)
+
+
+def far_body(place_ref, qslot_ref, q_ref, acc_in, m_in, l_in, in1, in2, in3, o_ref, qs, acc, m, l, top, scores):
+    z = place_ref[0]
     qs[...] = q_ref[:, 0].reshape(TOK, DH)
     acc[...] = acc_in[0]
     m[...] = m_in[0]
@@ -427,34 +422,26 @@
         for s in range(ref.shape[0]):
             block = qslot_ref[zp * BESIDE + s]
             pairs.append((block, lambda ref=ref, s=s: ref[s, 0, 0], lambda ref=ref, s=s: ref[s, 0, 1]))
-    outer = (r == 0) | (r == PLANE - 1)
-    for s in range(MID):
-
-        def either(kv, s=s):
-            return jnp.where(outer, big_ref[NB, 0, kv], mid_ref[s, 0, kv])
-
-        pairs.append((late_ref[s], lambda either=either: either(0), lambda either=either: either(1)))
     listed_pairs(pairs, qs, m, l, acc, top, scores)
     total = jnp.sum(l[...], axis=1, keepdims=True)
     o_ref[:, 0] = (acc[...] / total).astype(jnp.bfloat16).reshape(8, CH, DH)
 
 
-def far(place, qslot, late, q, state, crossed, first):
-    nh = crossed[0].shape[1]
-    tokens, held = head_specs(first)
-    blocks = [pl.BlockSpec((x.shape[0], 1, 2, BLK, DH), lambda h: (0, h, 0, 0, 0)) for x in crossed]
+def far(place, qslot, q, state, base, at):
+    nh = base[0].shape[1]
+    tokens, held = head_specs(at)
     return pl.pallas_call(
         far_body,
         grid=(nh,),
-        in_specs=[smem(), smem(), smem(), tokens, held, held, held] + blocks,
+        in_specs=[smem(), smem(), tokens, held, held, held] + block_specs(base),
         out_specs=pl.BlockSpec((8, 1, CH, DH), lambda h: (0, h, 0, 0)),
         out_shape=jax.ShapeDtypeStruct((8, nh, CH, DH), jnp.bfloat16),
         scratch_shapes=[pltpu.VMEM((TOK, DH), jnp.bfloat16)]
         + [pltpu.VMEM((TOK, DH), jnp.float32)] * 4
-        + [pltpu.VMEM((2 * BESIDE + BASE + MID, BLK, BLK), jnp.float32)],
+        + [pltpu.VMEM((2 * BESIDE + BASE, BLK, BLK), jnp.float32)],
         compiler_params=params(),
         name="far",
-    )(place, qslot, late, q, *state, *crossed)
+    )(place, qslot, q, *state, *base)
 
 
 def leave_body(groups, *refs):
@@ -485,8 +472,6 @@
 TM = ("z", "yh", "c")
 BIG_PAIRS = [(at_plane(z, 0), at_plane(z + 1, 0)) for z in range(3)] + [(at_plane(z + 1, 3), at_plane(z, 3)) for z in range(3)]
 
-MID_PAIRS = [(at_plane(z, 1), at_plane(z + 1, 1)) for z in range(3)] + [(at_plane(z + 1, 2), at_plane(z, 2)) for z in range(3)]
-
 
 def together(*values):
     return lax.optimization_barrier(values)
@@ -497,9 +482,6 @@
     r = 2 * yh + c
     place = jnp.stack([z, r, PLANE * z + r, hd, c]).astype(i32)
     rates = jnp.asarray(lane_rates())
-    first, rest = CHUNKS
-    a_at, b_at = first[0], rest[0]
-
     def around(x, shift):
         return lax.ppermute(x, "z", [(i, (i + shift) % 4) for i in range(4)])
 
@@ -515,37 +497,38 @@
         return lax.all_to_all(x, "head", 0, 0, tiled=True)
 
     def send(packed):
-        big, mid, *base = packed
+        big, *base = packed
         big = lax.ppermute(big, TM, BIG_PAIRS)
-        base = [around(x, shift) for shift, x in zip((1, 2, 3), base, strict=True)]
-        return [*base, big, lax.ppermute(mid, TM, MID_PAIRS)]
-
-    sent_a = enter_kv(place, rates, key, value, first)
-    far_list, key, value, query, sent_a = together(far_list, key, value, query, sent_a)
-    want, qslot, late, plane_pairs = tables(place, far_list, far_count)
+        return big, *(around(x, shift) for shift, x in zip((1, 2, 3), base, strict=True))
+
+    sent_a = enter_kv(place, rates, key, value, CHUNKS[0])
+    far_list, key, value, sent_a = together(far_list, key, value, sent_a)
+    want, qslot, plane_pairs = tables(place, far_list, far_count)
     asked = [around(want, -shift) for shift in (1, 2, 3)]
-    sent_b = enter_kv(place, rates, key, value, rest)
-    sent_q = enter_q(place, rates, query, first + rest)
+    sent_b = enter_kv(place, rates, key, value, CHUNKS[1])
     own_a = entry(sent_a)
-    own_a, sent_b, sent_q, asked = together(own_a, sent_b, sent_q, asked)
+    own_a, sent_b, asked = together(own_a, sent_b, asked)
+    own_b = entry(sent_b)
     sib_a = swap(own_a)
-    own_b = entry(sent_b)
     packed_a = pack(place, asked, own_a, sib_a)
-    crossed_a = send(packed_a)
-    own_b, sent_q, crossed_a = together(own_b, sent_q, crossed_a)
+    packed_a, query = together(packed_a, query)
+    big_a, in1_a, in2_a, in3_a = send(packed_a)
+    q_a, q_b = (enter_q(place, rates, query, rows) for rows in CHUNKS)
+    own_b, q_a, q_b, big_a, in1_a, in3_a = together(own_b, q_a, q_b, big_a, in1_a, in3_a)
     sib_b = swap(own_b)
-    q = by_head(sent_q)
+    q_a = by_head(q_a)
     packed_b = pack(place, asked, own_b, sib_b)
-    crossed_b = send(packed_b)
-    q, _ = together(q, packed_b)
-    state_a = near(place, plane_pairs, q, own_a, sib_a, a_at)
-    state_a = cross(place, q, crossed_a[3], state_a, a_at)
-    done_a = far(place, qslot, late, q, state_a, crossed_a, a_at)
+    packed_b, q_a, in2_a = together(packed_b, q_a, in2_a)
+    big_b, in1_b, in2_b, in3_b = send(packed_b)
+    q_b = by_head(q_b)
+    state_a = near(place, plane_pairs, q_a, own_a, sib_a, 0)
+    state_a = cross(place, q_a, big_a, in1_a, in3_a, state_a, 0)
+    done_a = far(place, qslot, q_a, state_a, (in1_a, in2_a, in3_a), 0)
     out_a = by_head(done_a)
-    q, _ = together(q, done_a)
-    state_b = near(place, plane_pairs, q, own_b, sib_b, b_at)
-    state_b = cross(place, q, crossed_b[3], state_b, b_at)
-    out_b = by_head(far(place, qslot, late, q, state_b, crossed_b, b_at))
+    q_b, _ = together(q_b, done_a)
+    state_b = near(place, plane_pairs, q_b, own_b, sib_b, 0)
+    state_b = cross(place, q_b, big_b, in1_b, in3_b, state_b, 0)
+    out_b = by_head(far(place, qslot, q_b, state_b, (in1_b, in2_b, in3_b), 0))
     return leave((out_a, out_b), CHUNKS)
 
 

time: 209 us -> 198 us (0.947)
  waiting for transfers between devices: 46.7 us -> 39.9 us
  local copies, waits for them, and re-layouts: 8.16 us -> 4.95 us
  Pallas kernels: 90.5 us -> 93.7 us
  starting transfers between devices: 47.1 us -> 44.3 us
    ppermute x2, waiting for transfers between devices: 0.01 us -> 21.1 us  [send(): big = lax.ppermute(big, TM, BIG_PAIRS)]
    ppermute x9, waiting for transfers between devices: 24.7 us -> 4.24 us  [around(): return lax.ppermute(x, 'z', [(i, (i + shift) % 4) for i in range(4)])]
    all_to_all x2 -> x3, waiting for transfers between devices: 11 us -> 0.01 us  [by_head(): return lax.all_to_all(x, 'head', 0, 0, tiled=True)]
    all_to_all x2, waiting for transfers between devices: 2.87 us -> 11.3 us  [entry(): lax.all_to_all(sent.reshape(16, nh, 2, CH, DH), ('yh', 'head'), 0, 0, til...]
    ppermute x2, waiting for transfers between devices: 8.13 us -> 3.24 us  [swap(): return lax.ppermute(x, 'c', [(0, 1), (1, 0)])]
    ppermute x2, starting transfers between devices: 12.4 us -> 7.63 us  [send(): big = lax.ppermute(big, TM, BIG_PAIRS)]
    all_to_all x2 -> x3, starting transfers between devices: 9.18 us -> 12.6 us  [by_head(): return lax.all_to_all(x, 'head', 0, 0, tiled=True)]
    unnamed x30 -> x24, local copies, waits for them, and re-layouts: 7.5 us -> 4.32 us
  transfers between devices with their start and end apart: 19 -> 18, of which waited for: 6 -> 6; matrix products, arithmetic and copies ran while one was open for 0% -> 0% of each run, Pallas kernels for 38% -> 44%
where the time goes in v3:
time: 198 us; the launch traced here: 197 us
  Pallas kernels  93.7 us (47%)
  starting transfers between devices  44.3 us (22%)
  waiting for transfers between devices  39.9 us (20%)
  blocking collectives  13.6 us (7%)
  local copies, waits for them, and re-layouts  4.95 us (2%)
    pallas_call x2, Pallas kernels, near(): pl.pallas_call(near_body, grid=(nh,), in_specs=[smem(), smem(), tokens, f...  34.4 us
    ppermute x2, waiting for transfers between devices, send(): big = lax.ppermute(big, TM, BIG_PAIRS)  21.1 us
    pallas_call x2, Pallas kernels, cross(): pl.pallas_call(cross_body, grid=(nh,), in_specs=[smem(), tokens] + block_...  18.1 us
    all_to_all x1, blocking collectives, by_head(): return lax.all_to_all(x, 'head', 0, 0, tiled=True)  13.6 us
    ppermute x9, starting transfers between devices, around(): return lax.ppermute(x, 'z', [(i, (i + shift) % 4) for i in range(4)])  13.2 us
    all_to_all x3, starting transfers between devices, by_head(): return lax.all_to_all(x, 'head', 0, 0, tiled=True)  12.6 us
    pallas_call x2, Pallas kernels, far(): pl.pallas_call(far_body, grid=(nh,), in_specs=[smem(), smem(), tokens, he...  11.9 us
    all_to_all x2, waiting for transfers between devices, entry(): lax.all_to_all(sent.reshape(16, nh, 2, CH, DH), ('yh', 'head'), 0, 0, til...  11.3 us
  transfers between devices with their start and end apart: 18, of which 6 were waited for; matrix products, arithmetic and copies ran while one was open for 0% of the time, Pallas kernels for 44%

profile of v3, /device:TPU:32, one launch (start us, length us, event | category | flops | bytes accessed | tf_op | source)
XLA Modules:
  0.0 196.6 jit_solution(16853698668415526701)
XLA Ops:
  0.6 3.5 %enter_kv.2 = bf16[2,8,1,2,160,128]{5,4,3,2,1,0:T(8,128)(2,1)} custom-call(s32[5]{0:T(128)} %stack.23.refs_0_.place_ref, f32[1,128]{1,0:T(1,128)} %constant.24.clone.refs_1_, bf16[160,24,128]{2,1,0:T(8,128)(2,1)} %refs_2_.2, bf16[160,24,128]{2,1,0:T(8,128)(2,1)} %refs_3_.2), custom_call_target="tpu_custom_call" | custom-call | tf_op jit(solution)/shard_map/enter_kv/pallas_call | solution.py:176
  4.2 7.0 %all-to-all-start = ((bf16[16,1,2,160,128]{4,3,2,1,0:T(8,128)(2,1)}), bf16[16,1,2,160,128]{4,3,2,1,0:T(8,128)(2,1)S(1)}, u32[]{:S(2)}, u32[]{:S(2)}) async-start(bf16[16,1,2,160,128]{4,3,2,1,0:T(8,128)(2,1)} %bitcast.18), calls=%async_computation | async-start | bytes 2621440 | tf_op jit(solution)/shard_map/all_to_all | solution.py:490
  11.2 4.3 %tables.1 = (s32[4,128]{1,0:T(4,128)}, s32[64]{0:T(128)}, s32[16]{0:T(128)}) custom-call(s32[5]{0:T(128)} %stack.23.refs_0_.place_ref, s32[10,16]{1,0:T(8,128)} %list_ref, s32[10,16]{1,0:T(8,128)} %count_ref.1), custom_call_target="tpu_custom_call" | custom-call | tf_op jit(solution)/shard_map/tables/pallas_call | solution.py:123
  21.2 4.4 %enter_kv.3 = bf16[2,8,2,2,160,128]{5,4,3,2,1,0:T(8,128)(2,1)} custom-call(s32[5]{0:T(128)} %stack.23.refs_0_.place_ref, f32[1,128]{1,0:T(1,128)} %constant.24.clone.refs_1_, bf16[160,24,128]{2,1,0:T(8,128)(2,1)} %refs_2_.2, bf16[160,24,128]{2,1,0:T(8,128)(2,1)} %refs_3_.2), custom_call_target="tpu_custom_call" | custom-call | tf_op jit(solution)/shard_map/enter_kv/pallas_call | solution.py:176
  25.6 6.4 %all-to-all-done = bf16[16,1,2,160,128]{4,3,2,1,0:T(8,128)(2,1)S(1)} async-done(((bf16[16,1,2,160,128]{4,3,2,1,0:T(8,128)(2,1)}), bf16[16,1,2,160,128]{4,3,2,1,0:T(8,128)(2,1)S(1)}, u32[]{:S(2)}, u32[]{:S(2)}) %all-to-all-start) | async-done | bytes 1310752 | tf_op jit(solution)/shard_map/all_to_all | solution.py:490
  33.1 3.7 %all-to-all-start.1 = ((bf16[16,2,2,160,128]{4,3,2,1,0:T(8,128)(2,1)}), bf16[16,2,2,160,128]{4,3,2,1,0:T(8,128)(2,1)S(1)}, u32[]{:S(2)}, u32[]{:S(2)}) async-start(bf16[16,2,2,160,128]{4,3,2,1,0:T(8,128)(2,1)} %bitcast.17), calls=%async_computation.1 | async-start | bytes 5242880 | tf_op jit(solution)/shard_map/all_to_all | solution.py:490
  36.9 3.2 %collective-permute-done.3.sib_ref = bf16[2,8,1,2,160,128]{5,4,3,2,1,0:T(8,128)(2,1)S(1)} collective-permute-done((bf16[2,8,1,2,160,128]{5,4,3,2,1,0:T(8,128)(2,1)}, bf16[2,8,1,2,160,128]{5,4,3,2,1,0:T(8,128)(2,1)S(1)}, u32[]{:S(2)}, u32[]{:S(2)}) %collective-permute-start.3) | collective-permute-done | bytes 1310752 | tf_op jit(solution)/shard_map/ppermute | solution.py:494
  46.3 3.8 %collective-permute-start.4 = (bf16[8,1,2,128,128]{4,3,2,1,0:T(8,128)(2,1)}, bf16[8,1,2,128,128]{4,3,2,1,0:T(8,128)(2,1)S(1)}, u32[]{:S(2)}, u32[]{:S(2)}) collective-permute-start(bf16[8,1,2,128,128]{4,3,2,1,0:T(8,128)(2,1)} %get-tuple-element.71), channel_id=1, source_target_pairs={{0,32},{32,64},{64,96},{56,24},{88,56},{120,88},{1,33},{33,65},{65... | collective-permute-start | bytes 1572872 | tf_op jit(solution)/shard_map/ppermute | solution.py:501
  56.0 13.7 %collective-permute-done.4.big_ref = bf16[8,1,2,128,128]{4,3,2,1,0:T(8,128)(2,1)S(1)} collective-permute-done((bf16[8,1,2,128,128]{4,3,2,1,0:T(8,128)(2,1)}, bf16[8,1,2,128,128]{4,3,2,1,0:T(8,128)(2,1)S(1)}, u32[]{:S(2)}, u32[]{:S(2)}) %collective-permute-start.4) | collective-permute-done | bytes 524320 | tf_op jit(solution)/shard_map/ppermute | solution.py:501
  70.6 4.9 %all-to-all-done.1 = bf16[16,2,2,160,128]{4,3,2,1,0:T(8,128)(2,1)S(1)} async-done(((bf16[16,2,2,160,128]{4,3,2,1,0:T(8,128)(2,1)}), bf16[16,2,2,160,128]{4,3,2,1,0:T(8,128)(2,1)S(1)}, u32[]{:S(2)}, u32[]{:S(2)}) %all-to-all-start.1) | async-done | bytes 2621472 | tf_op jit(solution)/shard_map/all_to_all | solution.py:490
  78.5 3.4 %all-to-all-start.2 = ((bf16[8,1,160,128]{3,2,1,0:T(8,128)(2,1)}), bf16[8,1,160,128]{3,2,1,0:T(8,128)(2,1)S(1)}, u32[]{:S(2)}, u32[]{:S(2)}) async-start(bf16[8,1,160,128]{3,2,1,0:T(8,128)(2,1)} %enter_q.2), calls=%async_computation.2 | async-start | bytes 655360 | tf_op jit(solution)/shard_map/all_to_all | solution.py:497
  81.9 5.5 %pack.3 = (bf16[8,2,2,128,128]{4,3,2,1,0:T(8,128)(2,1)}, bf16[12,2,2,128,128]{4,3,2,1,0:T(8,128)(2,1)}, bf16[8,2,2,128,128]{4,3,2,1,0:T(8,128)(2,1)}, bf16[12,2,2,128,128]{4,3,2,1,0:T(8,128)(2,1)}) custom-call(s32[5]{0:T(128)} %stack.23.refs_0_.place_ref, s32[4,128]{1,0:T(4,128)} %copy-done.11, s32[4,128]{1,0:T(4,128)} %copy-done.10, s32[4,128]{1,0:T(4,128)} %copy-done.9, ...), custom_call_target="tpu_custom_call" | custom-call | tf_op jit(solution)/shard_map/pack/pallas_call | solution.py:233
  87.4 4.2 %collective-permute-done.8.in2 = bf16[8,1,2,128,128]{4,3,2,1,0:T(8,128)(2,1)} collective-permute-done((bf16[8,1,2,128,128]{4,3,2,1,0:T(8,128)(2,1)}, bf16[8,1,2,128,128]{4,3,2,1,0:T(8,128)(2,1)}, u32[]{:S(2)}, u32[]{:S(2)}) %collective-permute-start.8) | collective-permute-done | bytes 524320 | tf_op jit(solution)/shard_map/ppermute | solution.py:486
  93.7 3.8 %collective-permute-start.9 = (bf16[8,2,2,128,128]{4,3,2,1,0:T(8,128)(2,1)}, bf16[8,2,2,128,128]{4,3,2,1,0:T(8,128)(2,1)}, u32[]{:S(2)}, u32[]{:S(2)}) collective-permute-start(bf16[8,2,2,128,128]{4,3,2,1,0:T(8,128)(2,1)} %get-tuple-element.95), channel_id=1, source_target_pairs={{0,32},{32,64},{64,96},{56,24},{88,56},{120,88},{1,33},{33,65},{65... | collective-permute-start | bytes 3145736 | tf_op jit(solution)/shard_map/ppermute | solution.py:501
  98.0 3.7 %all-to-all-start.4 = ((bf16[8,2,160,128]{3,2,1,0:T(8,128)(2,1)}), bf16[8,2,160,128]{3,2,1,0:T(8,128)(2,1)S(1)}, u32[]{:S(2)}, u32[]{:S(2)}) async-start(bf16[8,2,160,128]{3,2,1,0:T(8,128)(2,1)} %enter_q.3), calls=%async_computation.4 | async-start | bytes 1310720 | tf_op jit(solution)/shard_map/all_to_all | solution.py:497
  101.8 12.4 %near.2 = (f32[1,1280,128]{2,1,0:T(8,128)}, f32[1,1280,128]{2,1,0:T(8,128)}, f32[1,1280,128]{2,1,0:T(8,128)}) custom-call(s32[5]{0:T(128)} %stack.23.refs_0_.place_ref, s32[16]{0:T(128)} %get-tuple-element.85.plane_ref, bf16[8,1,160,128]{3,2,1,0:T(8,128)(2,1)} %copy-done.4, bf16[2,8,1,2,160,128]{5,4,3,2,1,0:T(8,128)(2,1)} %bitcast.16, ...), custom_call_target="tpu_custom_call" | custom-call | tf_op jit(solution)/shard_map/near/pallas_call | solution.py:345
  114.2 7.1 %cross.2 = (f32[1,1280,128]{2,1,0:T(8,128)}, f32[1,1280,128]{2,1,0:T(8,128)}, f32[1,1280,128]{2,1,0:T(8,128)}) custom-call(s32[5]{0:T(128)} %stack.23.refs_0_.place_ref, bf16[8,1,160,128]{3,2,1,0:T(8,128)(2,1)} %copy-done.4, bf16[8,1,2,128,128]{4,3,2,1,0:T(8,128)(2,1)} %copy-done.8, bf16[12,1,2,128,128]{4,3,2,1,0:T(8,128)(2,1)} %copy-done.6, ...), custom_call_target="tpu_custom_call" | custom-call | tf_op jit(solution)/shard_map/cross/pallas_call | solution.py:401
  121.3 4.9 %far.2 = bf16[8,1,160,128]{3,2,1,0:T(8,128)(2,1)} custom-call(s32[5]{0:T(128)} %stack.23.refs_0_.place_ref, s32[64]{0:T(128)} %get-tuple-element.56.qslot_ref, bf16[8,1,160,128]{3,2,1,0:T(8,128)(2,1)} %copy-done.4, f32[1,1280,128]{2,1,0:T(8,128)} %get-tuple-element.89.acc_in, f32[1,1280,128]{2,1,0:T(8,128)} %get-tuple-element.90.m_in, ...), custom_call_target="tpu_custom_call" | custom-call | tf_op jit(solution)/shard_map/far/pallas_call | solution.py:433
  126.3 5.5 %all-to-all-start.3 = ((bf16[8,1,160,128]{3,2,1,0:T(8,128)(2,1)}), bf16[8,1,160,128]{3,2,1,0:T(8,128)(2,1)S(1)}, u32[]{:S(2)}, u32[]{:S(2)}) async-start(bf16[8,1,160,128]{3,2,1,0:T(8,128)(2,1)} %far.2), calls=%async_computation.3 | async-start | bytes 655360 | tf_op jit(solution)/shard_map/all_to_all | solution.py:497
  131.7 22.0 %near.3 = (f32[2,1280,128]{2,1,0:T(8,128)}, f32[2,1280,128]{2,1,0:T(8,128)}, f32[2,1280,128]{2,1,0:T(8,128)}) custom-call(s32[5]{0:T(128)} %stack.23.refs_0_.place_ref, s32[16]{0:T(128)} %get-tuple-element.85.plane_ref, bf16[8,2,160,128]{3,2,1,0:T(8,128)(2,1)} %copy-done.2, bf16[2,8,2,2,160,128]{5,4,3,2,1,0:T(8,128)(2,1)} %bitcast.13, ...), custom_call_target="tpu_custom_call" | custom-call | tf_op jit(solution)/shard_map/near/pallas_call | solution.py:345
  153.7 7.4 %collective-permute-done.9.big_ref = bf16[8,2,2,128,128]{4,3,2,1,0:T(8,128)(2,1)} collective-permute-done((bf16[8,2,2,128,128]{4,3,2,1,0:T(8,128)(2,1)}, bf16[8,2,2,128,128]{4,3,2,1,0:T(8,128)(2,1)}, u32[]{:S(2)}, u32[]{:S(2)}) %collective-permute-start.9) | collective-permute-done | bytes 1048608 | tf_op jit(solution)/shard_map/ppermute | solution.py:501
  162.4 11.0 %cross.3 = (f32[2,1280,128]{2,1,0:T(8,128)}, f32[2,1280,128]{2,1,0:T(8,128)}, f32[2,1280,128]{2,1,0:T(8,128)}) custom-call(s32[5]{0:T(128)} %stack.23.refs_0_.place_ref, bf16[8,2,160,128]{3,2,1,0:T(8,128)(2,1)} %copy-done.2, bf16[8,2,2,128,128]{4,3,2,1,0:T(8,128)(2,1)} %collective-permute-done.9.big_ref, bf16[12,2,2,128,128]{4,3,2,1,0:T(8,128)(2,1)} %copy-done.3, ...), custom_call_target="tpu_custom_call" | custom-call | tf_op jit(solution)/shard_map/cross/pallas_call | solution.py:401
  173.3 7.0 %far.3 = bf16[8,2,160,128]{3,2,1,0:T(8,128)(2,1)} custom-call(s32[5]{0:T(128)} %stack.23.refs_0_.place_ref, s32[64]{0:T(128)} %get-tuple-element.56.qslot_ref, bf16[8,2,160,128]{3,2,1,0:T(8,128)(2,1)} %copy-done.2, f32[2,1280,128]{2,1,0:T(8,128)} %get-tuple-element.101.acc_in, f32[2,1280,128]{2,1,0:T(8,128)} %get-tuple-element.102.m_in, ...), custom_call_target="tpu_custom_call" | custom-call | tf_op jit(solution)/shard_map/far/pallas_call | solution.py:433
  180.3 13.6 %all_to_all.30.refs_1_ = bf16[8,2,160,128]{3,2,1,0:T(8,128)(2,1)} all-to-all(bf16[8,2,160,128]{3,2,1,0:T(8,128)(2,1)} %far.3), channel_id=1, replica_groups=mesh['z'=4,'yh'=2,'c'=2,'head'=8] {'head'}, dimensions={0} | all-to-all | bytes 1310720 | tf_op jit(solution)/shard_map/all_to_all | solution.py:497
  (52 shorter events, 29.9 us)
Async XLA Ops:
  4.2 27.9 %all-to-all-start = ((bf16[16,1,2,160,128]{4,3,2,1,0:T(8,128)(2,1)}), bf16[16,1,2,160,128]{4,3,2,1,0:T(8,128)(2,1)S(1)}, u32[]{:S(2)}, u32[]{:S(2)}) async-start(bf16[16,1,2,160,128]{4,3,2,1,0:T(8,128)(2,1)} %bitcast.18), calls=%async_computation | async-start | bytes 2621440 | tf_op jit(solution)/shard_map/all_to_all | solution.py:490
  15.5 10.0 %collective-permute-start.2 = (s32[4,128]{1,0:T(4,128)}, s32[4,128]{1,0:T(4,128)S(1)}, u32[]{:S(2)}, u32[]{:S(2)}) collective-permute-start(s32[4,128]{1,0:T(4,128)} %get-tuple-element.60), channel_id=1, source_target_pairs={{0,32},{32,64},{64,96},{96,0},{1,33},{33,65},{65,97},{97,1},{2,34}... | collective-permute-start | bytes 6152 | tf_op jit(solution)/shard_map/ppermute | solution.py:486
  17.5 8.1 %collective-permute-start.1 = (s32[4,128]{1,0:T(4,128)}, s32[4,128]{1,0:T(4,128)S(1)}, u32[]{:S(2)}, u32[]{:S(2)}) collective-permute-start(s32[4,128]{1,0:T(4,128)} %get-tuple-element.60), channel_id=1, source_target_pairs={{0,64},{32,96},{64,0},{96,32},{1,65},{33,97},{65,1},{97,33},{2,66}... | collective-permute-start | bytes 6152 | tf_op jit(solution)/shard_map/ppermute | solution.py:486
  18.6 6.9 %collective-permute-start = (s32[4,128]{1,0:T(4,128)}, s32[4,128]{1,0:T(4,128)S(1)}, u32[]{:S(2)}, u32[]{:S(2)}) collective-permute-start(s32[4,128]{1,0:T(4,128)} %get-tuple-element.60), channel_id=1, source_target_pairs={{0,96},{32,0},{64,32},{96,64},{1,97},{33,1},{65,33},{97,65},{2,98}... | collective-permute-start | bytes 6152 | tf_op jit(solution)/shard_map/ppermute | solution.py:486
  25.5 7.6 %copy-start.9 = (s32[4,128]{1,0:T(4,128)}, s32[4,128]{1,0:T(4,128)S(1)}, u32[]{:S(2)}) copy-start(s32[4,128]{1,0:T(4,128)S(1)} %collective-permute-done.2.ask3) | copy-start | bytes 6148
  25.6 14.6 %copy-start.10 = (s32[4,128]{1,0:T(4,128)}, s32[4,128]{1,0:T(4,128)S(1)}, u32[]{:S(2)}) copy-start(s32[4,128]{1,0:T(4,128)S(1)} %collective-permute-done.1.ask2) | copy-start | bytes 6148
  25.6 14.6 %copy-start.11 = (s32[4,128]{1,0:T(4,128)}, s32[4,128]{1,0:T(4,128)S(1)}, u32[]{:S(2)}) copy-start(s32[4,128]{1,0:T(4,128)S(1)} %collective-permute-done.ask1) | copy-start | bytes 6148
  33.1 42.4 %all-to-all-start.1 = ((bf16[16,2,2,160,128]{4,3,2,1,0:T(8,128)(2,1)}), bf16[16,2,2,160,128]{4,3,2,1,0:T(8,128)(2,1)S(1)}, u32[]{:S(2)}, u32[]{:S(2)}) async-start(bf16[16,2,2,160,128]{4,3,2,1,0:T(8,128)(2,1)} %bitcast.17), calls=%async_computation.1 | async-start | bytes 5242880 | tf_op jit(solution)/shard_map/all_to_all | solution.py:490
  36.8 3.3 %collective-permute-start.3 = (bf16[2,8,1,2,160,128]{5,4,3,2,1,0:T(8,128)(2,1)}, bf16[2,8,1,2,160,128]{5,4,3,2,1,0:T(8,128)(2,1)S(1)}, u32[]{:S(2)}, u32[]{:S(2)}) collective-permute-start(bf16[2,8,1,2,160,128]{5,4,3,2,1,0:T(8,128)(2,1)} %bitcast.14), channel_id=1, source_target_pairs={{0,8},{8,0},{1,9},{9,1},{2,10},{10,2},{3,11},{11,3},{4,12},{12,4},... | collective-permute-start | bytes 3932168 | tf_op jit(solution)/shard_map/ppermute | solution.py:494
  44.3 25.4 %collective-permute-start.5 = (bf16[12,1,2,128,128]{4,3,2,1,0:T(8,128)(2,1)}, bf16[12,1,2,128,128]{4,3,2,1,0:T(8,128)(2,1)S(1)}, u32[]{:S(2)}, u32[]{:S(2)}) collective-permute-start(bf16[12,1,2,128,128]{4,3,2,1,0:T(8,128)(2,1)} %get-tuple-element.72), channel_id=1, source_target_pairs={{0,32},{32,64},{64,96},{96,0},{1,33},{33,65},{65,97},{97,1},{2,34}... | collective-permute-start | bytes 2359304 | tf_op jit(solution)/shard_map/ppermute | solution.py:486
  46.2 24.4 %collective-permute-start.6 = (bf16[12,1,2,128,128]{4,3,2,1,0:T(8,128)(2,1)}, bf16[12,1,2,128,128]{4,3,2,1,0:T(8,128)(2,1)}, u32[]{:S(2)}, u32[]{:S(2)}) collective-permute-start(bf16[12,1,2,128,128]{4,3,2,1,0:T(8,128)(2,1)} %get-tuple-element.73), channel_id=1, source_target_pairs={{0,96},{32,0},{64,32},{96,64},{1,97},{33,1},{65,33},{97,65},{2,98}... | collective-permute-start | bytes 2359304 | tf_op jit(solution)/shard_map/ppermute | solution.py:486
  46.3 23.4 %collective-permute-start.4 = (bf16[8,1,2,128,128]{4,3,2,1,0:T(8,128)(2,1)}, bf16[8,1,2,128,128]{4,3,2,1,0:T(8,128)(2,1)S(1)}, u32[]{:S(2)}, u32[]{:S(2)}) collective-permute-start(bf16[8,1,2,128,128]{4,3,2,1,0:T(8,128)(2,1)} %get-tuple-element.71), channel_id=1, source_target_pairs={{0,32},{32,64},{64,96},{56,24},{88,56},{120,88},{1,33},{33,65},{65... | collective-permute-start | bytes 1572872 | tf_op jit(solution)/shard_map/ppermute | solution.py:501
  69.7 44.5 %copy-start.8 = (bf16[8,1,2,128,128]{4,3,2,1,0:T(8,128)(2,1)}, bf16[8,1,2,128,128]{4,3,2,1,0:T(8,128)(2,1)S(1)}, u32[]{:S(2)}) copy-start(bf16[8,1,2,128,128]{4,3,2,1,0:T(8,128)(2,1)S(1)} %collective-permute-done.4.big_ref) | copy-start | bytes 1572868
  75.5 6.4 %collective-permute-start.7 = (bf16[2,8,2,2,160,128]{5,4,3,2,1,0:T(8,128)(2,1)S(1)}, bf16[2,8,2,2,160,128]{5,4,3,2,1,0:T(8,128)(2,1)}, u32[]{:S(2)}, u32[]{:S(2)}) collective-permute-start(bf16[2,8,2,2,160,128]{5,4,3,2,1,0:T(8,128)(2,1)S(1)} %bitcast.11), channel_id=1, source_target_pairs={{0,8},{8,0},{1,9},{9,1},{2,10},{10,2},{3,11},{11,3},{4,12},{12,4},... | collective-permute-start | bytes 7864328 | tf_op jit(solution)/shard_map/ppermute | solution.py:494
  75.5 16.2 %collective-permute-start.8 = (bf16[8,1,2,128,128]{4,3,2,1,0:T(8,128)(2,1)}, bf16[8,1,2,128,128]{4,3,2,1,0:T(8,128)(2,1)}, u32[]{:S(2)}, u32[]{:S(2)}) collective-permute-start(bf16[8,1,2,128,128]{4,3,2,1,0:T(8,128)(2,1)} %get-tuple-element.80), channel_id=1, source_target_pairs={{0,64},{32,96},{64,0},{96,32},{1,65},{33,97},{65,1},{97,33},{2,66}... | collective-permute-start | bytes 1572872 | tf_op jit(solution)/shard_map/ppermute | solution.py:486
  78.5 13.2 %all-to-all-start.2 = ((bf16[8,1,160,128]{3,2,1,0:T(8,128)(2,1)}), bf16[8,1,160,128]{3,2,1,0:T(8,128)(2,1)S(1)}, u32[]{:S(2)}, u32[]{:S(2)}) async-start(bf16[8,1,160,128]{3,2,1,0:T(8,128)(2,1)} %enter_q.2), calls=%async_computation.2 | async-start | bytes 655360 | tf_op jit(solution)/shard_map/all_to_all | solution.py:497
  91.7 10.1 %copy-start.4 = (bf16[8,1,160,128]{3,2,1,0:T(8,128)(2,1)}, bf16[8,1,160,128]{3,2,1,0:T(8,128)(2,1)S(1)}, u32[]{:S(2)}) copy-start(bf16[8,1,160,128]{3,2,1,0:T(8,128)(2,1)S(1)} %all-to-all-done.2.q_ref) | copy-start | bytes 983044
  91.7 69.5 %collective-permute-start.10 = (bf16[12,2,2,128,128]{4,3,2,1,0:T(8,128)(2,1)}, bf16[12,2,2,128,128]{4,3,2,1,0:T(8,128)(2,1)S(1)}, u32[]{:S(2)}, u32[]{:S(2)}) collective-permute-start(bf16[12,2,2,128,128]{4,3,2,1,0:T(8,128)(2,1)} %get-tuple-element.96), channel_id=1, source_target_pairs={{0,32},{32,64},{64,96},{96,0},{1,33},{33,65},{65,97},{97,1},{2,34}... | collective-permute-start | bytes 4718600 | tf_op jit(solution)/shard_map/ppermute | solution.py:486
  93.6 67.6 %collective-permute-start.11 = (bf16[12,2,2,128,128]{4,3,2,1,0:T(8,128)(2,1)}, bf16[12,2,2,128,128]{4,3,2,1,0:T(8,128)(2,1)}, u32[]{:S(2)}, u32[]{:S(2)}) collective-permute-start(bf16[12,2,2,128,128]{4,3,2,1,0:T(8,128)(2,1)} %get-tuple-element.97), channel_id=1, source_target_pairs={{0,96},{32,0},{64,32},{96,64},{1,97},{33,1},{65,33},{97,65},{2,98}... | collective-permute-start | bytes 4718600 | tf_op jit(solution)/shard_map/ppermute | solution.py:486
  93.7 67.5 %collective-permute-start.9 = (bf16[8,2,2,128,128]{4,3,2,1,0:T(8,128)(2,1)}, bf16[8,2,2,128,128]{4,3,2,1,0:T(8,128)(2,1)}, u32[]{:S(2)}, u32[]{:S(2)}) collective-permute-start(bf16[8,2,2,128,128]{4,3,2,1,0:T(8,128)(2,1)} %get-tuple-element.95), channel_id=1, source_target_pairs={{0,32},{32,64},{64,96},{56,24},{88,56},{120,88},{1,33},{33,65},{65... | collective-permute-start | bytes 3145736 | tf_op jit(solution)/shard_map/ppermute | solution.py:501
  97.5 75.8 %collective-permute-start.12 = (bf16[8,2,2,128,128]{4,3,2,1,0:T(8,128)(2,1)}, bf16[8,2,2,128,128]{4,3,2,1,0:T(8,128)(2,1)}, u32[]{:S(2)}, u32[]{:S(2)}) collective-permute-start(bf16[8,2,2,128,128]{4,3,2,1,0:T(8,128)(2,1)} %get-tuple-element.104), channel_id=1, source_target_pairs={{0,64},{32,96},{64,0},{96,32},{1,65},{33,97},{65,1},{97,33},{2,66}... | collective-permute-start | bytes 3145736 | tf_op jit(solution)/shard_map/ppermute | solution.py:486
  98.0 28.2 %all-to-all-start.4 = ((bf16[8,2,160,128]{3,2,1,0:T(8,128)(2,1)}), bf16[8,2,160,128]{3,2,1,0:T(8,128)(2,1)S(1)}, u32[]{:S(2)}, u32[]{:S(2)}) async-start(bf16[8,2,160,128]{3,2,1,0:T(8,128)(2,1)} %enter_q.3), calls=%async_computation.4 | async-start | bytes 1310720 | tf_op jit(solution)/shard_map/all_to_all | solution.py:497
  126.3 54.0 %all-to-all-start.3 = ((bf16[8,1,160,128]{3,2,1,0:T(8,128)(2,1)}), bf16[8,1,160,128]{3,2,1,0:T(8,128)(2,1)S(1)}, u32[]{:S(2)}, u32[]{:S(2)}) async-start(bf16[8,1,160,128]{3,2,1,0:T(8,128)(2,1)} %far.2), calls=%async_computation.3 | async-start | bytes 655360 | tf_op jit(solution)/shard_map/all_to_all | solution.py:497
  180.3 13.6 %copy-start.7 = (bf16[8,1,160,128]{3,2,1,0:T(8,128)(2,1)}, bf16[8,1,160,128]{3,2,1,0:T(8,128)(2,1)S(1)}, u32[]{:S(2)}) copy-start(bf16[8,1,160,128]{3,2,1,0:T(8,128)(2,1)S(1)} %all-to-all-done.3.refs_0_) | copy-start | bytes 983044
  (6 other events, 16.2 us)

commit v4 on v3

--- a/solution.py
+++ b/solution.py
@@ -328,8 +328,8 @@
     listed_pairs([pair(p) for p in range(8)], qs, m, l, acc, top, scores)
 
 
-def head_specs(at=0):
-    tokens = pl.BlockSpec((8, 1, CH, DH), lambda h: (0, h + at if at else h, 0, 0))
+def head_specs():
+    tokens = pl.BlockSpec((8, 1, CH, DH), lambda h: (0, h, 0, 0))
     state = pl.BlockSpec((1, TOK, DH), lambda h: (h, 0, 0))
     return tokens, state
 
@@ -338,10 +338,10 @@
     return [jax.ShapeDtypeStruct((nh, TOK, DH), jnp.float32)] * 3
 
 
-def near(place, plane_pairs, q, own, sib, at):
+def near(place, plane_pairs, q, own, sib):
     nh = own.shape[2]
     frames = pl.BlockSpec((2, 8, 1, 2, CH, DH), lambda h: (0, 0, h, 0, 0, 0))
-    tokens, state = head_specs(at)
+    tokens, state = head_specs()
     return pl.pallas_call(
         near_body,
         grid=(nh,),
@@ -360,9 +360,18 @@
     )(place, plane_pairs, q, own, sib)
 
 
-def cross_body(place_ref, q_ref, big_ref, in1, in3, acc_in, m_in, l_in, acc_ref, m_ref, l_ref, kf, vf):
+def slots(z, qslot_ref, shift, ref):
+    zp = (z + 4 - shift) % 4
+    for s in range(ref.shape[0]):
+        yield qslot_ref[zp * BESIDE + s], lambda s=s: ref[s, 0, 0], lambda s=s: ref[s, 0, 1]
+
+
+def beside_body(
+    place_ref, qslot_ref, q_ref, big_ref, in1, in3, acc_in, m_in, l_in, acc_ref, m_ref, l_ref, qs, kf, vf, top, scores
+):
     z, r = place_ref[0], place_ref[1]
     touches = ((r == 0) & (z > 0)) | ((r == PLANE - 1) & (z < 3))
+    qs[...] = q_ref[:, 0].reshape(TOK, DH)
 
     @pl.when(touches)
     def _():
@@ -371,10 +380,9 @@
             for n in range(BIG, NB):
                 s = BASE + 1 + n - BIG
                 ref[n * BLK : (n + 1) * BLK] = jnp.where(r == 0, in1[s, 0, kv], in3[s, 0, kv])
-        q = q_ref[:, 0].reshape(TOK, DH)
         for t in range(TOK // QT):
             rows = slice(t * QT, (t + 1) * QT)
-            s = dot_t(q[rows], kf[...]) * SCALE
+            s = dot_t(qs[rows], kf[...]) * SCALE
             m_old = m_in[0, rows]
             m_new = jnp.maximum(m_old, jnp.max(by_lane(jnp.maximum, s), axis=1, keepdims=True))
             p = jnp.exp2(s - m_new[:, :1])
@@ -390,58 +398,55 @@
         m_ref[...] = m_in[...]
         l_ref[...] = l_in[...]
 
+    pairs = [*slots(z, qslot_ref, 1, in1), *slots(z, qslot_ref, 3, in3)]
+    listed_pairs(pairs, qs, m_ref.at[0], l_ref.at[0], acc_ref.at[0], top, scores)
+
 
 def block_specs(arrays):
     return [pl.BlockSpec((x.shape[0], 1, 2, BLK, DH), lambda h: (0, h, 0, 0, 0)) for x in arrays]
 
 
-def cross(place, q, big, in1, in3, state, at):
+def beside(place, qslot, q, big, in1, in3, state):
     nh = big.shape[1]
-    tokens, held = head_specs(at)
-    return pl.pallas_call(
-        cross_body,
+    tokens, held = head_specs()
+    return pl.pallas_call(
+        beside_body,
         grid=(nh,),
-        in_specs=[smem(), tokens] + block_specs((big, in1, in3)) + [held] * 3,
+        in_specs=[smem(), smem(), tokens] + block_specs((big, in1, in3)) + [held] * 3,
         out_specs=[held] * 3,
         out_shape=state_shapes(nh),
-        scratch_shapes=[pltpu.VMEM((TOK, DH), jnp.bfloat16)] * 2,
-        compiler_params=params(),
-        name="cross",
-    )(place, q, big, in1, in3, *state)
-
-
-def far_body(place_ref, qslot_ref, q_ref, acc_in, m_in, l_in, in1, in2, in3, o_ref, qs, acc, m, l, top, scores):
-    z = place_ref[0]
+        scratch_shapes=[pltpu.VMEM((TOK, DH), jnp.bfloat16)] * 3
+        + [pltpu.VMEM((TOK, DH), jnp.float32), pltpu.VMEM((2 * BESIDE, BLK, BLK), jnp.float32)],
+        compiler_params=params(),
+        name="beside",
+    )(place, qslot, q, big, in1, in3, *state)
+
+
+def across_body(place_ref, qslot_ref, q_ref, acc_in, m_in, l_in, in2, o_ref, qs, acc, m, l, top, scores):
     qs[...] = q_ref[:, 0].reshape(TOK, DH)
     acc[...] = acc_in[0]
     m[...] = m_in[0]
     l[...] = l_in[0]
-    pairs = []
-    for shift, ref in ((1, in1), (2, in2), (3, in3)):
-        zp = (z + 4 - shift) % 4
-        for s in range(ref.shape[0]):
-            block = qslot_ref[zp * BESIDE + s]
-            pairs.append((block, lambda ref=ref, s=s: ref[s, 0, 0], lambda ref=ref, s=s: ref[s, 0, 1]))
-    listed_pairs(pairs, qs, m, l, acc, top, scores)
+    listed_pairs([*slots(place_ref[0], qslot_ref, 2, in2)], qs, m, l, acc, top, scores)
     total = jnp.sum(l[...], axis=1, keepdims=True)
     o_ref[:, 0] = (acc[...] / total).astype(jnp.bfloat16).reshape(8, CH, DH)
 
 
-def far(place, qslot, q, state, base, at):
-    nh = base[0].shape[1]
-    tokens, held = head_specs(at)
-    return pl.pallas_call(
-        far_body,
+def across(place, qslot, q, state, in2):
+    nh = in2.shape[1]
+    tokens, held = head_specs()
+    return pl.pallas_call(
+        across_body,
         grid=(nh,),
-        in_specs=[smem(), smem(), tokens, held, held, held] + block_specs(base),
-        out_specs=pl.BlockSpec((8, 1, CH, DH), lambda h: (0, h, 0, 0)),
+        in_specs=[smem(), smem(), tokens, held, held, held] + block_specs((in2,)),
+        out_specs=tokens,
         out_shape=jax.ShapeDtypeStruct((8, nh, CH, DH), jnp.bfloat16),
         scratch_shapes=[pltpu.VMEM((TOK, DH), jnp.bfloat16)]
         + [pltpu.VMEM((TOK, DH), jnp.float32)] * 4
-        + [pltpu.VMEM((2 * BESIDE + BASE, BLK, BLK), jnp.float32)],
-        compiler_params=params(),
-        name="far",
-    )(place, qslot, q, *state, *base)
+        + [pltpu.VMEM((BASE, BLK, BLK), jnp.float32)],
+        compiler_params=params(),
+        name="across",
+    )(place, qslot, q, *state, in2)
 
 
 def leave_body(groups, *refs):
@@ -514,21 +519,21 @@
     packed_a, query = together(packed_a, query)
     big_a, in1_a, in2_a, in3_a = send(packed_a)
     q_a, q_b = (enter_q(place, rates, query, rows) for rows in CHUNKS)
-    own_b, q_a, q_b, big_a, in1_a, in3_a = together(own_b, q_a, q_b, big_a, in1_a, in3_a)
+    own_b, q_a, q_b, in1_a, in2_a, in3_a = together(own_b, q_a, q_b, in1_a, in2_a, in3_a)
     sib_b = swap(own_b)
     q_a = by_head(q_a)
     packed_b = pack(place, asked, own_b, sib_b)
-    packed_b, q_a, in2_a = together(packed_b, q_a, in2_a)
+    packed_b, q_a, big_a = together(packed_b, q_a, big_a)
     big_b, in1_b, in2_b, in3_b = send(packed_b)
     q_b = by_head(q_b)
-    state_a = near(place, plane_pairs, q_a, own_a, sib_a, 0)
-    state_a = cross(place, q_a, big_a, in1_a, in3_a, state_a, 0)
-    done_a = far(place, qslot, q_a, state_a, (in1_a, in2_a, in3_a), 0)
+    state_a = near(place, plane_pairs, q_a, own_a, sib_a)
+    state_a = beside(place, qslot, q_a, big_a, in1_a, in3_a, state_a)
+    done_a = across(place, qslot, q_a, state_a, in2_a)
     out_a = by_head(done_a)
     q_b, _ = together(q_b, done_a)
-    state_b = near(place, plane_pairs, q_b, own_b, sib_b, 0)
-    state_b = cross(place, q_b, big_b, in1_b, in3_b, state_b, 0)
-    out_b = by_head(far(place, qslot, q_b, state_b, (in1_b, in2_b, in3_b), 0))
+    state_b = near(place, plane_pairs, q_b, own_b, sib_b)
+    state_b = beside(place, qslot, q_b, big_b, in1_b, in3_b, state_b)
+    out_b = by_head(across(place, qslot, q_b, state_b, in2_b))
     return leave((out_a, out_b), CHUNKS)
 
 

time: 198 us -> 196 us (0.990)
  waiting for transfers between devices: 39.9 us -> 34.6 us
    ppermute x2, waiting for transfers between devices: 21.1 us -> 0.01 us  [send(): big = lax.ppermute(big, TM, BIG_PAIRS)]
    ppermute x9, waiting for transfers between devices: 4.24 us -> 22.9 us  [around(): return lax.ppermute(x, 'z', [(i, (i + shift) % 4) for i in range(4)])]
    all_to_all x2, waiting for transfers between devices: 11.3 us -> 6.44 us  [entry(): lax.all_to_all(sent.reshape(16, nh, 2, CH, DH), ('yh', 'head'), 0, 0, til...]
    ppermute x2, starting transfers between devices: 7.63 us -> 5.18 us  [send(): big = lax.ppermute(big, TM, BIG_PAIRS)]
    all_to_all x3, starting transfers between devices: 12.6 us -> 14.9 us  [by_head(): return lax.all_to_all(x, 'head', 0, 0, tiled=True)]
    all_to_all x3, waiting for transfers between devices: 0.01 us -> 2.05 us  [by_head(): return lax.all_to_all(x, 'head', 0, 0, tiled=True)]
    unnamed x24 -> x26, local copies, waits for them, and re-layouts: 4.32 us -> 5.14 us
  transfers between devices with their start and end apart: 18 -> 18, of which waited for: 6 -> 4; matrix products, arithmetic and copies ran while one was open for 0% -> 0% of each run, Pallas kernels for 44% -> 45%
where the time goes in v4:
time: 196 us; the launch traced here: 194 us
  Pallas kernels  94 us (48%)
  starting transfers between devices  43.9 us (22%)
  waiting for transfers between devices  34.6 us (18%)
  blocking collectives  15.2 us (8%)
  local copies, waits for them, and re-layouts  5.81 us (3%)
    pallas_call x2, Pallas kernels, near(): pl.pallas_call(near_body, grid=(nh,), in_specs=[smem(), smem(), tokens, f...  34.4 us
    ppermute x9, waiting for transfers between devices, around(): return lax.ppermute(x, 'z', [(i, (i + shift) % 4) for i in range(4)])  22.9 us
    pallas_call x2, Pallas kernels, beside(): pl.pallas_call(beside_body, grid=(nh,), in_specs=[smem(), smem(), tokens]...  22.3 us
    all_to_all x1, blocking collectives, by_head(): return lax.all_to_all(x, 'head', 0, 0, tiled=True)  15.2 us
    all_to_all x3, starting transfers between devices, by_head(): return lax.all_to_all(x, 'head', 0, 0, tiled=True)  14.9 us
    ppermute x9, starting transfers between devices, around(): return lax.ppermute(x, 'z', [(i, (i + shift) % 4) for i in range(4)])  12.9 us
    all_to_all x2, starting transfers between devices, entry(): lax.all_to_all(sent.reshape(16, nh, 2, CH, DH), ('yh', 'head'), 0, 0, til...  10.8 us
    pallas_call x2, Pallas kernels, pack(): pl.pallas_call(pack_body, grid=(nh, 2), in_specs=[smem()] * 4 + [whole, w...  8.6 us
  transfers between devices with their start and end apart: 18, of which 4 were waited for; matrix products, arithmetic and copies ran while one was open for 0% of the time, Pallas kernels for 45%

profile of v4, /device:TPU:32, one launch (start us, length us, event | category | flops | bytes accessed | tf_op | source)
XLA Modules:
  0.0 193.7 jit_solution(93985962517920569)
XLA Ops:
  0.7 3.5 %enter_kv.2 = bf16[2,8,1,2,160,128]{5,4,3,2,1,0:T(8,128)(2,1)} custom-call(s32[5]{0:T(128)} %stack.23.refs_0_.place_ref, f32[1,128]{1,0:T(1,128)} %constant.24.clone.refs_1_, bf16[160,24,128]{2,1,0:T(8,128)(2,1)} %refs_2_.2, bf16[160,24,128]{2,1,0:T(8,128)(2,1)} %refs_3_.2), custom_call_target="tpu_custom_call" | custom-call | tf_op jit(solution)/shard_map/enter_kv/pallas_call | solution.py:176
  4.2 7.0 %all-to-all-start = ((bf16[16,1,2,160,128]{4,3,2,1,0:T(8,128)(2,1)}), bf16[16,1,2,160,128]{4,3,2,1,0:T(8,128)(2,1)S(1)}, u32[]{:S(2)}, u32[]{:S(2)}) async-start(bf16[16,1,2,160,128]{4,3,2,1,0:T(8,128)(2,1)} %bitcast.18), calls=%async_computation | async-start | bytes 2621440 | tf_op jit(solution)/shard_map/all_to_all | solution.py:495
  11.2 4.3 %tables.1 = (s32[4,128]{1,0:T(4,128)}, s32[64]{0:T(128)}, s32[16]{0:T(128)}) custom-call(s32[5]{0:T(128)} %stack.23.refs_0_.place_ref, s32[10,16]{1,0:T(8,128)} %list_ref, s32[10,16]{1,0:T(8,128)} %count_ref.1), custom_call_target="tpu_custom_call" | custom-call | tf_op jit(solution)/shard_map/tables/pallas_call | solution.py:123
  21.2 4.4 %enter_kv.3 = bf16[2,8,2,2,160,128]{5,4,3,2,1,0:T(8,128)(2,1)} custom-call(s32[5]{0:T(128)} %stack.23.refs_0_.place_ref, f32[1,128]{1,0:T(1,128)} %constant.24.clone.refs_1_, bf16[160,24,128]{2,1,0:T(8,128)(2,1)} %refs_2_.2, bf16[160,24,128]{2,1,0:T(8,128)(2,1)} %refs_3_.2), custom_call_target="tpu_custom_call" | custom-call | tf_op jit(solution)/shard_map/enter_kv/pallas_call | solution.py:176
  25.6 6.4 %all-to-all-done = bf16[16,1,2,160,128]{4,3,2,1,0:T(8,128)(2,1)S(1)} async-done(((bf16[16,1,2,160,128]{4,3,2,1,0:T(8,128)(2,1)}), bf16[16,1,2,160,128]{4,3,2,1,0:T(8,128)(2,1)S(1)}, u32[]{:S(2)}, u32[]{:S(2)}) %all-to-all-start) | async-done | bytes 1310752 | tf_op jit(solution)/shard_map/all_to_all | solution.py:495
  33.1 3.7 %all-to-all-start.1 = ((bf16[16,2,2,160,128]{4,3,2,1,0:T(8,128)(2,1)}), bf16[16,2,2,160,128]{4,3,2,1,0:T(8,128)(2,1)S(1)}, u32[]{:S(2)}, u32[]{:S(2)}) async-start(bf16[16,2,2,160,128]{4,3,2,1,0:T(8,128)(2,1)} %bitcast.17), calls=%async_computation.1 | async-start | bytes 5242880 | tf_op jit(solution)/shard_map/all_to_all | solution.py:495
  37.0 3.2 %collective-permute-done.3.sib_ref = bf16[2,8,1,2,160,128]{5,4,3,2,1,0:T(8,128)(2,1)S(1)} collective-permute-done((bf16[2,8,1,2,160,128]{5,4,3,2,1,0:T(8,128)(2,1)}, bf16[2,8,1,2,160,128]{5,4,3,2,1,0:T(8,128)(2,1)S(1)}, u32[]{:S(2)}, u32[]{:S(2)}) %collective-permute-start.3) | collective-permute-done | bytes 1310752 | tf_op jit(solution)/shard_map/ppermute | solution.py:499
  41.3 3.0 %pack.2 = (bf16[8,1,2,128,128]{4,3,2,1,0:T(8,128)(2,1)}, bf16[12,1,2,128,128]{4,3,2,1,0:T(8,128)(2,1)}, bf16[8,1,2,128,128]{4,3,2,1,0:T(8,128)(2,1)}, bf16[12,1,2,128,128]{4,3,2,1,0:T(8,128)(2,1)}) custom-call(s32[5]{0:T(128)} %stack.23.refs_0_.place_ref, s32[4,128]{1,0:T(4,128)} %copy-done.12, s32[4,128]{1,0:T(4,128)} %copy-done.11, s32[4,128]{1,0:T(4,128)} %copy-done.10, ...), custom_call_target="tpu_custom_call" | custom-call | tf_op jit(solution)/shard_map/pack/pallas_call | solution.py:233
  46.4 3.0 %collective-permute-start.5 = (bf16[8,1,2,128,128]{4,3,2,1,0:T(8,128)(2,1)}, bf16[8,1,2,128,128]{4,3,2,1,0:T(8,128)(2,1)S(1)}, u32[]{:S(2)}, u32[]{:S(2)}) collective-permute-start(bf16[8,1,2,128,128]{4,3,2,1,0:T(8,128)(2,1)} %get-tuple-element.72), channel_id=1, source_target_pairs={{0,64},{32,96},{64,0},{96,32},{1,65},{33,97},{65,1},{97,33},{2,66}... | collective-permute-start | bytes 1572872 | tf_op jit(solution)/shard_map/ppermute | solution.py:491
  49.4 2.7 %enter_q.2 = bf16[8,1,160,128]{3,2,1,0:T(8,128)(2,1)} custom-call(s32[5]{0:T(128)} %stack.23.refs_0_.place_ref, f32[1,128]{1,0:T(1,128)} %constant.24.clone.refs_1_, bf16[160,24,128]{2,1,0:T(8,128)(2,1)} %refs_2_.4), custom_call_target="tpu_custom_call" | custom-call | tf_op jit(solution)/shard_map/enter_q/pallas_call | solution.py:197
  52.1 3.1 %enter_q.3 = bf16[8,2,160,128]{3,2,1,0:T(8,128)(2,1)} custom-call(s32[5]{0:T(128)} %stack.23.refs_0_.place_ref, f32[1,128]{1,0:T(1,128)} %constant.24.clone.refs_1_, bf16[160,24,128]{2,1,0:T(8,128)(2,1)} %refs_2_.4), custom_call_target="tpu_custom_call" | custom-call | tf_op jit(solution)/shard_map/enter_q/pallas_call | solution.py:197
  55.3 22.8 %collective-permute-done.5.in2 = bf16[8,1,2,128,128]{4,3,2,1,0:T(8,128)(2,1)S(1)} collective-permute-done((bf16[8,1,2,128,128]{4,3,2,1,0:T(8,128)(2,1)}, bf16[8,1,2,128,128]{4,3,2,1,0:T(8,128)(2,1)S(1)}, u32[]{:S(2)}, u32[]{:S(2)}) %collective-permute-start.5) | collective-permute-done | bytes 524320 | tf_op jit(solution)/shard_map/ppermute | solution.py:491
  81.8 5.5 %all-to-all-start.2 = ((bf16[8,1,160,128]{3,2,1,0:T(8,128)(2,1)}), bf16[8,1,160,128]{3,2,1,0:T(8,128)(2,1)S(1)}, u32[]{:S(2)}, u32[]{:S(2)}) async-start(bf16[8,1,160,128]{3,2,1,0:T(8,128)(2,1)} %enter_q.2), calls=%async_computation.2 | async-start | bytes 655360 | tf_op jit(solution)/shard_map/all_to_all | solution.py:502
  87.3 5.6 %pack.3 = (bf16[8,2,2,128,128]{4,3,2,1,0:T(8,128)(2,1)}, bf16[12,2,2,128,128]{4,3,2,1,0:T(8,128)(2,1)}, bf16[8,2,2,128,128]{4,3,2,1,0:T(8,128)(2,1)}, bf16[12,2,2,128,128]{4,3,2,1,0:T(8,128)(2,1)}) custom-call(s32[5]{0:T(128)} %stack.23.refs_0_.place_ref, s32[4,128]{1,0:T(4,128)} %copy-done.12, s32[4,128]{1,0:T(4,128)} %copy-done.11, s32[4,128]{1,0:T(4,128)} %copy-done.10, ...), custom_call_target="tpu_custom_call" | custom-call | tf_op jit(solution)/shard_map/pack/pallas_call | solution.py:233
  97.0 3.3 %collective-permute-start.9 = (bf16[8,2,2,128,128]{4,3,2,1,0:T(8,128)(2,1)}, bf16[8,2,2,128,128]{4,3,2,1,0:T(8,128)(2,1)}, u32[]{:S(2)}, u32[]{:S(2)}) collective-permute-start(bf16[8,2,2,128,128]{4,3,2,1,0:T(8,128)(2,1)} %get-tuple-element.95), channel_id=1, source_target_pairs={{0,32},{32,64},{64,96},{56,24},{88,56},{120,88},{1,33},{33,65},{65... | collective-permute-start | bytes 3145736 | tf_op jit(solution)/shard_map/ppermute | solution.py:506
  100.4 3.7 %all-to-all-start.4 = ((bf16[8,2,160,128]{3,2,1,0:T(8,128)(2,1)}), bf16[8,2,160,128]{3,2,1,0:T(8,128)(2,1)S(1)}, u32[]{:S(2)}, u32[]{:S(2)}) async-start(bf16[8,2,160,128]{3,2,1,0:T(8,128)(2,1)} %enter_q.3), calls=%async_computation.4 | async-start | bytes 1310720 | tf_op jit(solution)/shard_map/all_to_all | solution.py:502
  104.1 12.4 %near.2 = (f32[1,1280,128]{2,1,0:T(8,128)}, f32[1,1280,128]{2,1,0:T(8,128)}, f32[1,1280,128]{2,1,0:T(8,128)}) custom-call(s32[5]{0:T(128)} %stack.23.refs_0_.place_ref, s32[16]{0:T(128)} %get-tuple-element.85.plane_ref, bf16[8,1,160,128]{3,2,1,0:T(8,128)(2,1)} %copy-done.4, bf16[2,8,1,2,160,128]{5,4,3,2,1,0:T(8,128)(2,1)} %bitcast.16, ...), custom_call_target="tpu_custom_call" | custom-call | tf_op jit(solution)/shard_map/near/pallas_call | solution.py:345
  116.6 8.5 %beside.2 = (f32[1,1280,128]{2,1,0:T(8,128)}, f32[1,1280,128]{2,1,0:T(8,128)}, f32[1,1280,128]{2,1,0:T(8,128)}) custom-call(s32[5]{0:T(128)} %stack.23.refs_0_.place_ref, s32[64]{0:T(128)} %get-tuple-element.56.qslot_ref, bf16[8,1,160,128]{3,2,1,0:T(8,128)(2,1)} %copy-done.4, bf16[8,1,2,128,128]{4,3,2,1,0:T(8,128)(2,1)} %copy-done.8, ...), custom_call_target="tpu_custom_call" | custom-call | tf_op jit(solution)/shard_map/beside/pallas_call | solution.py:412
  125.0 3.4 %across.2 = bf16[8,1,160,128]{3,2,1,0:T(8,128)(2,1)} custom-call(s32[5]{0:T(128)} %stack.23.refs_0_.place_ref, s32[64]{0:T(128)} %get-tuple-element.56.qslot_ref, bf16[8,1,160,128]{3,2,1,0:T(8,128)(2,1)} %copy-done.4, f32[1,1280,128]{2,1,0:T(8,128)} %get-tuple-element.89.acc_in, f32[1,1280,128]{2,1,0:T(8,128)} %get-tuple-element.90.m_in, ...), custom_call_target="tpu_custom_call" | custom-call | tf_op jit(solution)/shard_map/across/pallas_call | solution.py:438
  128.5 5.7 %all-to-all-start.3 = ((bf16[8,1,160,128]{3,2,1,0:T(8,128)(2,1)}), bf16[8,1,160,128]{3,2,1,0:T(8,128)(2,1)S(1)}, u32[]{:S(2)}, u32[]{:S(2)}) async-start(bf16[8,1,160,128]{3,2,1,0:T(8,128)(2,1)} %across.2), calls=%async_computation.3 | async-start | bytes 655360 | tf_op jit(solution)/shard_map/all_to_all | solution.py:502
  134.2 22.0 %near.3 = (f32[2,1280,128]{2,1,0:T(8,128)}, f32[2,1280,128]{2,1,0:T(8,128)}, f32[2,1280,128]{2,1,0:T(8,128)}) custom-call(s32[5]{0:T(128)} %stack.23.refs_0_.place_ref, s32[16]{0:T(128)} %get-tuple-element.85.plane_ref, bf16[8,2,160,128]{3,2,1,0:T(8,128)(2,1)} %copy-done.2, bf16[2,8,2,2,160,128]{5,4,3,2,1,0:T(8,128)(2,1)} %bitcast.13, ...), custom_call_target="tpu_custom_call" | custom-call | tf_op jit(solution)/shard_map/near/pallas_call | solution.py:345
  157.5 13.8 %beside.3 = (f32[2,1280,128]{2,1,0:T(8,128)}, f32[2,1280,128]{2,1,0:T(8,128)}, f32[2,1280,128]{2,1,0:T(8,128)}) custom-call(s32[5]{0:T(128)} %stack.23.refs_0_.place_ref, s32[64]{0:T(128)} %get-tuple-element.56.qslot_ref, bf16[8,2,160,128]{3,2,1,0:T(8,128)(2,1)} %copy-done.2, bf16[8,2,2,128,128]{4,3,2,1,0:T(8,128)(2,1)} %collective-permute-done.9.big_ref, ...), custom_call_target="tpu_custom_call" | custom-call | tf_op jit(solution)/shard_map/beside/pallas_call | solution.py:412
  171.3 4.5 %across.3 = bf16[8,2,160,128]{3,2,1,0:T(8,128)(2,1)} custom-call(s32[5]{0:T(128)} %stack.23.refs_0_.place_ref, s32[64]{0:T(128)} %get-tuple-element.56.qslot_ref, bf16[8,2,160,128]{3,2,1,0:T(8,128)(2,1)} %copy-done.2, f32[2,1280,128]{2,1,0:T(8,128)} %get-tuple-element.101.acc_in, f32[2,1280,128]{2,1,0:T(8,128)} %get-tuple-element.102.m_in, ...), custom_call_target="tpu_custom_call" | custom-call | tf_op jit(solution)/shard_map/across/pallas_call | solution.py:438
  175.8 15.2 %all_to_all.30.refs_1_ = bf16[8,2,160,128]{3,2,1,0:T(8,128)(2,1)} all-to-all(bf16[8,2,160,128]{3,2,1,0:T(8,128)(2,1)} %across.3), channel_id=1, replica_groups=mesh['z'=4,'yh'=2,'c'=2,'head'=8] {'head'}, dimensions={0} | all-to-all | bytes 1310720 | tf_op jit(solution)/shard_map/all_to_all | solution.py:502
  (54 shorter events, 22.6 us)
Async XLA Ops:
  4.2 27.9 %all-to-all-start = ((bf16[16,1,2,160,128]{4,3,2,1,0:T(8,128)(2,1)}), bf16[16,1,2,160,128]{4,3,2,1,0:T(8,128)(2,1)S(1)}, u32[]{:S(2)}, u32[]{:S(2)}) async-start(bf16[16,1,2,160,128]{4,3,2,1,0:T(8,128)(2,1)} %bitcast.18), calls=%async_computation | async-start | bytes 2621440 | tf_op jit(solution)/shard_map/all_to_all | solution.py:495
  15.5 10.0 %collective-permute-start.2 = (s32[4,128]{1,0:T(4,128)}, s32[4,128]{1,0:T(4,128)S(1)}, u32[]{:S(2)}, u32[]{:S(2)}) collective-permute-start(s32[4,128]{1,0:T(4,128)} %get-tuple-element.60), channel_id=1, source_target_pairs={{0,32},{32,64},{64,96},{96,0},{1,33},{33,65},{65,97},{97,1},{2,34}... | collective-permute-start | bytes 6152 | tf_op jit(solution)/shard_map/ppermute | solution.py:491
  17.5 8.1 %collective-permute-start.1 = (s32[4,128]{1,0:T(4,128)}, s32[4,128]{1,0:T(4,128)S(1)}, u32[]{:S(2)}, u32[]{:S(2)}) collective-permute-start(s32[4,128]{1,0:T(4,128)} %get-tuple-element.60), channel_id=1, source_target_pairs={{0,64},{32,96},{64,0},{96,32},{1,65},{33,97},{65,1},{97,33},{2,66}... | collective-permute-start | bytes 6152 | tf_op jit(solution)/shard_map/ppermute | solution.py:491
  18.7 6.9 %collective-permute-start = (s32[4,128]{1,0:T(4,128)}, s32[4,128]{1,0:T(4,128)S(1)}, u32[]{:S(2)}, u32[]{:S(2)}) collective-permute-start(s32[4,128]{1,0:T(4,128)} %get-tuple-element.60), channel_id=1, source_target_pairs={{0,96},{32,0},{64,32},{96,64},{1,97},{33,1},{65,33},{97,65},{2,98}... | collective-permute-start | bytes 6152 | tf_op jit(solution)/shard_map/ppermute | solution.py:491
  25.6 7.6 %copy-start.10 = (s32[4,128]{1,0:T(4,128)}, s32[4,128]{1,0:T(4,128)S(1)}, u32[]{:S(2)}) copy-start(s32[4,128]{1,0:T(4,128)S(1)} %collective-permute-done.2.ask3) | copy-start | bytes 6148
  25.6 14.6 %copy-start.11 = (s32[4,128]{1,0:T(4,128)}, s32[4,128]{1,0:T(4,128)S(1)}, u32[]{:S(2)}) copy-start(s32[4,128]{1,0:T(4,128)S(1)} %collective-permute-done.1.ask2) | copy-start | bytes 6148
  25.6 14.6 %copy-start.12 = (s32[4,128]{1,0:T(4,128)}, s32[4,128]{1,0:T(4,128)S(1)}, u32[]{:S(2)}) copy-start(s32[4,128]{1,0:T(4,128)S(1)} %collective-permute-done.ask1) | copy-start | bytes 6148
  33.1 46.7 %all-to-all-start.1 = ((bf16[16,2,2,160,128]{4,3,2,1,0:T(8,128)(2,1)}), bf16[16,2,2,160,128]{4,3,2,1,0:T(8,128)(2,1)S(1)}, u32[]{:S(2)}, u32[]{:S(2)}) async-start(bf16[16,2,2,160,128]{4,3,2,1,0:T(8,128)(2,1)} %bitcast.17), calls=%async_computation.1 | async-start | bytes 5242880 | tf_op jit(solution)/shard_map/all_to_all | solution.py:495
  36.9 3.3 %collective-permute-start.3 = (bf16[2,8,1,2,160,128]{5,4,3,2,1,0:T(8,128)(2,1)}, bf16[2,8,1,2,160,128]{5,4,3,2,1,0:T(8,128)(2,1)S(1)}, u32[]{:S(2)}, u32[]{:S(2)}) collective-permute-start(bf16[2,8,1,2,160,128]{5,4,3,2,1,0:T(8,128)(2,1)} %bitcast.14), channel_id=1, source_target_pairs={{0,8},{8,0},{1,9},{9,1},{2,10},{10,2},{3,11},{11,3},{4,12},{12,4},... | collective-permute-start | bytes 3932168 | tf_op jit(solution)/shard_map/ppermute | solution.py:499
  44.4 33.7 %collective-permute-start.4 = (bf16[12,1,2,128,128]{4,3,2,1,0:T(8,128)(2,1)}, bf16[12,1,2,128,128]{4,3,2,1,0:T(8,128)(2,1)S(1)}, u32[]{:S(2)}, u32[]{:S(2)}) collective-permute-start(bf16[12,1,2,128,128]{4,3,2,1,0:T(8,128)(2,1)} %get-tuple-element.71), channel_id=1, source_target_pairs={{0,32},{32,64},{64,96},{96,0},{1,33},{33,65},{65,97},{97,1},{2,34}... | collective-permute-start | bytes 2359304 | tf_op jit(solution)/shard_map/ppermute | solution.py:491
  46.3 33.5 %collective-permute-start.6 = (bf16[12,1,2,128,128]{4,3,2,1,0:T(8,128)(2,1)}, bf16[12,1,2,128,128]{4,3,2,1,0:T(8,128)(2,1)}, u32[]{:S(2)}, u32[]{:S(2)}) collective-permute-start(bf16[12,1,2,128,128]{4,3,2,1,0:T(8,128)(2,1)} %get-tuple-element.73), channel_id=1, source_target_pairs={{0,96},{32,0},{64,32},{96,64},{1,97},{33,1},{65,33},{97,65},{2,98}... | collective-permute-start | bytes 2359304 | tf_op jit(solution)/shard_map/ppermute | solution.py:491
  46.4 31.7 %collective-permute-start.5 = (bf16[8,1,2,128,128]{4,3,2,1,0:T(8,128)(2,1)}, bf16[8,1,2,128,128]{4,3,2,1,0:T(8,128)(2,1)S(1)}, u32[]{:S(2)}, u32[]{:S(2)}) collective-permute-start(bf16[8,1,2,128,128]{4,3,2,1,0:T(8,128)(2,1)} %get-tuple-element.72), channel_id=1, source_target_pairs={{0,64},{32,96},{64,0},{96,32},{1,65},{33,97},{65,1},{97,33},{2,66}... | collective-permute-start | bytes 1572872 | tf_op jit(solution)/shard_map/ppermute | solution.py:491
  79.8 7.5 %collective-permute-start.7 = (bf16[2,8,2,2,160,128]{5,4,3,2,1,0:T(8,128)(2,1)S(1)}, bf16[2,8,2,2,160,128]{5,4,3,2,1,0:T(8,128)(2,1)}, u32[]{:S(2)}, u32[]{:S(2)}) collective-permute-start(bf16[2,8,2,2,160,128]{5,4,3,2,1,0:T(8,128)(2,1)S(1)} %bitcast.11), channel_id=1, source_target_pairs={{0,8},{8,0},{1,9},{9,1},{2,10},{10,2},{3,11},{11,3},{4,12},{12,4},... | collective-permute-start | bytes 7864328 | tf_op jit(solution)/shard_map/ppermute | solution.py:499
  79.9 13.0 %collective-permute-start.8 = (bf16[8,1,2,128,128]{4,3,2,1,0:T(8,128)(2,1)}, bf16[8,1,2,128,128]{4,3,2,1,0:T(8,128)(2,1)S(1)}, u32[]{:S(2)}, u32[]{:S(2)}) collective-permute-start(bf16[8,1,2,128,128]{4,3,2,1,0:T(8,128)(2,1)} %get-tuple-element.80), channel_id=1, source_target_pairs={{0,32},{32,64},{64,96},{56,24},{88,56},{120,88},{1,33},{33,65},{65... | collective-permute-start | bytes 1572872 | tf_op jit(solution)/shard_map/ppermute | solution.py:506
  81.8 13.1 %all-to-all-start.2 = ((bf16[8,1,160,128]{3,2,1,0:T(8,128)(2,1)}), bf16[8,1,160,128]{3,2,1,0:T(8,128)(2,1)S(1)}, u32[]{:S(2)}, u32[]{:S(2)}) async-start(bf16[8,1,160,128]{3,2,1,0:T(8,128)(2,1)} %enter_q.2), calls=%async_computation.2 | async-start | bytes 655360 | tf_op jit(solution)/shard_map/all_to_all | solution.py:502
  92.9 23.7 %copy-start.8 = (bf16[8,1,2,128,128]{4,3,2,1,0:T(8,128)(2,1)}, bf16[8,1,2,128,128]{4,3,2,1,0:T(8,128)(2,1)S(1)}, u32[]{:S(2)}) copy-start(bf16[8,1,2,128,128]{4,3,2,1,0:T(8,128)(2,1)S(1)} %collective-permute-done.8.big_ref) | copy-start | bytes 1572868
  94.9 9.2 %copy-start.4 = (bf16[8,1,160,128]{3,2,1,0:T(8,128)(2,1)}, bf16[8,1,160,128]{3,2,1,0:T(8,128)(2,1)S(1)}, u32[]{:S(2)}) copy-start(bf16[8,1,160,128]{3,2,1,0:T(8,128)(2,1)S(1)} %all-to-all-done.2.q_ref) | copy-start | bytes 983044
  94.9 61.3 %collective-permute-start.10 = (bf16[12,2,2,128,128]{4,3,2,1,0:T(8,128)(2,1)}, bf16[12,2,2,128,128]{4,3,2,1,0:T(8,128)(2,1)S(1)}, u32[]{:S(2)}, u32[]{:S(2)}) collective-permute-start(bf16[12,2,2,128,128]{4,3,2,1,0:T(8,128)(2,1)} %get-tuple-element.96), channel_id=1, source_target_pairs={{0,32},{32,64},{64,96},{96,0},{1,33},{33,65},{65,97},{97,1},{2,34}... | collective-permute-start | bytes 4718600 | tf_op jit(solution)/shard_map/ppermute | solution.py:491
  96.3 59.9 %collective-permute-start.11 = (bf16[12,2,2,128,128]{4,3,2,1,0:T(8,128)(2,1)}, bf16[12,2,2,128,128]{4,3,2,1,0:T(8,128)(2,1)}, u32[]{:S(2)}, u32[]{:S(2)}) collective-permute-start(bf16[12,2,2,128,128]{4,3,2,1,0:T(8,128)(2,1)} %get-tuple-element.97), channel_id=1, source_target_pairs={{0,96},{32,0},{64,32},{96,64},{1,97},{33,1},{65,33},{97,65},{2,98}... | collective-permute-start | bytes 4718600 | tf_op jit(solution)/shard_map/ppermute | solution.py:491
  97.0 59.2 %collective-permute-start.9 = (bf16[8,2,2,128,128]{4,3,2,1,0:T(8,128)(2,1)}, bf16[8,2,2,128,128]{4,3,2,1,0:T(8,128)(2,1)}, u32[]{:S(2)}, u32[]{:S(2)}) collective-permute-start(bf16[8,2,2,128,128]{4,3,2,1,0:T(8,128)(2,1)} %get-tuple-element.95), channel_id=1, source_target_pairs={{0,32},{32,64},{64,96},{56,24},{88,56},{120,88},{1,33},{33,65},{65... | collective-permute-start | bytes 3145736 | tf_op jit(solution)/shard_map/ppermute | solution.py:506
  100.2 71.1 %collective-permute-start.12 = (bf16[8,2,2,128,128]{4,3,2,1,0:T(8,128)(2,1)}, bf16[8,2,2,128,128]{4,3,2,1,0:T(8,128)(2,1)}, u32[]{:S(2)}, u32[]{:S(2)}) collective-permute-start(bf16[8,2,2,128,128]{4,3,2,1,0:T(8,128)(2,1)} %get-tuple-element.104), channel_id=1, source_target_pairs={{0,64},{32,96},{64,0},{96,32},{1,65},{33,97},{65,1},{97,33},{2,66}... | collective-permute-start | bytes 3145736 | tf_op jit(solution)/shard_map/ppermute | solution.py:491
  100.4 28.1 %all-to-all-start.4 = ((bf16[8,2,160,128]{3,2,1,0:T(8,128)(2,1)}), bf16[8,2,160,128]{3,2,1,0:T(8,128)(2,1)S(1)}, u32[]{:S(2)}, u32[]{:S(2)}) async-start(bf16[8,2,160,128]{3,2,1,0:T(8,128)(2,1)} %enter_q.3), calls=%async_computation.4 | async-start | bytes 1310720 | tf_op jit(solution)/shard_map/all_to_all | solution.py:502
  128.5 47.3 %all-to-all-start.3 = ((bf16[8,1,160,128]{3,2,1,0:T(8,128)(2,1)}), bf16[8,1,160,128]{3,2,1,0:T(8,128)(2,1)S(1)}, u32[]{:S(2)}, u32[]{:S(2)}) async-start(bf16[8,1,160,128]{3,2,1,0:T(8,128)(2,1)} %across.2), calls=%async_computation.3 | async-start | bytes 655360 | tf_op jit(solution)/shard_map/all_to_all | solution.py:502
  175.8 15.2 %copy-start.6 = (bf16[8,1,160,128]{3,2,1,0:T(8,128)(2,1)}, bf16[8,1,160,128]{3,2,1,0:T(8,128)(2,1)S(1)}, u32[]{:S(2)}) copy-start(bf16[8,1,160,128]{3,2,1,0:T(8,128)(2,1)S(1)} %all-to-all-done.3.refs_0_) | copy-start | bytes 983044
  (7 other events, 18.3 us)

commit v5 on v4

--- a/solution.py
+++ b/solution.py
@@ -299,27 +299,37 @@
     def part(index, size):
         return pl.ds(pl.multiple_of(index * size, size), size)
 
-    third = (r > 0) & (r < PLANE - 1)
-    frames = [part(i, TOK) for i in (r, jnp.where(r == 0, 1, r - 1), jnp.where(third, r + 1, r))]
-
-    def tile(t, carry):
-        rows = part(t, QT)
-        q = qs[rows, :]
-        scored = [dot_t(q, kf[at, :]) * SCALE for at in frames]
-        scored[2] = jnp.where(third, scored[2], NONE)
-        tops = [by_lane(jnp.maximum, s) for s in scored]
-        best = jnp.max(jnp.maximum(jnp.maximum(tops[0], tops[1]), tops[2]), axis=1, keepdims=True)
-        total = mixed = 0.0
-        for s, at in zip(scored, frames, strict=True):
-            p = jnp.exp2(s - best)
-            total = total + by_lane(jnp.add, p)
-            mixed = mixed + jnp.dot(p.astype(jnp.bfloat16), vf[at, :], preferred_element_type=jnp.float32)
-        m[rows, :] = jnp.broadcast_to(best, (QT, DH))
-        l[rows, :] = total
-        acc[rows, :] = mixed
-        return carry
-
-    lax.fori_loop(0, TOK // QT, tile, jnp.int32(0))
+    def attend(frames):
+        def tile(t, carry):
+            rows = part(t, QT)
+            q = qs[rows, :]
+            scored = [dot_t(q, kf[at, :]) * SCALE for at in frames]
+            tops = [by_lane(jnp.maximum, s) for s in scored]
+            while len(tops) > 1:
+                tops = [jnp.maximum(tops[0], tops[1]), *tops[2:]]
+            best = jnp.max(tops[0], axis=1, keepdims=True)
+            total = mixed = 0.0
+            for s, at in zip(scored, frames, strict=True):
+                p = jnp.exp2(s - best)
+                total = total + by_lane(jnp.add, p)
+                mixed = mixed + jnp.dot(p.astype(jnp.bfloat16), vf[at, :], preferred_element_type=jnp.float32)
+            m[rows, :] = jnp.broadcast_to(best, (QT, DH))
+            l[rows, :] = total
+            acc[rows, :] = mixed
+            return carry
+
+        lax.fori_loop(0, TOK // QT, tile, jnp.int32(0))
+
+    inner = (r > 0) & (r < PLANE - 1)
+    last = PLANE - 1
+
+    @pl.when(inner)
+    def _():
+        attend([part(i, TOK) for i in (r, jnp.maximum(r - 1, 0), jnp.minimum(r + 1, last))])
+
+    @pl.when(jnp.logical_not(inner))
+    def _():
+        attend([part(i, TOK) for i in (r, jnp.where(r == 0, 1, last - 1))])
 
     def pair(p):
         at = part(plane_ref[2 * p + 1], BLK)

time: 196 us -> 190 us (0.969)
  Pallas kernels: 94 us -> 86.5 us
  waiting for transfers between devices: 34.6 us -> 38.1 us
    pallas_call x2, Pallas kernels: 34.4 us -> 27 us  [near(): pl.pallas_call(near_body, grid=(nh,), in_specs=[smem(), smem(), tokens, f...]
    ppermute x2, waiting for transfers between devices: 0.01 us -> 3.48 us  [send(): big = lax.ppermute(big, TM, BIG_PAIRS)]
  transfers between devices with their start and end apart: 18 -> 18, of which waited for: 4 -> 5; matrix products, arithmetic and copies ran while one was open for 0% -> 0% of each run, Pallas kernels for 45% -> 43%
where the time goes in v5:
time: 190 us; the launch traced here: 188 us
  Pallas kernels  86.5 us (46%)
  starting transfers between devices  43.9 us (23%)
  waiting for transfers between devices  38.1 us (20%)
  blocking collectives  13.7 us (7%)
  local copies, waits for them, and re-layouts  5.82 us (3%)
    pallas_call x2, Pallas kernels, near(): pl.pallas_call(near_body, grid=(nh,), in_specs=[smem(), smem(), tokens, f...  27 us
    ppermute x9, waiting for transfers between devices, around(): return lax.ppermute(x, 'z', [(i, (i + shift) % 4) for i in range(4)])  22.9 us
    pallas_call x2, Pallas kernels, beside(): pl.pallas_call(beside_body, grid=(nh,), in_specs=[smem(), smem(), tokens]...  22.3 us
    all_to_all x3, starting transfers between devices, by_head(): return lax.all_to_all(x, 'head', 0, 0, tiled=True)  14.9 us
    all_to_all x1, blocking collectives, by_head(): return lax.all_to_all(x, 'head', 0, 0, tiled=True)  13.7 us
    ppermute x9, starting transfers between devices, around(): return lax.ppermute(x, 'z', [(i, (i + shift) % 4) for i in range(4)])  12.9 us
    all_to_all x2, starting transfers between devices, entry(): lax.all_to_all(sent.reshape(16, nh, 2, CH, DH), ('yh', 'head'), 0, 0, til...  10.8 us
    pallas_call x2, Pallas kernels, pack(): pl.pallas_call(pack_body, grid=(nh, 2), in_specs=[smem()] * 4 + [whole, w...  8.6 us
  transfers between devices with their start and end apart: 18, of which 5 were waited for; matrix products, arithmetic and copies ran while one was open for 0% of the time, Pallas kernels for 43%

profile of v5, /device:TPU:32, one launch (start us, length us, event | category | flops | bytes accessed | tf_op | source)
XLA Modules:
  0.0 188.2 jit_solution(9561809015003036479)
XLA Ops:
  0.7 3.5 %enter_kv.2 = bf16[2,8,1,2,160,128]{5,4,3,2,1,0:T(8,128)(2,1)} custom-call(s32[5]{0:T(128)} %stack.23.refs_0_.place_ref, f32[1,128]{1,0:T(1,128)} %constant.24.clone.refs_1_, bf16[160,24,128]{2,1,0:T(8,128)(2,1)} %refs_2_.2, bf16[160,24,128]{2,1,0:T(8,128)(2,1)} %refs_3_.2), custom_call_target="tpu_custom_call" | custom-call | tf_op jit(solution)/shard_map/enter_kv/pallas_call | solution.py:176
  4.2 7.0 %all-to-all-start = ((bf16[16,1,2,160,128]{4,3,2,1,0:T(8,128)(2,1)}), bf16[16,1,2,160,128]{4,3,2,1,0:T(8,128)(2,1)S(1)}, u32[]{:S(2)}, u32[]{:S(2)}) async-start(bf16[16,1,2,160,128]{4,3,2,1,0:T(8,128)(2,1)} %bitcast.18), calls=%async_computation | async-start | bytes 2621440 | tf_op jit(solution)/shard_map/all_to_all | solution.py:505
  11.2 4.3 %tables.1 = (s32[4,128]{1,0:T(4,128)}, s32[64]{0:T(128)}, s32[16]{0:T(128)}) custom-call(s32[5]{0:T(128)} %stack.23.refs_0_.place_ref, s32[10,16]{1,0:T(8,128)} %list_ref, s32[10,16]{1,0:T(8,128)} %count_ref.1), custom_call_target="tpu_custom_call" | custom-call | tf_op jit(solution)/shard_map/tables/pallas_call | solution.py:123
  21.2 4.4 %enter_kv.3 = bf16[2,8,2,2,160,128]{5,4,3,2,1,0:T(8,128)(2,1)} custom-call(s32[5]{0:T(128)} %stack.23.refs_0_.place_ref, f32[1,128]{1,0:T(1,128)} %constant.24.clone.refs_1_, bf16[160,24,128]{2,1,0:T(8,128)(2,1)} %refs_2_.2, bf16[160,24,128]{2,1,0:T(8,128)(2,1)} %refs_3_.2), custom_call_target="tpu_custom_call" | custom-call | tf_op jit(solution)/shard_map/enter_kv/pallas_call | solution.py:176
  25.6 6.4 %all-to-all-done = bf16[16,1,2,160,128]{4,3,2,1,0:T(8,128)(2,1)S(1)} async-done(((bf16[16,1,2,160,128]{4,3,2,1,0:T(8,128)(2,1)}), bf16[16,1,2,160,128]{4,3,2,1,0:T(8,128)(2,1)S(1)}, u32[]{:S(2)}, u32[]{:S(2)}) %all-to-all-start) | async-done | bytes 1310752 | tf_op jit(solution)/shard_map/all_to_all | solution.py:505
  33.1 3.7 %all-to-all-start.1 = ((bf16[16,2,2,160,128]{4,3,2,1,0:T(8,128)(2,1)}), bf16[16,2,2,160,128]{4,3,2,1,0:T(8,128)(2,1)S(1)}, u32[]{:S(2)}, u32[]{:S(2)}) async-start(bf16[16,2,2,160,128]{4,3,2,1,0:T(8,128)(2,1)} %bitcast.17), calls=%async_computation.1 | async-start | bytes 5242880 | tf_op jit(solution)/shard_map/all_to_all | solution.py:505
  37.0 3.2 %collective-permute-done.3.sib_ref = bf16[2,8,1,2,160,128]{5,4,3,2,1,0:T(8,128)(2,1)S(1)} collective-permute-done((bf16[2,8,1,2,160,128]{5,4,3,2,1,0:T(8,128)(2,1)}, bf16[2,8,1,2,160,128]{5,4,3,2,1,0:T(8,128)(2,1)S(1)}, u32[]{:S(2)}, u32[]{:S(2)}) %collective-permute-start.3) | collective-permute-done | bytes 1310752 | tf_op jit(solution)/shard_map/ppermute | solution.py:509
  41.3 3.0 %pack.2 = (bf16[8,1,2,128,128]{4,3,2,1,0:T(8,128)(2,1)}, bf16[12,1,2,128,128]{4,3,2,1,0:T(8,128)(2,1)}, bf16[8,1,2,128,128]{4,3,2,1,0:T(8,128)(2,1)}, bf16[12,1,2,128,128]{4,3,2,1,0:T(8,128)(2,1)}) custom-call(s32[5]{0:T(128)} %stack.23.refs_0_.place_ref, s32[4,128]{1,0:T(4,128)} %copy-done.12, s32[4,128]{1,0:T(4,128)} %copy-done.11, s32[4,128]{1,0:T(4,128)} %copy-done.10, ...), custom_call_target="tpu_custom_call" | custom-call | tf_op jit(solution)/shard_map/pack/pallas_call | solution.py:233
  46.4 3.0 %collective-permute-start.5 = (bf16[8,1,2,128,128]{4,3,2,1,0:T(8,128)(2,1)}, bf16[8,1,2,128,128]{4,3,2,1,0:T(8,128)(2,1)S(1)}, u32[]{:S(2)}, u32[]{:S(2)}) collective-permute-start(bf16[8,1,2,128,128]{4,3,2,1,0:T(8,128)(2,1)} %get-tuple-element.72), channel_id=1, source_target_pairs={{0,64},{32,96},{64,0},{96,32},{1,65},{33,97},{65,1},{97,33},{2,66}... | collective-permute-start | bytes 1572872 | tf_op jit(solution)/shard_map/ppermute | solution.py:501
  52.1 3.1 %enter_q.3 = bf16[8,2,160,128]{3,2,1,0:T(8,128)(2,1)} custom-call(s32[5]{0:T(128)} %stack.23.refs_0_.place_ref, f32[1,128]{1,0:T(1,128)} %constant.24.clone.refs_1_, bf16[160,24,128]{2,1,0:T(8,128)(2,1)} %refs_2_.4), custom_call_target="tpu_custom_call" | custom-call | tf_op jit(solution)/shard_map/enter_q/pallas_call | solution.py:197
  55.3 22.8 %collective-permute-done.5.in2 = bf16[8,1,2,128,128]{4,3,2,1,0:T(8,128)(2,1)S(1)} collective-permute-done((bf16[8,1,2,128,128]{4,3,2,1,0:T(8,128)(2,1)}, bf16[8,1,2,128,128]{4,3,2,1,0:T(8,128)(2,1)S(1)}, u32[]{:S(2)}, u32[]{:S(2)}) %collective-permute-start.5) | collective-permute-done | bytes 524320 | tf_op jit(solution)/shard_map/ppermute | solution.py:501
  81.8 5.5 %all-to-all-start.2 = ((bf16[8,1,160,128]{3,2,1,0:T(8,128)(2,1)}), bf16[8,1,160,128]{3,2,1,0:T(8,128)(2,1)S(1)}, u32[]{:S(2)}, u32[]{:S(2)}) async-start(bf16[8,1,160,128]{3,2,1,0:T(8,128)(2,1)} %enter_q.2), calls=%async_computation.2 | async-start | bytes 655360 | tf_op jit(solution)/shard_map/all_to_all | solution.py:512
  87.3 5.6 %pack.3 = (bf16[8,2,2,128,128]{4,3,2,1,0:T(8,128)(2,1)}, bf16[12,2,2,128,128]{4,3,2,1,0:T(8,128)(2,1)}, bf16[8,2,2,128,128]{4,3,2,1,0:T(8,128)(2,1)}, bf16[12,2,2,128,128]{4,3,2,1,0:T(8,128)(2,1)}) custom-call(s32[5]{0:T(128)} %stack.23.refs_0_.place_ref, s32[4,128]{1,0:T(4,128)} %copy-done.12, s32[4,128]{1,0:T(4,128)} %copy-done.11, s32[4,128]{1,0:T(4,128)} %copy-done.10, ...), custom_call_target="tpu_custom_call" | custom-call | tf_op jit(solution)/shard_map/pack/pallas_call | solution.py:233
  97.0 3.3 %collective-permute-start.9 = (bf16[8,2,2,128,128]{4,3,2,1,0:T(8,128)(2,1)}, bf16[8,2,2,128,128]{4,3,2,1,0:T(8,128)(2,1)}, u32[]{:S(2)}, u32[]{:S(2)}) collective-permute-start(bf16[8,2,2,128,128]{4,3,2,1,0:T(8,128)(2,1)} %get-tuple-element.95), channel_id=1, source_target_pairs={{0,32},{32,64},{64,96},{56,24},{88,56},{120,88},{1,33},{33,65},{65... | collective-permute-start | bytes 3145736 | tf_op jit(solution)/shard_map/ppermute | solution.py:516
  100.4 3.7 %all-to-all-start.4 = ((bf16[8,2,160,128]{3,2,1,0:T(8,128)(2,1)}), bf16[8,2,160,128]{3,2,1,0:T(8,128)(2,1)S(1)}, u32[]{:S(2)}, u32[]{:S(2)}) async-start(bf16[8,2,160,128]{3,2,1,0:T(8,128)(2,1)} %enter_q.3), calls=%async_computation.4 | async-start | bytes 1310720 | tf_op jit(solution)/shard_map/all_to_all | solution.py:512
  104.1 10.1 %near.2 = (f32[1,1280,128]{2,1,0:T(8,128)}, f32[1,1280,128]{2,1,0:T(8,128)}, f32[1,1280,128]{2,1,0:T(8,128)}) custom-call(s32[5]{0:T(128)} %stack.23.refs_0_.place_ref, s32[16]{0:T(128)} %get-tuple-element.85.plane_ref, bf16[8,1,160,128]{3,2,1,0:T(8,128)(2,1)} %copy-done.4, bf16[2,8,1,2,160,128]{5,4,3,2,1,0:T(8,128)(2,1)} %bitcast.16, ...), custom_call_target="tpu_custom_call" | custom-call | tf_op jit(solution)/shard_map/near/pallas_call | solution.py:355
  114.2 8.5 %beside.2 = (f32[1,1280,128]{2,1,0:T(8,128)}, f32[1,1280,128]{2,1,0:T(8,128)}, f32[1,1280,128]{2,1,0:T(8,128)}) custom-call(s32[5]{0:T(128)} %stack.23.refs_0_.place_ref, s32[64]{0:T(128)} %get-tuple-element.56.qslot_ref, bf16[8,1,160,128]{3,2,1,0:T(8,128)(2,1)} %copy-done.4, bf16[8,1,2,128,128]{4,3,2,1,0:T(8,128)(2,1)} %copy-done.8, ...), custom_call_target="tpu_custom_call" | custom-call | tf_op jit(solution)/shard_map/beside/pallas_call | solution.py:422
  122.7 3.4 %across.2 = bf16[8,1,160,128]{3,2,1,0:T(8,128)(2,1)} custom-call(s32[5]{0:T(128)} %stack.23.refs_0_.place_ref, s32[64]{0:T(128)} %get-tuple-element.56.qslot_ref, bf16[8,1,160,128]{3,2,1,0:T(8,128)(2,1)} %copy-done.4, f32[1,1280,128]{2,1,0:T(8,128)} %get-tuple-element.89.acc_in, f32[1,1280,128]{2,1,0:T(8,128)} %get-tuple-element.90.m_in, ...), custom_call_target="tpu_custom_call" | custom-call | tf_op jit(solution)/shard_map/across/pallas_call | solution.py:448
  126.1 5.7 %all-to-all-start.3 = ((bf16[8,1,160,128]{3,2,1,0:T(8,128)(2,1)}), bf16[8,1,160,128]{3,2,1,0:T(8,128)(2,1)S(1)}, u32[]{:S(2)}, u32[]{:S(2)}) async-start(bf16[8,1,160,128]{3,2,1,0:T(8,128)(2,1)} %across.2), calls=%async_computation.3 | async-start | bytes 655360 | tf_op jit(solution)/shard_map/all_to_all | solution.py:512
  131.8 16.9 %near.3 = (f32[2,1280,128]{2,1,0:T(8,128)}, f32[2,1280,128]{2,1,0:T(8,128)}, f32[2,1280,128]{2,1,0:T(8,128)}) custom-call(s32[5]{0:T(128)} %stack.23.refs_0_.place_ref, s32[16]{0:T(128)} %get-tuple-element.85.plane_ref, bf16[8,2,160,128]{3,2,1,0:T(8,128)(2,1)} %copy-done.2, bf16[2,8,2,2,160,128]{5,4,3,2,1,0:T(8,128)(2,1)} %bitcast.13, ...), custom_call_target="tpu_custom_call" | custom-call | tf_op jit(solution)/shard_map/near/pallas_call | solution.py:355
  148.7 3.5 %collective-permute-done.9.big_ref = bf16[8,2,2,128,128]{4,3,2,1,0:T(8,128)(2,1)} collective-permute-done((bf16[8,2,2,128,128]{4,3,2,1,0:T(8,128)(2,1)}, bf16[8,2,2,128,128]{4,3,2,1,0:T(8,128)(2,1)}, u32[]{:S(2)}, u32[]{:S(2)}) %collective-permute-start.9) | collective-permute-done | bytes 1048608 | tf_op jit(solution)/shard_map/ppermute | solution.py:516
  153.5 13.8 %beside.3 = (f32[2,1280,128]{2,1,0:T(8,128)}, f32[2,1280,128]{2,1,0:T(8,128)}, f32[2,1280,128]{2,1,0:T(8,128)}) custom-call(s32[5]{0:T(128)} %stack.23.refs_0_.place_ref, s32[64]{0:T(128)} %get-tuple-element.56.qslot_ref, bf16[8,2,160,128]{3,2,1,0:T(8,128)(2,1)} %copy-done.2, bf16[8,2,2,128,128]{4,3,2,1,0:T(8,128)(2,1)} %collective-permute-done.9.big_ref, ...), custom_call_target="tpu_custom_call" | custom-call | tf_op jit(solution)/shard_map/beside/pallas_call | solution.py:422
  167.3 4.5 %across.3 = bf16[8,2,160,128]{3,2,1,0:T(8,128)(2,1)} custom-call(s32[5]{0:T(128)} %stack.23.refs_0_.place_ref, s32[64]{0:T(128)} %get-tuple-element.56.qslot_ref, bf16[8,2,160,128]{3,2,1,0:T(8,128)(2,1)} %copy-done.2, f32[2,1280,128]{2,1,0:T(8,128)} %get-tuple-element.101.acc_in, f32[2,1280,128]{2,1,0:T(8,128)} %get-tuple-element.102.m_in, ...), custom_call_target="tpu_custom_call" | custom-call | tf_op jit(solution)/shard_map/across/pallas_call | solution.py:448
  171.8 13.7 %all_to_all.30.refs_1_ = bf16[8,2,160,128]{3,2,1,0:T(8,128)(2,1)} all-to-all(bf16[8,2,160,128]{3,2,1,0:T(8,128)(2,1)} %across.3), channel_id=1, replica_groups=mesh['z'=4,'yh'=2,'c'=2,'head'=8] {'head'}, dimensions={0} | all-to-all | bytes 1310720 | tf_op jit(solution)/shard_map/all_to_all | solution.py:512
  (54 shorter events, 25.4 us)
Async XLA Ops:
  4.2 27.9 %all-to-all-start = ((bf16[16,1,2,160,128]{4,3,2,1,0:T(8,128)(2,1)}), bf16[16,1,2,160,128]{4,3,2,1,0:T(8,128)(2,1)S(1)}, u32[]{:S(2)}, u32[]{:S(2)}) async-start(bf16[16,1,2,160,128]{4,3,2,1,0:T(8,128)(2,1)} %bitcast.18), calls=%async_computation | async-start | bytes 2621440 | tf_op jit(solution)/shard_map/all_to_all | solution.py:505
  15.5 10.0 %collective-permute-start.2 = (s32[4,128]{1,0:T(4,128)}, s32[4,128]{1,0:T(4,128)S(1)}, u32[]{:S(2)}, u32[]{:S(2)}) collective-permute-start(s32[4,128]{1,0:T(4,128)} %get-tuple-element.60), channel_id=1, source_target_pairs={{0,32},{32,64},{64,96},{96,0},{1,33},{33,65},{65,97},{97,1},{2,34}... | collective-permute-start | bytes 6152 | tf_op jit(solution)/shard_map/ppermute | solution.py:501
  17.5 8.1 %collective-permute-start.1 = (s32[4,128]{1,0:T(4,128)}, s32[4,128]{1,0:T(4,128)S(1)}, u32[]{:S(2)}, u32[]{:S(2)}) collective-permute-start(s32[4,128]{1,0:T(4,128)} %get-tuple-element.60), channel_id=1, source_target_pairs={{0,64},{32,96},{64,0},{96,32},{1,65},{33,97},{65,1},{97,33},{2,66}... | collective-permute-start | bytes 6152 | tf_op jit(solution)/shard_map/ppermute | solution.py:501
  18.7 6.9 %collective-permute-start = (s32[4,128]{1,0:T(4,128)}, s32[4,128]{1,0:T(4,128)S(1)}, u32[]{:S(2)}, u32[]{:S(2)}) collective-permute-start(s32[4,128]{1,0:T(4,128)} %get-tuple-element.60), channel_id=1, source_target_pairs={{0,96},{32,0},{64,32},{96,64},{1,97},{33,1},{65,33},{97,65},{2,98}... | collective-permute-start | bytes 6152 | tf_op jit(solution)/shard_map/ppermute | solution.py:501
  25.6 7.6 %copy-start.10 = (s32[4,128]{1,0:T(4,128)}, s32[4,128]{1,0:T(4,128)S(1)}, u32[]{:S(2)}) copy-start(s32[4,128]{1,0:T(4,128)S(1)} %collective-permute-done.2.ask3) | copy-start | bytes 6148
  25.6 14.6 %copy-start.11 = (s32[4,128]{1,0:T(4,128)}, s32[4,128]{1,0:T(4,128)S(1)}, u32[]{:S(2)}) copy-start(s32[4,128]{1,0:T(4,128)S(1)} %collective-permute-done.1.ask2) | copy-start | bytes 6148
  25.6 14.6 %copy-start.12 = (s32[4,128]{1,0:T(4,128)}, s32[4,128]{1,0:T(4,128)S(1)}, u32[]{:S(2)}) copy-start(s32[4,128]{1,0:T(4,128)S(1)} %collective-permute-done.ask1) | copy-start | bytes 6148
  33.1 46.7 %all-to-all-start.1 = ((bf16[16,2,2,160,128]{4,3,2,1,0:T(8,128)(2,1)}), bf16[16,2,2,160,128]{4,3,2,1,0:T(8,128)(2,1)S(1)}, u32[]{:S(2)}, u32[]{:S(2)}) async-start(bf16[16,2,2,160,128]{4,3,2,1,0:T(8,128)(2,1)} %bitcast.17), calls=%async_computation.1 | async-start | bytes 5242880 | tf_op jit(solution)/shard_map/all_to_all | solution.py:505
  36.9 3.3 %collective-permute-start.3 = (bf16[2,8,1,2,160,128]{5,4,3,2,1,0:T(8,128)(2,1)}, bf16[2,8,1,2,160,128]{5,4,3,2,1,0:T(8,128)(2,1)S(1)}, u32[]{:S(2)}, u32[]{:S(2)}) collective-permute-start(bf16[2,8,1,2,160,128]{5,4,3,2,1,0:T(8,128)(2,1)} %bitcast.14), channel_id=1, source_target_pairs={{0,8},{8,0},{1,9},{9,1},{2,10},{10,2},{3,11},{11,3},{4,12},{12,4},... | collective-permute-start | bytes 3932168 | tf_op jit(solution)/shard_map/ppermute | solution.py:509
  44.4 33.7 %collective-permute-start.4 = (bf16[12,1,2,128,128]{4,3,2,1,0:T(8,128)(2,1)}, bf16[12,1,2,128,128]{4,3,2,1,0:T(8,128)(2,1)S(1)}, u32[]{:S(2)}, u32[]{:S(2)}) collective-permute-start(bf16[12,1,2,128,128]{4,3,2,1,0:T(8,128)(2,1)} %get-tuple-element.71), channel_id=1, source_target_pairs={{0,32},{32,64},{64,96},{96,0},{1,33},{33,65},{65,97},{97,1},{2,34}... | collective-permute-start | bytes 2359304 | tf_op jit(solution)/shard_map/ppermute | solution.py:501
  46.3 33.5 %collective-permute-start.6 = (bf16[12,1,2,128,128]{4,3,2,1,0:T(8,128)(2,1)}, bf16[12,1,2,128,128]{4,3,2,1,0:T(8,128)(2,1)}, u32[]{:S(2)}, u32[]{:S(2)}) collective-permute-start(bf16[12,1,2,128,128]{4,3,2,1,0:T(8,128)(2,1)} %get-tuple-element.73), channel_id=1, source_target_pairs={{0,96},{32,0},{64,32},{96,64},{1,97},{33,1},{65,33},{97,65},{2,98}... | collective-permute-start | bytes 2359304 | tf_op jit(solution)/shard_map/ppermute | solution.py:501
  46.4 31.7 %collective-permute-start.5 = (bf16[8,1,2,128,128]{4,3,2,1,0:T(8,128)(2,1)}, bf16[8,1,2,128,128]{4,3,2,1,0:T(8,128)(2,1)S(1)}, u32[]{:S(2)}, u32[]{:S(2)}) collective-permute-start(bf16[8,1,2,128,128]{4,3,2,1,0:T(8,128)(2,1)} %get-tuple-element.72), channel_id=1, source_target_pairs={{0,64},{32,96},{64,0},{96,32},{1,65},{33,97},{65,1},{97,33},{2,66}... | collective-permute-start | bytes 1572872 | tf_op jit(solution)/shard_map/ppermute | solution.py:501
  79.8 7.5 %collective-permute-start.7 = (bf16[2,8,2,2,160,128]{5,4,3,2,1,0:T(8,128)(2,1)S(1)}, bf16[2,8,2,2,160,128]{5,4,3,2,1,0:T(8,128)(2,1)}, u32[]{:S(2)}, u32[]{:S(2)}) collective-permute-start(bf16[2,8,2,2,160,128]{5,4,3,2,1,0:T(8,128)(2,1)S(1)} %bitcast.11), channel_id=1, source_target_pairs={{0,8},{8,0},{1,9},{9,1},{2,10},{10,2},{3,11},{11,3},{4,12},{12,4},... | collective-permute-start | bytes 7864328 | tf_op jit(solution)/shard_map/ppermute | solution.py:509
  79.9 13.0 %collective-permute-start.8 = (bf16[8,1,2,128,128]{4,3,2,1,0:T(8,128)(2,1)}, bf16[8,1,2,128,128]{4,3,2,1,0:T(8,128)(2,1)S(1)}, u32[]{:S(2)}, u32[]{:S(2)}) collective-permute-start(bf16[8,1,2,128,128]{4,3,2,1,0:T(8,128)(2,1)} %get-tuple-element.80), channel_id=1, source_target_pairs={{0,32},{32,64},{64,96},{56,24},{88,56},{120,88},{1,33},{33,65},{65... | collective-permute-start | bytes 1572872 | tf_op jit(solution)/shard_map/ppermute | solution.py:516
  81.8 13.1 %all-to-all-start.2 = ((bf16[8,1,160,128]{3,2,1,0:T(8,128)(2,1)}), bf16[8,1,160,128]{3,2,1,0:T(8,128)(2,1)S(1)}, u32[]{:S(2)}, u32[]{:S(2)}) async-start(bf16[8,1,160,128]{3,2,1,0:T(8,128)(2,1)} %enter_q.2), calls=%async_computation.2 | async-start | bytes 655360 | tf_op jit(solution)/shard_map/all_to_all | solution.py:512
  92.9 21.3 %copy-start.8 = (bf16[8,1,2,128,128]{4,3,2,1,0:T(8,128)(2,1)}, bf16[8,1,2,128,128]{4,3,2,1,0:T(8,128)(2,1)S(1)}, u32[]{:S(2)}) copy-start(bf16[8,1,2,128,128]{4,3,2,1,0:T(8,128)(2,1)S(1)} %collective-permute-done.8.big_ref) | copy-start | bytes 1572868
  94.9 9.2 %copy-start.4 = (bf16[8,1,160,128]{3,2,1,0:T(8,128)(2,1)}, bf16[8,1,160,128]{3,2,1,0:T(8,128)(2,1)S(1)}, u32[]{:S(2)}) copy-start(bf16[8,1,160,128]{3,2,1,0:T(8,128)(2,1)S(1)} %all-to-all-done.2.q_ref) | copy-start | bytes 983044
  94.9 57.3 %collective-permute-start.10 = (bf16[12,2,2,128,128]{4,3,2,1,0:T(8,128)(2,1)}, bf16[12,2,2,128,128]{4,3,2,1,0:T(8,128)(2,1)S(1)}, u32[]{:S(2)}, u32[]{:S(2)}) collective-permute-start(bf16[12,2,2,128,128]{4,3,2,1,0:T(8,128)(2,1)} %get-tuple-element.96), channel_id=1, source_target_pairs={{0,32},{32,64},{64,96},{96,0},{1,33},{33,65},{65,97},{97,1},{2,34}... | collective-permute-start | bytes 4718600 | tf_op jit(solution)/shard_map/ppermute | solution.py:501
  96.3 55.9 %collective-permute-start.11 = (bf16[12,2,2,128,128]{4,3,2,1,0:T(8,128)(2,1)}, bf16[12,2,2,128,128]{4,3,2,1,0:T(8,128)(2,1)}, u32[]{:S(2)}, u32[]{:S(2)}) collective-permute-start(bf16[12,2,2,128,128]{4,3,2,1,0:T(8,128)(2,1)} %get-tuple-element.97), channel_id=1, source_target_pairs={{0,96},{32,0},{64,32},{96,64},{1,97},{33,1},{65,33},{97,65},{2,98}... | collective-permute-start | bytes 4718600 | tf_op jit(solution)/shard_map/ppermute | solution.py:501
  97.0 55.3 %collective-permute-start.9 = (bf16[8,2,2,128,128]{4,3,2,1,0:T(8,128)(2,1)}, bf16[8,2,2,128,128]{4,3,2,1,0:T(8,128)(2,1)}, u32[]{:S(2)}, u32[]{:S(2)}) collective-permute-start(bf16[8,2,2,128,128]{4,3,2,1,0:T(8,128)(2,1)} %get-tuple-element.95), channel_id=1, source_target_pairs={{0,32},{32,64},{64,96},{56,24},{88,56},{120,88},{1,33},{33,65},{65... | collective-permute-start | bytes 3145736 | tf_op jit(solution)/shard_map/ppermute | solution.py:516
  100.2 67.1 %collective-permute-start.12 = (bf16[8,2,2,128,128]{4,3,2,1,0:T(8,128)(2,1)}, bf16[8,2,2,128,128]{4,3,2,1,0:T(8,128)(2,1)}, u32[]{:S(2)}, u32[]{:S(2)}) collective-permute-start(bf16[8,2,2,128,128]{4,3,2,1,0:T(8,128)(2,1)} %get-tuple-element.104), channel_id=1, source_target_pairs={{0,64},{32,96},{64,0},{96,32},{1,65},{33,97},{65,1},{97,33},{2,66}... | collective-permute-start | bytes 3145736 | tf_op jit(solution)/shard_map/ppermute | solution.py:501
  100.4 25.7 %all-to-all-start.4 = ((bf16[8,2,160,128]{3,2,1,0:T(8,128)(2,1)}), bf16[8,2,160,128]{3,2,1,0:T(8,128)(2,1)S(1)}, u32[]{:S(2)}, u32[]{:S(2)}) async-start(bf16[8,2,160,128]{3,2,1,0:T(8,128)(2,1)} %enter_q.3), calls=%async_computation.4 | async-start | bytes 1310720 | tf_op jit(solution)/shard_map/all_to_all | solution.py:512
  126.1 45.7 %all-to-all-start.3 = ((bf16[8,1,160,128]{3,2,1,0:T(8,128)(2,1)}), bf16[8,1,160,128]{3,2,1,0:T(8,128)(2,1)S(1)}, u32[]{:S(2)}, u32[]{:S(2)}) async-start(bf16[8,1,160,128]{3,2,1,0:T(8,128)(2,1)} %across.2), calls=%async_computation.3 | async-start | bytes 655360 | tf_op jit(solution)/shard_map/all_to_all | solution.py:512
  171.8 13.7 %copy-start.6 = (bf16[8,1,160,128]{3,2,1,0:T(8,128)(2,1)}, bf16[8,1,160,128]{3,2,1,0:T(8,128)(2,1)S(1)}, u32[]{:S(2)}) copy-start(bf16[8,1,160,128]{3,2,1,0:T(8,128)(2,1)S(1)} %all-to-all-done.3.refs_0_) | copy-start | bytes 983044
  (7 other events, 18.3 us)

commit v6 on v5

--- a/solution.py
+++ b/solution.py
@@ -376,9 +376,8 @@
         yield qslot_ref[zp * BESIDE + s], lambda s=s: ref[s, 0, 0], lambda s=s: ref[s, 0, 1]
 
 
-def beside_body(
-    place_ref, qslot_ref, q_ref, big_ref, in1, in3, acc_in, m_in, l_in, acc_ref, m_ref, l_ref, qs, kf, vf, top, scores
-):
+def received(place_ref, qslot_ref, q_ref, big_ref, came, acc_in, m_in, l_in, acc, m, l, qs, kf, vf, top, scores):
+    in1, in3 = came[1], came[3]
     z, r = place_ref[0], place_ref[1]
     touches = ((r == 0) & (z > 0)) | ((r == PLANE - 1) & (z < 3))
     qs[...] = q_ref[:, 0].reshape(TOK, DH)
@@ -397,19 +396,35 @@
             m_new = jnp.maximum(m_old, jnp.max(by_lane(jnp.maximum, s), axis=1, keepdims=True))
             p = jnp.exp2(s - m_new[:, :1])
             fade = jnp.exp2(m_old - m_new)
-            m_ref[0, rows] = m_new
-            l_ref[0, rows] = l_in[0, rows] * fade + by_lane(jnp.add, p)
+            m[rows] = m_new
+            l[rows] = l_in[0, rows] * fade + by_lane(jnp.add, p)
             mixed = jnp.dot(p.astype(jnp.bfloat16), vf[...], preferred_element_type=jnp.float32)
-            acc_ref[0, rows] = acc_in[0, rows] * fade + mixed
+            acc[rows] = acc_in[0, rows] * fade + mixed
 
     @pl.when(jnp.logical_not(touches))
     def _():
-        acc_ref[...] = acc_in[...]
-        m_ref[...] = m_in[...]
-        l_ref[...] = l_in[...]
-
-    pairs = [*slots(z, qslot_ref, 1, in1), *slots(z, qslot_ref, 3, in3)]
-    listed_pairs(pairs, qs, m_ref.at[0], l_ref.at[0], acc_ref.at[0], top, scores)
+        acc[...] = acc_in[0]
+        m[...] = m_in[0]
+        l[...] = l_in[0]
+
+    pairs = [pair for shift, ref in came.items() for pair in slots(z, qslot_ref, shift, ref)]
+    listed_pairs(pairs, qs, m, l, acc, top, scores)
+
+
+def beside_body(place_ref, qslot_ref, q_ref, big_ref, in1, in3, acc_in, m_in, l_in, acc_ref, m_ref, l_ref, *scratch):
+    state = (acc_ref.at[0], m_ref.at[0], l_ref.at[0])
+    received(place_ref, qslot_ref, q_ref, big_ref, {1: in1, 3: in3}, acc_in, m_in, l_in, *state, *scratch)
+
+
+def all_body(place_ref, qslot_ref, q_ref, big_ref, in1, in2, in3, acc_in, m_in, l_in, o_ref, acc, m, l, *scratch):
+    came = {1: in1, 2: in2, 3: in3}
+    received(place_ref, qslot_ref, q_ref, big_ref, came, acc_in, m_in, l_in, acc, m, l, *scratch)
+    divide(o_ref, acc, l)
+
+
+def divide(o_ref, acc, l):
+    total = jnp.sum(l[...], axis=1, keepdims=True)
+    o_ref[:, 0] = (acc[...] / total).astype(jnp.bfloat16).reshape(8, CH, DH)
 
 
 def block_specs(arrays):
@@ -438,8 +453,24 @@
     m[...] = m_in[0]
     l[...] = l_in[0]
     listed_pairs([*slots(place_ref[0], qslot_ref, 2, in2)], qs, m, l, acc, top, scores)
-    total = jnp.sum(l[...], axis=1, keepdims=True)
-    o_ref[:, 0] = (acc[...] / total).astype(jnp.bfloat16).reshape(8, CH, DH)
+    divide(o_ref, acc, l)
+
+
+def everything(place, qslot, q, state, big, in1, in2, in3):
+    nh = big.shape[1]
+    tokens, held = head_specs()
+    return pl.pallas_call(
+        all_body,
+        grid=(nh,),
+        in_specs=[smem(), smem(), tokens] + block_specs((big, in1, in2, in3)) + [held] * 3,
+        out_specs=tokens,
+        out_shape=jax.ShapeDtypeStruct((8, nh, CH, DH), jnp.bfloat16),
+        scratch_shapes=[pltpu.VMEM((TOK, DH), jnp.float32)] * 3
+        + [pltpu.VMEM((TOK, DH), jnp.bfloat16)] * 3
+        + [pltpu.VMEM((TOK, DH), jnp.float32), pltpu.VMEM((2 * BESIDE + BASE, BLK, BLK), jnp.float32)],
+        compiler_params=params(),
+        name="everything",
+    )(place, qslot, q, big, in1, in2, in3, *state)
 
 
 def across(place, qslot, q, state, in2):
@@ -531,14 +562,13 @@
     q_a, q_b = (enter_q(place, rates, query, rows) for rows in CHUNKS)
     own_b, q_a, q_b, in1_a, in2_a, in3_a = together(own_b, q_a, q_b, in1_a, in2_a, in3_a)
     sib_b = swap(own_b)
-    q_a = by_head(q_a)
     packed_b = pack(place, asked, own_b, sib_b)
     packed_b, q_a, big_a = together(packed_b, q_a, big_a)
     big_b, in1_b, in2_b, in3_b = send(packed_b)
+    q_a = by_head(q_a)
     q_b = by_head(q_b)
     state_a = near(place, plane_pairs, q_a, own_a, sib_a)
-    state_a = beside(place, qslot, q_a, big_a, in1_a, in3_a, state_a)
-    done_a = across(place, qslot, q_a, state_a, in2_a)
+    done_a = everything(place, qslot, q_a, state_a, big_a, in1_a, in2_a, in3_a)
     out_a = by_head(done_a)
     q_b, _ = together(q_b, done_a)
     state_b = near(place, plane_pairs, q_b, own_b, sib_b)

time: 190 us -> 191 us (level)
  Pallas kernels: 86.5 us -> 83.2 us
  waiting for transfers between devices: 38.1 us -> 40.9 us
    pallas_call x0 -> x1, Pallas kernels: none -> 8.74 us  [everything(): pl.pallas_call(all_body, grid=(nh,), in_specs=[smem(), smem(), tokens] +...]
    pallas_call x2 -> x1, Pallas kernels: 22.3 us -> 13.8 us  [beside(): pl.pallas_call(beside_body, grid=(nh,), in_specs=[smem(), smem(), tokens]...]
    ppermute x2, waiting for transfers between devices: 3.48 us -> 0.01 us  [send(): big = lax.ppermute(big, TM, BIG_PAIRS)]
    pallas_call x2 -> x1, Pallas kernels: 7.89 us -> 4.47 us  [across(): pl.pallas_call(across_body, grid=(nh,), in_specs=[smem(), smem(), tokens,...]
    all_to_all x3, waiting for transfers between devices: 2.05 us -> 5.42 us  [by_head(): return lax.all_to_all(x, 'head', 0, 0, tiled=True)]
    ppermute x2, waiting for transfers between devices: 3.24 us -> 6.2 us  [swap(): return lax.ppermute(x, 'c', [(0, 1), (1, 0)])]
  transfers between devices with their start and end apart: 18 -> 18, of which waited for: 5 -> 5; matrix products, arithmetic and copies ran while one was open for 0% -> 0% of each run, Pallas kernels for 43% -> 41%
where the time goes in v6:
time: 191 us; the launch traced here: 188 us
  Pallas kernels  83.2 us (44%)
  starting transfers between devices  42.5 us (22%)
  waiting for transfers between devices  40.9 us (21%)
  blocking collectives  15.2 us (8%)
  local copies, waits for them, and re-layouts  6.37 us (3%)
    pallas_call x2, Pallas kernels, near(): pl.pallas_call(near_body, grid=(nh,), in_specs=[smem(), smem(), tokens, f...  26.9 us
    ppermute x9, waiting for transfers between devices, around(): return lax.ppermute(x, 'z', [(i, (i + shift) % 4) for i in range(4)])  22.9 us
    all_to_all x1, blocking collectives, by_head(): return lax.all_to_all(x, 'head', 0, 0, tiled=True)  15.2 us
    all_to_all x3, starting transfers between devices, by_head(): return lax.all_to_all(x, 'head', 0, 0, tiled=True)  14.6 us
    pallas_call x1, Pallas kernels, beside(): pl.pallas_call(beside_body, grid=(nh,), in_specs=[smem(), smem(), tokens]...  13.8 us
    ppermute x9, starting transfers between devices, around(): return lax.ppermute(x, 'z', [(i, (i + shift) % 4) for i in range(4)])  13.1 us
    all_to_all x2, starting transfers between devices, entry(): lax.all_to_all(sent.reshape(16, nh, 2, CH, DH), ('yh', 'head'), 0, 0, til...  10.8 us
    pallas_call x1, Pallas kernels, everything(): pl.pallas_call(all_body, grid=(nh,), in_specs=[smem(), smem(), tokens] +...  8.74 us
  transfers between devices with their start and end apart: 18, of which 5 were waited for; matrix products, arithmetic and copies ran while one was open for 0% of the time, Pallas kernels for 41%

profile of v6, /device:TPU:32, one launch (start us, length us, event | category | flops | bytes accessed | tf_op | source)
XLA Modules:
  0.0 188.4 jit_solution(10829969042152484287)
XLA Ops:
  0.6 3.5 %enter_kv.2 = bf16[2,8,1,2,160,128]{5,4,3,2,1,0:T(8,128)(2,1)} custom-call(s32[5]{0:T(128)} %stack.23.refs_0_.place_ref, f32[1,128]{1,0:T(1,128)} %constant.24.clone.refs_1_, bf16[160,24,128]{2,1,0:T(8,128)(2,1)} %refs_2_.2, bf16[160,24,128]{2,1,0:T(8,128)(2,1)} %refs_3_.2), custom_call_target="tpu_custom_call" | custom-call | tf_op jit(solution)/shard_map/enter_kv/pallas_call | solution.py:176
  4.1 7.0 %all-to-all-start = ((bf16[16,1,2,160,128]{4,3,2,1,0:T(8,128)(2,1)}), bf16[16,1,2,160,128]{4,3,2,1,0:T(8,128)(2,1)S(1)}, u32[]{:S(2)}, u32[]{:S(2)}) async-start(bf16[16,1,2,160,128]{4,3,2,1,0:T(8,128)(2,1)} %bitcast.18), calls=%async_computation | async-start | bytes 2621440 | tf_op jit(solution)/shard_map/all_to_all | solution.py:536
  11.2 4.3 %tables.1 = (s32[4,128]{1,0:T(4,128)}, s32[64]{0:T(128)}, s32[16]{0:T(128)}) custom-call(s32[5]{0:T(128)} %stack.23.refs_0_.place_ref, s32[10,16]{1,0:T(8,128)} %list_ref, s32[10,16]{1,0:T(8,128)} %count_ref.1), custom_call_target="tpu_custom_call" | custom-call | tf_op jit(solution)/shard_map/tables/pallas_call | solution.py:123
  21.1 4.4 %enter_kv.3 = bf16[2,8,2,2,160,128]{5,4,3,2,1,0:T(8,128)(2,1)} custom-call(s32[5]{0:T(128)} %stack.23.refs_0_.place_ref, f32[1,128]{1,0:T(1,128)} %constant.24.clone.refs_1_, bf16[160,24,128]{2,1,0:T(8,128)(2,1)} %refs_2_.2, bf16[160,24,128]{2,1,0:T(8,128)(2,1)} %refs_3_.2), custom_call_target="tpu_custom_call" | custom-call | tf_op jit(solution)/shard_map/enter_kv/pallas_call | solution.py:176
  25.5 6.4 %all-to-all-done = bf16[16,1,2,160,128]{4,3,2,1,0:T(8,128)(2,1)S(1)} async-done(((bf16[16,1,2,160,128]{4,3,2,1,0:T(8,128)(2,1)}), bf16[16,1,2,160,128]{4,3,2,1,0:T(8,128)(2,1)S(1)}, u32[]{:S(2)}, u32[]{:S(2)}) %all-to-all-start) | async-done | bytes 1310752 | tf_op jit(solution)/shard_map/all_to_all | solution.py:536
  33.1 3.7 %all-to-all-start.1 = ((bf16[16,2,2,160,128]{4,3,2,1,0:T(8,128)(2,1)}), bf16[16,2,2,160,128]{4,3,2,1,0:T(8,128)(2,1)S(1)}, u32[]{:S(2)}, u32[]{:S(2)}) async-start(bf16[16,2,2,160,128]{4,3,2,1,0:T(8,128)(2,1)} %bitcast.17), calls=%async_computation.1 | async-start | bytes 5242880 | tf_op jit(solution)/shard_map/all_to_all | solution.py:536
  36.9 3.2 %collective-permute-done.3.sib_ref = bf16[2,8,1,2,160,128]{5,4,3,2,1,0:T(8,128)(2,1)S(1)} collective-permute-done((bf16[2,8,1,2,160,128]{5,4,3,2,1,0:T(8,128)(2,1)}, bf16[2,8,1,2,160,128]{5,4,3,2,1,0:T(8,128)(2,1)S(1)}, u32[]{:S(2)}, u32[]{:S(2)}) %collective-permute-start.3) | collective-permute-done | bytes 1310752 | tf_op jit(solution)/shard_map/ppermute | solution.py:540
  41.3 3.0 %pack.2 = (bf16[8,1,2,128,128]{4,3,2,1,0:T(8,128)(2,1)}, bf16[12,1,2,128,128]{4,3,2,1,0:T(8,128)(2,1)}, bf16[8,1,2,128,128]{4,3,2,1,0:T(8,128)(2,1)}, bf16[12,1,2,128,128]{4,3,2,1,0:T(8,128)(2,1)}) custom-call(s32[5]{0:T(128)} %stack.23.refs_0_.place_ref, s32[4,128]{1,0:T(4,128)} %copy-done.12, s32[4,128]{1,0:T(4,128)} %copy-done.11, s32[4,128]{1,0:T(4,128)} %copy-done.10, ...), custom_call_target="tpu_custom_call" | custom-call | tf_op jit(solution)/shard_map/pack/pallas_call | solution.py:233
  46.3 3.0 %collective-permute-start.5 = (bf16[8,1,2,128,128]{4,3,2,1,0:T(8,128)(2,1)}, bf16[8,1,2,128,128]{4,3,2,1,0:T(8,128)(2,1)S(1)}, u32[]{:S(2)}, u32[]{:S(2)}) collective-permute-start(bf16[8,1,2,128,128]{4,3,2,1,0:T(8,128)(2,1)} %get-tuple-element.69), channel_id=1, source_target_pairs={{0,64},{32,96},{64,0},{96,32},{1,65},{33,97},{65,1},{97,33},{2,66}... | collective-permute-start | bytes 1572872 | tf_op jit(solution)/shard_map/ppermute | solution.py:532
  49.3 2.7 %enter_q.2 = bf16[8,1,160,128]{3,2,1,0:T(8,128)(2,1)} custom-call(s32[5]{0:T(128)} %stack.23.refs_0_.place_ref, f32[1,128]{1,0:T(1,128)} %constant.24.clone.refs_1_, bf16[160,24,128]{2,1,0:T(8,128)(2,1)} %refs_2_.4), custom_call_target="tpu_custom_call" | custom-call | tf_op jit(solution)/shard_map/enter_q/pallas_call | solution.py:197
  52.0 3.1 %enter_q.3 = bf16[8,2,160,128]{3,2,1,0:T(8,128)(2,1)} custom-call(s32[5]{0:T(128)} %stack.23.refs_0_.place_ref, f32[1,128]{1,0:T(1,128)} %constant.24.clone.refs_1_, bf16[160,24,128]{2,1,0:T(8,128)(2,1)} %refs_2_.4), custom_call_target="tpu_custom_call" | custom-call | tf_op jit(solution)/shard_map/enter_q/pallas_call | solution.py:197
  55.1 22.8 %collective-permute-done.5.in2 = bf16[8,1,2,128,128]{4,3,2,1,0:T(8,128)(2,1)S(1)} collective-permute-done((bf16[8,1,2,128,128]{4,3,2,1,0:T(8,128)(2,1)}, bf16[8,1,2,128,128]{4,3,2,1,0:T(8,128)(2,1)S(1)}, u32[]{:S(2)}, u32[]{:S(2)}) %collective-permute-start.5) | collective-permute-done | bytes 524320 | tf_op jit(solution)/shard_map/ppermute | solution.py:532
  80.8 3.0 %collective-permute-done.7.sib_ref = bf16[2,8,2,2,160,128]{5,4,3,2,1,0:T(8,128)(2,1)S(1)} collective-permute-done((bf16[2,8,2,2,160,128]{5,4,3,2,1,0:T(8,128)(2,1)S(1)}, bf16[2,8,2,2,160,128]{5,4,3,2,1,0:T(8,128)(2,1)S(1)}, u32[]{:S(2)}, u32[]{:S(2)}) %collective-permute-start.7) | collective-permute-done | bytes 2621472 | tf_op jit(solution)/shard_map/ppermute | solution.py:540
  85.3 5.4 %pack.3 = (bf16[8,2,2,128,128]{4,3,2,1,0:T(8,128)(2,1)}, bf16[12,2,2,128,128]{4,3,2,1,0:T(8,128)(2,1)}, bf16[8,2,2,128,128]{4,3,2,1,0:T(8,128)(2,1)}, bf16[12,2,2,128,128]{4,3,2,1,0:T(8,128)(2,1)}) custom-call(s32[5]{0:T(128)} %stack.23.refs_0_.place_ref, s32[4,128]{1,0:T(4,128)} %copy-done.12, s32[4,128]{1,0:T(4,128)} %copy-done.11, s32[4,128]{1,0:T(4,128)} %copy-done.10, ...), custom_call_target="tpu_custom_call" | custom-call | tf_op jit(solution)/shard_map/pack/pallas_call | solution.py:233
  92.9 5.4 %all-to-all-start.2 = ((bf16[8,1,160,128]{3,2,1,0:T(8,128)(2,1)}), bf16[8,1,160,128]{3,2,1,0:T(8,128)(2,1)S(1)}, u32[]{:S(2)}, u32[]{:S(2)}) async-start(bf16[8,1,160,128]{3,2,1,0:T(8,128)(2,1)} %enter_q.2), calls=%async_computation.2 | async-start | bytes 655360 | tf_op jit(solution)/shard_map/all_to_all | solution.py:543
  100.6 5.4 %all-to-all-done.2.q_ref = bf16[8,1,160,128]{3,2,1,0:T(8,128)(2,1)S(1)} async-done(((bf16[8,1,160,128]{3,2,1,0:T(8,128)(2,1)}), bf16[8,1,160,128]{3,2,1,0:T(8,128)(2,1)S(1)}, u32[]{:S(2)}, u32[]{:S(2)}) %all-to-all-start.2) | async-done | bytes 327712 | tf_op jit(solution)/shard_map/all_to_all | solution.py:543
  106.0 3.5 %all-to-all-start.4 = ((bf16[8,2,160,128]{3,2,1,0:T(8,128)(2,1)}), bf16[8,2,160,128]{3,2,1,0:T(8,128)(2,1)S(1)}, u32[]{:S(2)}, u32[]{:S(2)}) async-start(bf16[8,2,160,128]{3,2,1,0:T(8,128)(2,1)} %enter_q.3), calls=%async_computation.4 | async-start | bytes 1310720 | tf_op jit(solution)/shard_map/all_to_all | solution.py:543
  109.6 10.0 %near.2 = (f32[1,1280,128]{2,1,0:T(8,128)}, f32[1,1280,128]{2,1,0:T(8,128)}, f32[1,1280,128]{2,1,0:T(8,128)}) custom-call(s32[5]{0:T(128)} %stack.23.refs_0_.place_ref, s32[16]{0:T(128)} %get-tuple-element.83.plane_ref, bf16[8,1,160,128]{3,2,1,0:T(8,128)(2,1)} %copy-done.5, bf16[2,8,1,2,160,128]{5,4,3,2,1,0:T(8,128)(2,1)} %bitcast.16, ...), custom_call_target="tpu_custom_call" | custom-call | tf_op jit(solution)/shard_map/near/pallas_call | solution.py:355
  119.6 8.7 %everything.1 = bf16[8,1,160,128]{3,2,1,0:T(8,128)(2,1)} custom-call(s32[5]{0:T(128)} %stack.23.refs_0_.place_ref, s32[64]{0:T(128)} %get-tuple-element.53.qslot_ref, bf16[8,1,160,128]{3,2,1,0:T(8,128)(2,1)} %copy-done.5, bf16[8,1,2,128,128]{4,3,2,1,0:T(8,128)(2,1)} %collective-permute-done.8.big_ref, bf16[12,1,2,128,128]{4,3,2,1,0:T(8,128)(2,1)} %copy-done.8, ...), custom_call_target="tpu_custom_call" | custom-call | tf_op jit(solution)/shard_map/everything/pallas_call | solution.py:462
  128.4 5.6 %all-to-all-start.3 = ((bf16[8,1,160,128]{3,2,1,0:T(8,128)(2,1)}), bf16[8,1,160,128]{3,2,1,0:T(8,128)(2,1)S(1)}, u32[]{:S(2)}, u32[]{:S(2)}) async-start(bf16[8,1,160,128]{3,2,1,0:T(8,128)(2,1)} %everything.1), calls=%async_computation.3 | async-start | bytes 655360 | tf_op jit(solution)/shard_map/all_to_all | solution.py:543
  134.0 16.9 %near.3 = (f32[2,1280,128]{2,1,0:T(8,128)}, f32[2,1280,128]{2,1,0:T(8,128)}, f32[2,1280,128]{2,1,0:T(8,128)}) custom-call(s32[5]{0:T(128)} %stack.23.refs_0_.place_ref, s32[16]{0:T(128)} %get-tuple-element.83.plane_ref, bf16[8,2,160,128]{3,2,1,0:T(8,128)(2,1)} %copy-done.2, bf16[2,8,2,2,160,128]{5,4,3,2,1,0:T(8,128)(2,1)} %bitcast.13, ...), custom_call_target="tpu_custom_call" | custom-call | tf_op jit(solution)/shard_map/near/pallas_call | solution.py:355
  152.2 13.8 %beside.1 = (f32[2,1280,128]{2,1,0:T(8,128)}, f32[2,1280,128]{2,1,0:T(8,128)}, f32[2,1280,128]{2,1,0:T(8,128)}) custom-call(s32[5]{0:T(128)} %stack.23.refs_0_.place_ref, s32[64]{0:T(128)} %get-tuple-element.53.qslot_ref, bf16[8,2,160,128]{3,2,1,0:T(8,128)(2,1)} %copy-done.2, bf16[8,2,2,128,128]{4,3,2,1,0:T(8,128)(2,1)} %collective-permute-done.9.big_ref, ...), custom_call_target="tpu_custom_call" | custom-call | tf_op jit(solution)/shard_map/beside/pallas_call | solution.py:437
  166.0 4.5 %across.1 = bf16[8,2,160,128]{3,2,1,0:T(8,128)(2,1)} custom-call(s32[5]{0:T(128)} %stack.23.refs_0_.place_ref, s32[64]{0:T(128)} %get-tuple-element.53.qslot_ref, bf16[8,2,160,128]{3,2,1,0:T(8,128)(2,1)} %copy-done.2, f32[2,1280,128]{2,1,0:T(8,128)} %get-tuple-element.95.acc_in, f32[2,1280,128]{2,1,0:T(8,128)} %get-tuple-element.96.m_in, ...), custom_call_target="tpu_custom_call" | custom-call | tf_op jit(solution)/shard_map/across/pallas_call | solution.py:479
  170.5 15.2 %all_to_all.30.refs_1_ = bf16[8,2,160,128]{3,2,1,0:T(8,128)(2,1)} all-to-all(bf16[8,2,160,128]{3,2,1,0:T(8,128)(2,1)} %across.1), channel_id=1, replica_groups=mesh['z'=4,'yh'=2,'c'=2,'head'=8] {'head'}, dimensions={0} | all-to-all | bytes 1310720 | tf_op jit(solution)/shard_map/all_to_all | solution.py:543
  (53 shorter events, 23.3 us)
Async XLA Ops:
  4.1 27.9 %all-to-all-start = ((bf16[16,1,2,160,128]{4,3,2,1,0:T(8,128)(2,1)}), bf16[16,1,2,160,128]{4,3,2,1,0:T(8,128)(2,1)S(1)}, u32[]{:S(2)}, u32[]{:S(2)}) async-start(bf16[16,1,2,160,128]{4,3,2,1,0:T(8,128)(2,1)} %bitcast.18), calls=%async_computation | async-start | bytes 2621440 | tf_op jit(solution)/shard_map/all_to_all | solution.py:536
  15.5 10.0 %collective-permute-start.2 = (s32[4,128]{1,0:T(4,128)}, s32[4,128]{1,0:T(4,128)S(1)}, u32[]{:S(2)}, u32[]{:S(2)}) collective-permute-start(s32[4,128]{1,0:T(4,128)} %get-tuple-element.57), channel_id=1, source_target_pairs={{0,32},{32,64},{64,96},{96,0},{1,33},{33,65},{65,97},{97,1},{2,34}... | collective-permute-start | bytes 6152 | tf_op jit(solution)/shard_map/ppermute | solution.py:532
  17.4 8.1 %collective-permute-start.1 = (s32[4,128]{1,0:T(4,128)}, s32[4,128]{1,0:T(4,128)S(1)}, u32[]{:S(2)}, u32[]{:S(2)}) collective-permute-start(s32[4,128]{1,0:T(4,128)} %get-tuple-element.57), channel_id=1, source_target_pairs={{0,64},{32,96},{64,0},{96,32},{1,65},{33,97},{65,1},{97,33},{2,66}... | collective-permute-start | bytes 6152 | tf_op jit(solution)/shard_map/ppermute | solution.py:532
  18.6 6.9 %collective-permute-start = (s32[4,128]{1,0:T(4,128)}, s32[4,128]{1,0:T(4,128)S(1)}, u32[]{:S(2)}, u32[]{:S(2)}) collective-permute-start(s32[4,128]{1,0:T(4,128)} %get-tuple-element.57), channel_id=1, source_target_pairs={{0,96},{32,0},{64,32},{96,64},{1,97},{33,1},{65,33},{97,65},{2,98}... | collective-permute-start | bytes 6152 | tf_op jit(solution)/shard_map/ppermute | solution.py:532
  25.5 7.6 %copy-start.10 = (s32[4,128]{1,0:T(4,128)}, s32[4,128]{1,0:T(4,128)S(1)}, u32[]{:S(2)}) copy-start(s32[4,128]{1,0:T(4,128)S(1)} %collective-permute-done.2.ask3) | copy-start | bytes 6148
  25.5 14.6 %copy-start.11 = (s32[4,128]{1,0:T(4,128)}, s32[4,128]{1,0:T(4,128)S(1)}, u32[]{:S(2)}) copy-start(s32[4,128]{1,0:T(4,128)S(1)} %collective-permute-done.1.ask2) | copy-start | bytes 6148
  25.5 14.6 %copy-start.12 = (s32[4,128]{1,0:T(4,128)}, s32[4,128]{1,0:T(4,128)S(1)}, u32[]{:S(2)}) copy-start(s32[4,128]{1,0:T(4,128)S(1)} %collective-permute-done.ask1) | copy-start | bytes 6148
  33.1 45.7 %all-to-all-start.1 = ((bf16[16,2,2,160,128]{4,3,2,1,0:T(8,128)(2,1)}), bf16[16,2,2,160,128]{4,3,2,1,0:T(8,128)(2,1)S(1)}, u32[]{:S(2)}, u32[]{:S(2)}) async-start(bf16[16,2,2,160,128]{4,3,2,1,0:T(8,128)(2,1)} %bitcast.17), calls=%async_computation.1 | async-start | bytes 5242880 | tf_op jit(solution)/shard_map/all_to_all | solution.py:536
  36.8 3.3 %collective-permute-start.3 = (bf16[2,8,1,2,160,128]{5,4,3,2,1,0:T(8,128)(2,1)}, bf16[2,8,1,2,160,128]{5,4,3,2,1,0:T(8,128)(2,1)S(1)}, u32[]{:S(2)}, u32[]{:S(2)}) collective-permute-start(bf16[2,8,1,2,160,128]{5,4,3,2,1,0:T(8,128)(2,1)} %bitcast.14), channel_id=1, source_target_pairs={{0,8},{8,0},{1,9},{9,1},{2,10},{10,2},{3,11},{11,3},{4,12},{12,4},... | collective-permute-start | bytes 3932168 | tf_op jit(solution)/shard_map/ppermute | solution.py:540
  44.2 33.7 %collective-permute-start.4 = (bf16[12,1,2,128,128]{4,3,2,1,0:T(8,128)(2,1)}, bf16[12,1,2,128,128]{4,3,2,1,0:T(8,128)(2,1)S(1)}, u32[]{:S(2)}, u32[]{:S(2)}) collective-permute-start(bf16[12,1,2,128,128]{4,3,2,1,0:T(8,128)(2,1)} %get-tuple-element.68), channel_id=1, source_target_pairs={{0,32},{32,64},{64,96},{96,0},{1,33},{33,65},{65,97},{97,1},{2,34}... | collective-permute-start | bytes 2359304 | tf_op jit(solution)/shard_map/ppermute | solution.py:532
  46.2 32.6 %collective-permute-start.6 = (bf16[12,1,2,128,128]{4,3,2,1,0:T(8,128)(2,1)}, bf16[12,1,2,128,128]{4,3,2,1,0:T(8,128)(2,1)}, u32[]{:S(2)}, u32[]{:S(2)}) collective-permute-start(bf16[12,1,2,128,128]{4,3,2,1,0:T(8,128)(2,1)} %get-tuple-element.70), channel_id=1, source_target_pairs={{0,96},{32,0},{64,32},{96,64},{1,97},{33,1},{65,33},{97,65},{2,98}... | collective-permute-start | bytes 2359304 | tf_op jit(solution)/shard_map/ppermute | solution.py:532
  46.3 31.7 %collective-permute-start.5 = (bf16[8,1,2,128,128]{4,3,2,1,0:T(8,128)(2,1)}, bf16[8,1,2,128,128]{4,3,2,1,0:T(8,128)(2,1)S(1)}, u32[]{:S(2)}, u32[]{:S(2)}) collective-permute-start(bf16[8,1,2,128,128]{4,3,2,1,0:T(8,128)(2,1)} %get-tuple-element.69), channel_id=1, source_target_pairs={{0,64},{32,96},{64,0},{96,32},{1,65},{33,97},{65,1},{97,33},{2,66}... | collective-permute-start | bytes 1572872 | tf_op jit(solution)/shard_map/ppermute | solution.py:532
  78.8 40.9 %copy-start.8 = (bf16[12,1,2,128,128]{4,3,2,1,0:T(8,128)(2,1)}, bf16[12,1,2,128,128]{4,3,2,1,0:T(8,128)(2,1)S(1)}, u32[]{:S(2)}) copy-start(bf16[12,1,2,128,128]{4,3,2,1,0:T(8,128)(2,1)S(1)} %collective-permute-done.4.in1) | copy-start | bytes 2359300
  78.8 5.0 %collective-permute-start.7 = (bf16[2,8,2,2,160,128]{5,4,3,2,1,0:T(8,128)(2,1)S(1)}, bf16[2,8,2,2,160,128]{5,4,3,2,1,0:T(8,128)(2,1)S(1)}, u32[]{:S(2)}, u32[]{:S(2)}) collective-permute-start(bf16[2,8,2,2,160,128]{5,4,3,2,1,0:T(8,128)(2,1)S(1)} %bitcast.11), channel_id=1, source_target_pairs={{0,8},{8,0},{1,9},{9,1},{2,10},{10,2},{3,11},{11,3},{4,12},{12,4},... | collective-permute-start | bytes 7864328 | tf_op jit(solution)/shard_map/ppermute | solution.py:540
  78.9 11.9 %collective-permute-start.8 = (bf16[8,1,2,128,128]{4,3,2,1,0:T(8,128)(2,1)}, bf16[8,1,2,128,128]{4,3,2,1,0:T(8,128)(2,1)}, u32[]{:S(2)}, u32[]{:S(2)}) collective-permute-start(bf16[8,1,2,128,128]{4,3,2,1,0:T(8,128)(2,1)} %get-tuple-element.77), channel_id=1, source_target_pairs={{0,32},{32,64},{64,96},{56,24},{88,56},{120,88},{1,33},{33,65},{65... | collective-permute-start | bytes 1572872 | tf_op jit(solution)/shard_map/ppermute | solution.py:547
  90.8 60.2 %collective-permute-start.10 = (bf16[12,2,2,128,128]{4,3,2,1,0:T(8,128)(2,1)}, bf16[12,2,2,128,128]{4,3,2,1,0:T(8,128)(2,1)S(1)}, u32[]{:S(2)}, u32[]{:S(2)}) collective-permute-start(bf16[12,2,2,128,128]{4,3,2,1,0:T(8,128)(2,1)} %get-tuple-element.90), channel_id=1, source_target_pairs={{0,32},{32,64},{64,96},{96,0},{1,33},{33,65},{65,97},{97,1},{2,34}... | collective-permute-start | bytes 4718600 | tf_op jit(solution)/shard_map/ppermute | solution.py:532
  90.8 60.1 %collective-permute-start.11 = (bf16[12,2,2,128,128]{4,3,2,1,0:T(8,128)(2,1)}, bf16[12,2,2,128,128]{4,3,2,1,0:T(8,128)(2,1)}, u32[]{:S(2)}, u32[]{:S(2)}) collective-permute-start(bf16[12,2,2,128,128]{4,3,2,1,0:T(8,128)(2,1)} %get-tuple-element.91), channel_id=1, source_target_pairs={{0,96},{32,0},{64,32},{96,64},{1,97},{33,1},{65,33},{97,65},{2,98}... | collective-permute-start | bytes 4718600 | tf_op jit(solution)/shard_map/ppermute | solution.py:532
  92.9 13.2 %all-to-all-start.2 = ((bf16[8,1,160,128]{3,2,1,0:T(8,128)(2,1)}), bf16[8,1,160,128]{3,2,1,0:T(8,128)(2,1)S(1)}, u32[]{:S(2)}, u32[]{:S(2)}) async-start(bf16[8,1,160,128]{3,2,1,0:T(8,128)(2,1)} %enter_q.2), calls=%async_computation.2 | async-start | bytes 655360 | tf_op jit(solution)/shard_map/all_to_all | solution.py:543
  98.3 52.6 %collective-permute-start.9 = (bf16[8,2,2,128,128]{4,3,2,1,0:T(8,128)(2,1)}, bf16[8,2,2,128,128]{4,3,2,1,0:T(8,128)(2,1)}, u32[]{:S(2)}, u32[]{:S(2)}) collective-permute-start(bf16[8,2,2,128,128]{4,3,2,1,0:T(8,128)(2,1)} %get-tuple-element.89), channel_id=1, source_target_pairs={{0,32},{32,64},{64,96},{56,24},{88,56},{120,88},{1,33},{33,65},{65... | collective-permute-start | bytes 3145736 | tf_op jit(solution)/shard_map/ppermute | solution.py:547
  100.3 65.7 %collective-permute-start.12 = (bf16[8,2,2,128,128]{4,3,2,1,0:T(8,128)(2,1)}, bf16[8,2,2,128,128]{4,3,2,1,0:T(8,128)(2,1)}, u32[]{:S(2)}, u32[]{:S(2)}) collective-permute-start(bf16[8,2,2,128,128]{4,3,2,1,0:T(8,128)(2,1)} %get-tuple-element.98), channel_id=1, source_target_pairs={{0,64},{32,96},{64,0},{96,32},{1,65},{33,97},{65,1},{97,33},{2,66}... | collective-permute-start | bytes 3145736 | tf_op jit(solution)/shard_map/ppermute | solution.py:532
  106.0 22.3 %all-to-all-start.4 = ((bf16[8,2,160,128]{3,2,1,0:T(8,128)(2,1)}), bf16[8,2,160,128]{3,2,1,0:T(8,128)(2,1)S(1)}, u32[]{:S(2)}, u32[]{:S(2)}) async-start(bf16[8,2,160,128]{3,2,1,0:T(8,128)(2,1)} %enter_q.3), calls=%async_computation.4 | async-start | bytes 1310720 | tf_op jit(solution)/shard_map/all_to_all | solution.py:543
  128.4 5.6 %copy-start.2 = (bf16[8,2,160,128]{3,2,1,0:T(8,128)(2,1)}, bf16[8,2,160,128]{3,2,1,0:T(8,128)(2,1)S(1)}, u32[]{:S(2)}) copy-start(bf16[8,2,160,128]{3,2,1,0:T(8,128)(2,1)S(1)} %all-to-all-done.4.q_ref) | copy-start | bytes 1966084
  128.4 42.1 %all-to-all-start.3 = ((bf16[8,1,160,128]{3,2,1,0:T(8,128)(2,1)}), bf16[8,1,160,128]{3,2,1,0:T(8,128)(2,1)S(1)}, u32[]{:S(2)}, u32[]{:S(2)}) async-start(bf16[8,1,160,128]{3,2,1,0:T(8,128)(2,1)} %everything.1), calls=%async_computation.3 | async-start | bytes 655360 | tf_op jit(solution)/shard_map/all_to_all | solution.py:543
  170.5 15.2 %copy-start.7 = (bf16[8,1,160,128]{3,2,1,0:T(8,128)(2,1)}, bf16[8,1,160,128]{3,2,1,0:T(8,128)(2,1)S(1)}, u32[]{:S(2)}) copy-start(bf16[8,1,160,128]{3,2,1,0:T(8,128)(2,1)S(1)} %all-to-all-done.3.refs_0_) | copy-start | bytes 983044
  (7 other events, 14.3 us)

commit v7 on v6

--- a/solution.py
+++ b/solution.py
@@ -560,10 +560,10 @@
     packed_a, query = together(packed_a, query)
     big_a, in1_a, in2_a, in3_a = send(packed_a)
     q_a, q_b = (enter_q(place, rates, query, rows) for rows in CHUNKS)
-    own_b, q_a, q_b, in1_a, in2_a, in3_a = together(own_b, q_a, q_b, in1_a, in2_a, in3_a)
+    own_b, q_a, q_b, big_a, in1_a, in3_a = together(own_b, q_a, q_b, big_a, in1_a, in3_a)
     sib_b = swap(own_b)
     packed_b = pack(place, asked, own_b, sib_b)
-    packed_b, q_a, big_a = together(packed_b, q_a, big_a)
+    packed_b, q_a, in2_a = together(packed_b, q_a, in2_a)
     big_b, in1_b, in2_b, in3_b = send(packed_b)
     q_a = by_head(q_a)
     q_b = by_head(q_b)

time: 191 us -> 199 us (1.042)
  waiting for transfers between devices: 40.9 us -> 49.4 us
    ppermute x2, waiting for transfers between devices: 0.01 us -> 25.1 us  [send(): big = lax.ppermute(big, TM, BIG_PAIRS)]
    ppermute x9, waiting for transfers between devices: 22.9 us -> 4.3 us  [around(): return lax.ppermute(x, 'z', [(i, (i + shift) % 4) for i in range(4)])]
    all_to_all x2, waiting for transfers between devices: 6.44 us -> 11.4 us  [entry(): lax.all_to_all(sent.reshape(16, nh, 2, CH, DH), ('yh', 'head'), 0, 0, til...]
    ppermute x2, starting transfers between devices: 3.9 us -> 7.64 us  [send(): big = lax.ppermute(big, TM, BIG_PAIRS)]
    all_to_all x3, waiting for transfers between devices: 5.42 us -> 3.35 us  [by_head(): return lax.all_to_all(x, 'head', 0, 0, tiled=True)]
    all_to_all x3, starting transfers between devices: 14.6 us -> 12.6 us  [by_head(): return lax.all_to_all(x, 'head', 0, 0, tiled=True)]
  transfers between devices with their start and end apart: 18 -> 18, of which waited for: 5 -> 8; matrix products, arithmetic and copies ran while one was open for 0% -> 0% of each run, Pallas kernels for 41% -> 39%
where the time goes in v7:
time: 199 us; the launch traced here: 197 us
  Pallas kernels  83.2 us (42%)
  waiting for transfers between devices  49.4 us (25%)
  starting transfers between devices  44.3 us (22%)
  blocking collectives  13.6 us (7%)
  local copies, waits for them, and re-layouts  6.39 us (3%)
    pallas_call x2, Pallas kernels, near(): pl.pallas_call(near_body, grid=(nh,), in_specs=[smem(), smem(), tokens, f...  27 us
    ppermute x2, waiting for transfers between devices, send(): big = lax.ppermute(big, TM, BIG_PAIRS)  25.1 us
    pallas_call x1, Pallas kernels, beside(): pl.pallas_call(beside_body, grid=(nh,), in_specs=[smem(), smem(), tokens]...  13.8 us
    all_to_all x1, blocking collectives, by_head(): return lax.all_to_all(x, 'head', 0, 0, tiled=True)  13.6 us
    ppermute x9, starting transfers between devices, around(): return lax.ppermute(x, 'z', [(i, (i + shift) % 4) for i in range(4)])  13.2 us
    all_to_all x3, starting transfers between devices, by_head(): return lax.all_to_all(x, 'head', 0, 0, tiled=True)  12.6 us
    all_to_all x2, waiting for transfers between devices, entry(): lax.all_to_all(sent.reshape(16, nh, 2, CH, DH), ('yh', 'head'), 0, 0, til...  11.4 us
    all_to_all x2, starting transfers between devices, entry(): lax.all_to_all(sent.reshape(16, nh, 2, CH, DH), ('yh', 'head'), 0, 0, til...  10.8 us
  transfers between devices with their start and end apart: 18, of which 8 were waited for; matrix products, arithmetic and copies ran while one was open for 0% of the time, Pallas kernels for 39%

profile of v7, /device:TPU:32, one launch (start us, length us, event | category | flops | bytes accessed | tf_op | source)
XLA Modules:
  0.0 197.0 jit_solution(4105853838492487778)
XLA Ops:
  0.6 3.5 %enter_kv.2 = bf16[2,8,1,2,160,128]{5,4,3,2,1,0:T(8,128)(2,1)} custom-call(s32[5]{0:T(128)} %stack.23.refs_0_.place_ref, f32[1,128]{1,0:T(1,128)} %constant.24.clone.refs_1_, bf16[160,24,128]{2,1,0:T(8,128)(2,1)} %refs_2_.2, bf16[160,24,128]{2,1,0:T(8,128)(2,1)} %refs_3_.2), custom_call_target="tpu_custom_call" | custom-call | tf_op jit(solution)/shard_map/enter_kv/pallas_call | solution.py:176
  4.1 7.0 %all-to-all-start = ((bf16[16,1,2,160,128]{4,3,2,1,0:T(8,128)(2,1)}), bf16[16,1,2,160,128]{4,3,2,1,0:T(8,128)(2,1)S(1)}, u32[]{:S(2)}, u32[]{:S(2)}) async-start(bf16[16,1,2,160,128]{4,3,2,1,0:T(8,128)(2,1)} %bitcast.18), calls=%async_computation | async-start | bytes 2621440 | tf_op jit(solution)/shard_map/all_to_all | solution.py:536
  11.2 4.3 %tables.1 = (s32[4,128]{1,0:T(4,128)}, s32[64]{0:T(128)}, s32[16]{0:T(128)}) custom-call(s32[5]{0:T(128)} %stack.23.refs_0_.place_ref, s32[10,16]{1,0:T(8,128)} %list_ref, s32[10,16]{1,0:T(8,128)} %count_ref.1), custom_call_target="tpu_custom_call" | custom-call | tf_op jit(solution)/shard_map/tables/pallas_call | solution.py:123
  21.1 4.4 %enter_kv.3 = bf16[2,8,2,2,160,128]{5,4,3,2,1,0:T(8,128)(2,1)} custom-call(s32[5]{0:T(128)} %stack.23.refs_0_.place_ref, f32[1,128]{1,0:T(1,128)} %constant.24.clone.refs_1_, bf16[160,24,128]{2,1,0:T(8,128)(2,1)} %refs_2_.2, bf16[160,24,128]{2,1,0:T(8,128)(2,1)} %refs_3_.2), custom_call_target="tpu_custom_call" | custom-call | tf_op jit(solution)/shard_map/enter_kv/pallas_call | solution.py:176
  25.5 6.4 %all-to-all-done = bf16[16,1,2,160,128]{4,3,2,1,0:T(8,128)(2,1)S(1)} async-done(((bf16[16,1,2,160,128]{4,3,2,1,0:T(8,128)(2,1)}), bf16[16,1,2,160,128]{4,3,2,1,0:T(8,128)(2,1)S(1)}, u32[]{:S(2)}, u32[]{:S(2)}) %all-to-all-start) | async-done | bytes 1310752 | tf_op jit(solution)/shard_map/all_to_all | solution.py:536
  33.1 3.7 %all-to-all-start.1 = ((bf16[16,2,2,160,128]{4,3,2,1,0:T(8,128)(2,1)}), bf16[16,2,2,160,128]{4,3,2,1,0:T(8,128)(2,1)S(1)}, u32[]{:S(2)}, u32[]{:S(2)}) async-start(bf16[16,2,2,160,128]{4,3,2,1,0:T(8,128)(2,1)} %bitcast.17), calls=%async_computation.1 | async-start | bytes 5242880 | tf_op jit(solution)/shard_map/all_to_all | solution.py:536
  36.9 3.2 %collective-permute-done.3.sib_ref = bf16[2,8,1,2,160,128]{5,4,3,2,1,0:T(8,128)(2,1)S(1)} collective-permute-done((bf16[2,8,1,2,160,128]{5,4,3,2,1,0:T(8,128)(2,1)}, bf16[2,8,1,2,160,128]{5,4,3,2,1,0:T(8,128)(2,1)S(1)}, u32[]{:S(2)}, u32[]{:S(2)}) %collective-permute-start.3) | collective-permute-done | bytes 1310752 | tf_op jit(solution)/shard_map/ppermute | solution.py:540
  46.3 3.8 %collective-permute-start.4 = (bf16[8,1,2,128,128]{4,3,2,1,0:T(8,128)(2,1)}, bf16[8,1,2,128,128]{4,3,2,1,0:T(8,128)(2,1)S(1)}, u32[]{:S(2)}, u32[]{:S(2)}) collective-permute-start(bf16[8,1,2,128,128]{4,3,2,1,0:T(8,128)(2,1)} %get-tuple-element.68), channel_id=1, source_target_pairs={{0,32},{32,64},{64,96},{56,24},{88,56},{120,88},{1,33},{33,65},{65... | collective-permute-start | bytes 1572872 | tf_op jit(solution)/shard_map/ppermute | solution.py:547
  56.0 13.7 %collective-permute-done.4.big_ref = bf16[8,1,2,128,128]{4,3,2,1,0:T(8,128)(2,1)S(1)} collective-permute-done((bf16[8,1,2,128,128]{4,3,2,1,0:T(8,128)(2,1)}, bf16[8,1,2,128,128]{4,3,2,1,0:T(8,128)(2,1)S(1)}, u32[]{:S(2)}, u32[]{:S(2)}) %collective-permute-start.4) | collective-permute-done | bytes 524320 | tf_op jit(solution)/shard_map/ppermute | solution.py:547
  70.5 5.0 %all-to-all-done.1 = bf16[16,2,2,160,128]{4,3,2,1,0:T(8,128)(2,1)S(1)} async-done(((bf16[16,2,2,160,128]{4,3,2,1,0:T(8,128)(2,1)}), bf16[16,2,2,160,128]{4,3,2,1,0:T(8,128)(2,1)S(1)}, u32[]{:S(2)}, u32[]{:S(2)}) %all-to-all-start.1) | async-done | bytes 2621472 | tf_op jit(solution)/shard_map/all_to_all | solution.py:536
  81.9 5.4 %pack.3 = (bf16[8,2,2,128,128]{4,3,2,1,0:T(8,128)(2,1)}, bf16[12,2,2,128,128]{4,3,2,1,0:T(8,128)(2,1)}, bf16[8,2,2,128,128]{4,3,2,1,0:T(8,128)(2,1)}, bf16[12,2,2,128,128]{4,3,2,1,0:T(8,128)(2,1)}) custom-call(s32[5]{0:T(128)} %stack.23.refs_0_.place_ref, s32[4,128]{1,0:T(4,128)} %copy-done.12, s32[4,128]{1,0:T(4,128)} %copy-done.11, s32[4,128]{1,0:T(4,128)} %copy-done.10, ...), custom_call_target="tpu_custom_call" | custom-call | tf_op jit(solution)/shard_map/pack/pallas_call | solution.py:233
  87.3 4.3 %collective-permute-done.8.in2 = bf16[8,1,2,128,128]{4,3,2,1,0:T(8,128)(2,1)} collective-permute-done((bf16[8,1,2,128,128]{4,3,2,1,0:T(8,128)(2,1)}, bf16[8,1,2,128,128]{4,3,2,1,0:T(8,128)(2,1)}, u32[]{:S(2)}, u32[]{:S(2)}) %collective-permute-start.8) | collective-permute-done | bytes 524320 | tf_op jit(solution)/shard_map/ppermute | solution.py:532
  93.6 3.4 %all-to-all-start.2 = ((bf16[8,1,160,128]{3,2,1,0:T(8,128)(2,1)}), bf16[8,1,160,128]{3,2,1,0:T(8,128)(2,1)S(1)}, u32[]{:S(2)}, u32[]{:S(2)}) async-start(bf16[8,1,160,128]{3,2,1,0:T(8,128)(2,1)} %enter_q.2), calls=%async_computation.2 | async-start | bytes 655360 | tf_op jit(solution)/shard_map/all_to_all | solution.py:543
  97.1 3.8 %collective-permute-start.9 = (bf16[8,2,2,128,128]{4,3,2,1,0:T(8,128)(2,1)}, bf16[8,2,2,128,128]{4,3,2,1,0:T(8,128)(2,1)}, u32[]{:S(2)}, u32[]{:S(2)}) collective-permute-start(bf16[8,2,2,128,128]{4,3,2,1,0:T(8,128)(2,1)} %get-tuple-element.89), channel_id=1, source_target_pairs={{0,32},{32,64},{64,96},{56,24},{88,56},{120,88},{1,33},{33,65},{65... | collective-permute-start | bytes 3145736 | tf_op jit(solution)/shard_map/ppermute | solution.py:547
  101.4 3.3 %all-to-all-done.2.q_ref = bf16[8,1,160,128]{3,2,1,0:T(8,128)(2,1)S(1)} async-done(((bf16[8,1,160,128]{3,2,1,0:T(8,128)(2,1)}), bf16[8,1,160,128]{3,2,1,0:T(8,128)(2,1)S(1)}, u32[]{:S(2)}, u32[]{:S(2)}) %all-to-all-start.2) | async-done | bytes 327712 | tf_op jit(solution)/shard_map/all_to_all | solution.py:543
  104.8 3.5 %all-to-all-start.4 = ((bf16[8,2,160,128]{3,2,1,0:T(8,128)(2,1)}), bf16[8,2,160,128]{3,2,1,0:T(8,128)(2,1)S(1)}, u32[]{:S(2)}, u32[]{:S(2)}) async-start(bf16[8,2,160,128]{3,2,1,0:T(8,128)(2,1)} %enter_q.3), calls=%async_computation.4 | async-start | bytes 1310720 | tf_op jit(solution)/shard_map/all_to_all | solution.py:543
  108.3 10.0 %near.2 = (f32[1,1280,128]{2,1,0:T(8,128)}, f32[1,1280,128]{2,1,0:T(8,128)}, f32[1,1280,128]{2,1,0:T(8,128)}) custom-call(s32[5]{0:T(128)} %stack.23.refs_0_.place_ref, s32[16]{0:T(128)} %get-tuple-element.83.plane_ref, bf16[8,1,160,128]{3,2,1,0:T(8,128)(2,1)} %copy-done.5, bf16[2,8,1,2,160,128]{5,4,3,2,1,0:T(8,128)(2,1)} %bitcast.16, ...), custom_call_target="tpu_custom_call" | custom-call | tf_op jit(solution)/shard_map/near/pallas_call | solution.py:355
  118.4 8.7 %everything.1 = bf16[8,1,160,128]{3,2,1,0:T(8,128)(2,1)} custom-call(s32[5]{0:T(128)} %stack.23.refs_0_.place_ref, s32[64]{0:T(128)} %get-tuple-element.53.qslot_ref, bf16[8,1,160,128]{3,2,1,0:T(8,128)(2,1)} %copy-done.5, bf16[8,1,2,128,128]{4,3,2,1,0:T(8,128)(2,1)} %copy-done.9, bf16[12,1,2,128,128]{4,3,2,1,0:T(8,128)(2,1)} %copy-done.8, ...), custom_call_target="tpu_custom_call" | custom-call | tf_op jit(solution)/shard_map/everything/pallas_call | solution.py:462
  127.1 5.6 %all-to-all-start.3 = ((bf16[8,1,160,128]{3,2,1,0:T(8,128)(2,1)}), bf16[8,1,160,128]{3,2,1,0:T(8,128)(2,1)S(1)}, u32[]{:S(2)}, u32[]{:S(2)}) async-start(bf16[8,1,160,128]{3,2,1,0:T(8,128)(2,1)} %everything.1), calls=%async_computation.3 | async-start | bytes 655360 | tf_op jit(solution)/shard_map/all_to_all | solution.py:543
  132.8 16.9 %near.3 = (f32[2,1280,128]{2,1,0:T(8,128)}, f32[2,1280,128]{2,1,0:T(8,128)}, f32[2,1280,128]{2,1,0:T(8,128)}) custom-call(s32[5]{0:T(128)} %stack.23.refs_0_.place_ref, s32[16]{0:T(128)} %get-tuple-element.83.plane_ref, bf16[8,2,160,128]{3,2,1,0:T(8,128)(2,1)} %copy-done.2, bf16[2,8,2,2,160,128]{5,4,3,2,1,0:T(8,128)(2,1)} %bitcast.13, ...), custom_call_target="tpu_custom_call" | custom-call | tf_op jit(solution)/shard_map/near/pallas_call | solution.py:355
  149.7 11.4 %collective-permute-done.9.big_ref = bf16[8,2,2,128,128]{4,3,2,1,0:T(8,128)(2,1)} collective-permute-done((bf16[8,2,2,128,128]{4,3,2,1,0:T(8,128)(2,1)}, bf16[8,2,2,128,128]{4,3,2,1,0:T(8,128)(2,1)}, u32[]{:S(2)}, u32[]{:S(2)}) %collective-permute-start.9) | collective-permute-done | bytes 1048608 | tf_op jit(solution)/shard_map/ppermute | solution.py:547
  162.4 13.8 %beside.1 = (f32[2,1280,128]{2,1,0:T(8,128)}, f32[2,1280,128]{2,1,0:T(8,128)}, f32[2,1280,128]{2,1,0:T(8,128)}) custom-call(s32[5]{0:T(128)} %stack.23.refs_0_.place_ref, s32[64]{0:T(128)} %get-tuple-element.53.qslot_ref, bf16[8,2,160,128]{3,2,1,0:T(8,128)(2,1)} %copy-done.2, bf16[8,2,2,128,128]{4,3,2,1,0:T(8,128)(2,1)} %collective-permute-done.9.big_ref, ...), custom_call_target="tpu_custom_call" | custom-call | tf_op jit(solution)/shard_map/beside/pallas_call | solution.py:437
  176.2 4.5 %across.1 = bf16[8,2,160,128]{3,2,1,0:T(8,128)(2,1)} custom-call(s32[5]{0:T(128)} %stack.23.refs_0_.place_ref, s32[64]{0:T(128)} %get-tuple-element.53.qslot_ref, bf16[8,2,160,128]{3,2,1,0:T(8,128)(2,1)} %copy-done.2, f32[2,1280,128]{2,1,0:T(8,128)} %get-tuple-element.95.acc_in, f32[2,1280,128]{2,1,0:T(8,128)} %get-tuple-element.96.m_in, ...), custom_call_target="tpu_custom_call" | custom-call | tf_op jit(solution)/shard_map/across/pallas_call | solution.py:479
  180.7 13.6 %all_to_all.30.refs_1_ = bf16[8,2,160,128]{3,2,1,0:T(8,128)(2,1)} all-to-all(bf16[8,2,160,128]{3,2,1,0:T(8,128)(2,1)} %across.1), channel_id=1, replica_groups=mesh['z'=4,'yh'=2,'c'=2,'head'=8] {'head'}, dimensions={0} | all-to-all | bytes 1310720 | tf_op jit(solution)/shard_map/all_to_all | solution.py:543
  (53 shorter events, 33.3 us)
Async XLA Ops:
  4.1 27.9 %all-to-all-start = ((bf16[16,1,2,160,128]{4,3,2,1,0:T(8,128)(2,1)}), bf16[16,1,2,160,128]{4,3,2,1,0:T(8,128)(2,1)S(1)}, u32[]{:S(2)}, u32[]{:S(2)}) async-start(bf16[16,1,2,160,128]{4,3,2,1,0:T(8,128)(2,1)} %bitcast.18), calls=%async_computation | async-start | bytes 2621440 | tf_op jit(solution)/shard_map/all_to_all | solution.py:536
  15.5 10.0 %collective-permute-start.2 = (s32[4,128]{1,0:T(4,128)}, s32[4,128]{1,0:T(4,128)S(1)}, u32[]{:S(2)}, u32[]{:S(2)}) collective-permute-start(s32[4,128]{1,0:T(4,128)} %get-tuple-element.57), channel_id=1, source_target_pairs={{0,32},{32,64},{64,96},{96,0},{1,33},{33,65},{65,97},{97,1},{2,34}... | collective-permute-start | bytes 6152 | tf_op jit(solution)/shard_map/ppermute | solution.py:532
  17.4 8.1 %collective-permute-start.1 = (s32[4,128]{1,0:T(4,128)}, s32[4,128]{1,0:T(4,128)S(1)}, u32[]{:S(2)}, u32[]{:S(2)}) collective-permute-start(s32[4,128]{1,0:T(4,128)} %get-tuple-element.57), channel_id=1, source_target_pairs={{0,64},{32,96},{64,0},{96,32},{1,65},{33,97},{65,1},{97,33},{2,66}... | collective-permute-start | bytes 6152 | tf_op jit(solution)/shard_map/ppermute | solution.py:532
  18.6 6.9 %collective-permute-start = (s32[4,128]{1,0:T(4,128)}, s32[4,128]{1,0:T(4,128)S(1)}, u32[]{:S(2)}, u32[]{:S(2)}) collective-permute-start(s32[4,128]{1,0:T(4,128)} %get-tuple-element.57), channel_id=1, source_target_pairs={{0,96},{32,0},{64,32},{96,64},{1,97},{33,1},{65,33},{97,65},{2,98}... | collective-permute-start | bytes 6152 | tf_op jit(solution)/shard_map/ppermute | solution.py:532
  25.5 7.6 %copy-start.10 = (s32[4,128]{1,0:T(4,128)}, s32[4,128]{1,0:T(4,128)S(1)}, u32[]{:S(2)}) copy-start(s32[4,128]{1,0:T(4,128)S(1)} %collective-permute-done.2.ask3) | copy-start | bytes 6148
  25.5 14.6 %copy-start.11 = (s32[4,128]{1,0:T(4,128)}, s32[4,128]{1,0:T(4,128)S(1)}, u32[]{:S(2)}) copy-start(s32[4,128]{1,0:T(4,128)S(1)} %collective-permute-done.1.ask2) | copy-start | bytes 6148
  25.5 14.6 %copy-start.12 = (s32[4,128]{1,0:T(4,128)}, s32[4,128]{1,0:T(4,128)S(1)}, u32[]{:S(2)}) copy-start(s32[4,128]{1,0:T(4,128)S(1)} %collective-permute-done.ask1) | copy-start | bytes 6148
  33.1 42.4 %all-to-all-start.1 = ((bf16[16,2,2,160,128]{4,3,2,1,0:T(8,128)(2,1)}), bf16[16,2,2,160,128]{4,3,2,1,0:T(8,128)(2,1)S(1)}, u32[]{:S(2)}, u32[]{:S(2)}) async-start(bf16[16,2,2,160,128]{4,3,2,1,0:T(8,128)(2,1)} %bitcast.17), calls=%async_computation.1 | async-start | bytes 5242880 | tf_op jit(solution)/shard_map/all_to_all | solution.py:536
  36.8 3.3 %collective-permute-start.3 = (bf16[2,8,1,2,160,128]{5,4,3,2,1,0:T(8,128)(2,1)}, bf16[2,8,1,2,160,128]{5,4,3,2,1,0:T(8,128)(2,1)S(1)}, u32[]{:S(2)}, u32[]{:S(2)}) collective-permute-start(bf16[2,8,1,2,160,128]{5,4,3,2,1,0:T(8,128)(2,1)} %bitcast.14), channel_id=1, source_target_pairs={{0,8},{8,0},{1,9},{9,1},{2,10},{10,2},{3,11},{11,3},{4,12},{12,4},... | collective-permute-start | bytes 3932168 | tf_op jit(solution)/shard_map/ppermute | solution.py:540
  44.2 25.4 %collective-permute-start.5 = (bf16[12,1,2,128,128]{4,3,2,1,0:T(8,128)(2,1)}, bf16[12,1,2,128,128]{4,3,2,1,0:T(8,128)(2,1)S(1)}, u32[]{:S(2)}, u32[]{:S(2)}) collective-permute-start(bf16[12,1,2,128,128]{4,3,2,1,0:T(8,128)(2,1)} %get-tuple-element.69), channel_id=1, source_target_pairs={{0,32},{32,64},{64,96},{96,0},{1,33},{33,65},{65,97},{97,1},{2,34}... | collective-permute-start | bytes 2359304 | tf_op jit(solution)/shard_map/ppermute | solution.py:532
  46.2 24.3 %collective-permute-start.6 = (bf16[12,1,2,128,128]{4,3,2,1,0:T(8,128)(2,1)}, bf16[12,1,2,128,128]{4,3,2,1,0:T(8,128)(2,1)}, u32[]{:S(2)}, u32[]{:S(2)}) collective-permute-start(bf16[12,1,2,128,128]{4,3,2,1,0:T(8,128)(2,1)} %get-tuple-element.70), channel_id=1, source_target_pairs={{0,96},{32,0},{64,32},{96,64},{1,97},{33,1},{65,33},{97,65},{2,98}... | collective-permute-start | bytes 2359304 | tf_op jit(solution)/shard_map/ppermute | solution.py:532
  46.3 23.4 %collective-permute-start.4 = (bf16[8,1,2,128,128]{4,3,2,1,0:T(8,128)(2,1)}, bf16[8,1,2,128,128]{4,3,2,1,0:T(8,128)(2,1)S(1)}, u32[]{:S(2)}, u32[]{:S(2)}) collective-permute-start(bf16[8,1,2,128,128]{4,3,2,1,0:T(8,128)(2,1)} %get-tuple-element.68), channel_id=1, source_target_pairs={{0,32},{32,64},{64,96},{56,24},{88,56},{120,88},{1,33},{33,65},{65... | collective-permute-start | bytes 1572872 | tf_op jit(solution)/shard_map/ppermute | solution.py:547
  70.5 47.9 %copy-start.8 = (bf16[12,1,2,128,128]{4,3,2,1,0:T(8,128)(2,1)}, bf16[12,1,2,128,128]{4,3,2,1,0:T(8,128)(2,1)S(1)}, u32[]{:S(2)}) copy-start(bf16[12,1,2,128,128]{4,3,2,1,0:T(8,128)(2,1)S(1)} %collective-permute-done.5.in1) | copy-start | bytes 2359300
  75.5 4.9 %collective-permute-start.7 = (bf16[2,8,2,2,160,128]{5,4,3,2,1,0:T(8,128)(2,1)S(1)}, bf16[2,8,2,2,160,128]{5,4,3,2,1,0:T(8,128)(2,1)S(1)}, u32[]{:S(2)}, u32[]{:S(2)}) collective-permute-start(bf16[2,8,2,2,160,128]{5,4,3,2,1,0:T(8,128)(2,1)S(1)} %bitcast.11), channel_id=1, source_target_pairs={{0,8},{8,0},{1,9},{9,1},{2,10},{10,2},{3,11},{11,3},{4,12},{12,4},... | collective-permute-start | bytes 7864328 | tf_op jit(solution)/shard_map/ppermute | solution.py:540
  75.5 16.2 %collective-permute-start.8 = (bf16[8,1,2,128,128]{4,3,2,1,0:T(8,128)(2,1)}, bf16[8,1,2,128,128]{4,3,2,1,0:T(8,128)(2,1)}, u32[]{:S(2)}, u32[]{:S(2)}) collective-permute-start(bf16[8,1,2,128,128]{4,3,2,1,0:T(8,128)(2,1)} %get-tuple-element.77), channel_id=1, source_target_pairs={{0,64},{32,96},{64,0},{96,32},{1,65},{33,97},{65,1},{97,33},{2,66}... | collective-permute-start | bytes 1572872 | tf_op jit(solution)/shard_map/ppermute | solution.py:532
  91.6 69.5 %collective-permute-start.10 = (bf16[12,2,2,128,128]{4,3,2,1,0:T(8,128)(2,1)}, bf16[12,2,2,128,128]{4,3,2,1,0:T(8,128)(2,1)S(1)}, u32[]{:S(2)}, u32[]{:S(2)}) collective-permute-start(bf16[12,2,2,128,128]{4,3,2,1,0:T(8,128)(2,1)} %get-tuple-element.90), channel_id=1, source_target_pairs={{0,32},{32,64},{64,96},{96,0},{1,33},{33,65},{65,97},{97,1},{2,34}... | collective-permute-start | bytes 4718600 | tf_op jit(solution)/shard_map/ppermute | solution.py:532
  93.5 67.6 %collective-permute-start.11 = (bf16[12,2,2,128,128]{4,3,2,1,0:T(8,128)(2,1)}, bf16[12,2,2,128,128]{4,3,2,1,0:T(8,128)(2,1)}, u32[]{:S(2)}, u32[]{:S(2)}) collective-permute-start(bf16[12,2,2,128,128]{4,3,2,1,0:T(8,128)(2,1)} %get-tuple-element.91), channel_id=1, source_target_pairs={{0,96},{32,0},{64,32},{96,64},{1,97},{33,1},{65,33},{97,65},{2,98}... | collective-permute-start | bytes 4718600 | tf_op jit(solution)/shard_map/ppermute | solution.py:532
  93.6 11.1 %all-to-all-start.2 = ((bf16[8,1,160,128]{3,2,1,0:T(8,128)(2,1)}), bf16[8,1,160,128]{3,2,1,0:T(8,128)(2,1)S(1)}, u32[]{:S(2)}, u32[]{:S(2)}) async-start(bf16[8,1,160,128]{3,2,1,0:T(8,128)(2,1)} %enter_q.2), calls=%async_computation.2 | async-start | bytes 655360 | tf_op jit(solution)/shard_map/all_to_all | solution.py:543
  97.1 64.0 %collective-permute-start.9 = (bf16[8,2,2,128,128]{4,3,2,1,0:T(8,128)(2,1)}, bf16[8,2,2,128,128]{4,3,2,1,0:T(8,128)(2,1)}, u32[]{:S(2)}, u32[]{:S(2)}) collective-permute-start(bf16[8,2,2,128,128]{4,3,2,1,0:T(8,128)(2,1)} %get-tuple-element.89), channel_id=1, source_target_pairs={{0,32},{32,64},{64,96},{56,24},{88,56},{120,88},{1,33},{33,65},{65... | collective-permute-start | bytes 3145736 | tf_op jit(solution)/shard_map/ppermute | solution.py:547
  100.9 75.3 %collective-permute-start.12 = (bf16[8,2,2,128,128]{4,3,2,1,0:T(8,128)(2,1)}, bf16[8,2,2,128,128]{4,3,2,1,0:T(8,128)(2,1)}, u32[]{:S(2)}, u32[]{:S(2)}) collective-permute-start(bf16[8,2,2,128,128]{4,3,2,1,0:T(8,128)(2,1)} %get-tuple-element.98), channel_id=1, source_target_pairs={{0,64},{32,96},{64,0},{96,32},{1,65},{33,97},{65,1},{97,33},{2,66}... | collective-permute-start | bytes 3145736 | tf_op jit(solution)/shard_map/ppermute | solution.py:532
  104.8 22.4 %all-to-all-start.4 = ((bf16[8,2,160,128]{3,2,1,0:T(8,128)(2,1)}), bf16[8,2,160,128]{3,2,1,0:T(8,128)(2,1)S(1)}, u32[]{:S(2)}, u32[]{:S(2)}) async-start(bf16[8,2,160,128]{3,2,1,0:T(8,128)(2,1)} %enter_q.3), calls=%async_computation.4 | async-start | bytes 1310720 | tf_op jit(solution)/shard_map/all_to_all | solution.py:543
  127.1 5.6 %copy-start.2 = (bf16[8,2,160,128]{3,2,1,0:T(8,128)(2,1)}, bf16[8,2,160,128]{3,2,1,0:T(8,128)(2,1)S(1)}, u32[]{:S(2)}) copy-start(bf16[8,2,160,128]{3,2,1,0:T(8,128)(2,1)S(1)} %all-to-all-done.4.q_ref) | copy-start | bytes 1966084
  127.1 53.5 %all-to-all-start.3 = ((bf16[8,1,160,128]{3,2,1,0:T(8,128)(2,1)}), bf16[8,1,160,128]{3,2,1,0:T(8,128)(2,1)S(1)}, u32[]{:S(2)}, u32[]{:S(2)}) async-start(bf16[8,1,160,128]{3,2,1,0:T(8,128)(2,1)} %everything.1), calls=%async_computation.3 | async-start | bytes 655360 | tf_op jit(solution)/shard_map/all_to_all | solution.py:543
  180.7 13.6 %copy-start.7 = (bf16[8,1,160,128]{3,2,1,0:T(8,128)(2,1)}, bf16[8,1,160,128]{3,2,1,0:T(8,128)(2,1)S(1)}, u32[]{:S(2)}) copy-start(bf16[8,1,160,128]{3,2,1,0:T(8,128)(2,1)S(1)} %all-to-all-done.3.refs_0_) | copy-start | bytes 983044
  (7 other events, 14.2 us)
